TPU v7x, 32 devices: a whole 2x2x4 slice. The times are simulated.
32 devices in a mesh: dp: 2 (over x), ctx: 16 (over z, y, core).
Axes of the slice: x: 2, y: 2, z: 4, core: 2. Of those that a mesh axis runs over, the one named last changes fastest.
Arguments:
- queries: bfloat16 [2, 2048, 1024], P('dp', 'ctx')
- keys: bfloat16 [2, 2048, 1024], P('dp', 'ctx')
- values: bfloat16 [2, 2048, 1024], P('dp', 'ctx'), may hold values from -6 to 6
- out_weight: bfloat16 [1024, 1024], P('dp'), may hold values from -0.1875 to 0.1875
- out_grad: bfloat16 [2, 2048, 1024], P('dp', 'ctx'), may hold values from -6 to 6
- key_blocks: int32 [2, 8, 16, 2], P('dp'), may hold values from 0 to 15, as said below
- block_counts: int32 [2, 8, 16], P('dp'), may hold values from 1 to 2, as said below
Outputs:
- output: bfloat16 [2, 2048, 1024], P('dp', 'ctx')
- grad_queries: bfloat16 [2, 2048, 1024], P('dp', 'ctx')
- grad_keys: bfloat16 [2, 2048, 1024], P('dp', 'ctx')
- grad_values: bfloat16 [2, 2048, 1024], P('dp', 'ctx')
- grad_weight: float32 [1024, 1024], P(('dp', 'ctx'))
Inputs may be any that keep to these rules, and one draw needn't show every extreme that they name: For netlist b, head h and query block s, key_blocks[b, h, s, 0] is s and entries 1 to block_counts[b, h, s] - 1 are distinct blocks below s; later entries are block numbers that are not attended. block_counts[b, h, s] is at most s + 1; head 0's last block attends 2 blocks in every netlist.
All inputs are finite; a program needn't handle non-finite values.
Results may differ from a plain program's by a relative error of at most 0.02.
Values may be sent and summed in bfloat16 or wider, within the bound.
No kernel may reach another device: no remote copies, remote signals or barrier semaphores. Data moves between devices by JAX's collectives and lax.ppermute only.
A program may use at most 128 MiB of HBM per device.

v0:
```python
import jax
import jax.numpy as jnp
from jax import lax
from jax.sharding import PartitionSpec as P

HEADS = 8
HEAD_SIZE = 128
BLOCK = 128
SLOTS = 2


def partner_2(block, axis, distance):
    count = lax.axis_size(axis)
    route = []
    for low in range(count):
        high = low | 1 << distance
        if high != low and high < count:
            route += [(low, high), (high, low)]
    return lax.ppermute(block, axis, route)


def to_dest(tokens, group, rows_sub, width):
    heads_first = tokens.reshape(group, rows_sub, HEADS, width).transpose(2, 0, 1, 3)
    return heads_first.reshape(HEADS * group, rows_sub, width)


def from_source(received, group, rows_sub):
    ordered = received.reshape(HEADS, group, rows_sub, HEAD_SIZE).transpose(1, 2, 0, 3)
    return ordered.reshape(group * rows_sub, HEADS * HEAD_SIZE)


def attend_local(query_heads, kv_heads, output_grad_heads, idx, cnt):
    score_scale = HEAD_SIZE ** (-0.5)
    nblocks = query_heads.shape[0]
    rows_sub = query_heads.shape[1]
    valid_entries = jnp.arange(SLOTS)[:, None] < cnt[None, :]

    def scores_at(slot_index):
        selected_entries = jnp.take(kv_heads, idx[:, slot_index], axis=0)
        return (
            jnp.einsum(
                "lqo,lco->lqc",
                query_heads,
                selected_entries[..., :HEAD_SIZE],
                preferred_element_type=jnp.float32,
            )
            * score_scale
        )

    logit_scores = lax.map(scores_at, jnp.arange(SLOTS))
    valid_mask = valid_entries[:, :, None, None]
    highest_choice = jnp.max(
        jnp.where(valid_mask, logit_scores, -jnp.inf), axis=(0, 3), keepdims=True
    )
    exponent_values = jnp.where(valid_mask, jnp.exp(logit_scores - highest_choice), 0.0)
    probs = exponent_values / jnp.sum(exponent_values, axis=(0, 3), keepdims=True)
    block_probabilities = probs.astype(jnp.bfloat16)

    def out_step(running_sum, slot_index):
        selected_entries = jnp.take(kv_heads, idx[:, slot_index], axis=0)
        return (
            running_sum
            + jnp.einsum(
                "zij,zjh->zih",
                block_probabilities[slot_index],
                selected_entries[..., HEAD_SIZE:],
                preferred_element_type=jnp.float32,
            ),
            None,
        )

    running_sum, _ = lax.scan(
        out_step, jnp.zeros((nblocks, rows_sub, HEAD_SIZE), jnp.float32), jnp.arange(SLOTS)
    )
    attn = running_sum.astype(jnp.bfloat16)
    delta = jnp.sum(output_grad_heads.astype(jnp.float32) * attn.astype(jnp.float32), axis=-1)

    def back_step(carry, slot_index):
        query_gradient, kv_acc = carry
        selected_entries = jnp.take(kv_heads, idx[:, slot_index], axis=0)
        prob_gradient = jnp.einsum(
            "lqo,lco->lqc",
            output_grad_heads,
            selected_entries[..., HEAD_SIZE:],
            preferred_element_type=jnp.float32,
        )
        score_gradient = (probs[slot_index] * (prob_gradient - delta[..., None])).astype(
            jnp.bfloat16
        )
        query_gradient = query_gradient + jnp.einsum(
            "zij,zjh->zih",
            score_gradient,
            selected_entries[..., :HEAD_SIZE],
            preferred_element_type=jnp.float32,
        )
        key_contribution = jnp.einsum(
            "mja,mju->mau", score_gradient, query_heads, preferred_element_type=jnp.float32
        )
        value_term = jnp.einsum(
            "mja,mju->mau",
            block_probabilities[slot_index],
            output_grad_heads,
            preferred_element_type=jnp.float32,
        )
        kv_acc = kv_acc.at[idx[:, slot_index]].add(
            jnp.concatenate([key_contribution, value_term], axis=-1)
        )
        return ((query_gradient, kv_acc), None)

    start = (
        jnp.zeros((nblocks, rows_sub, HEAD_SIZE), jnp.float32),
        jnp.zeros((nblocks, kv_heads.shape[1], 2 * HEAD_SIZE), jnp.float32),
    )
    (query_gradient, kv_acc), _ = lax.scan(back_step, start, jnp.arange(SLOTS))
    query_gradient = (query_gradient * score_scale).astype(jnp.bfloat16)
    kv_part = jnp.concatenate(
        [kv_acc[..., :HEAD_SIZE] * score_scale, kv_acc[..., HEAD_SIZE:]], axis=-1
    ).astype(jnp.bfloat16)
    return (attn, query_gradient, kv_part)


def local(queries, keys, values, out_weight, out_grad, key_blocks, block_counts):
    ctx_count = lax.axis_size("ctx")
    group = ctx_count // HEADS
    rows_sub = BLOCK // group
    position = lax.axis_index("ctx")
    head = position // group
    member = position % group
    weight_full = lax.all_gather(out_weight, "dp", axis=0, tiled=True)
    tok_grad = out_grad[0]
    d_out = lax.dot_general(
        tok_grad, weight_full, (((1,), (1,)), ((), ())), preferred_element_type=jnp.float32
    ).astype(jnp.bfloat16)
    q_send = to_dest(queries[0], group, rows_sub, HEAD_SIZE)
    do_send = to_dest(d_out, group, rows_sub, HEAD_SIZE)
    kv_tok = jnp.concatenate(
        [keys[0].reshape(BLOCK, HEADS, HEAD_SIZE), values[0].reshape(BLOCK, HEADS, HEAD_SIZE)],
        axis=-1,
    )
    kv_piece = to_dest(kv_tok.reshape(BLOCK, HEADS * 2 * HEAD_SIZE), group, rows_sub, 2 * HEAD_SIZE)
    query_heads, kv_own, output_grad_heads = (
        lax.all_to_all(q_send, "ctx", split_axis=0, concat_axis=0, tiled=True),
        lax.all_to_all(kv_piece, "ctx", split_axis=0, concat_axis=0, tiled=True),
        lax.all_to_all(do_send, "ctx", split_axis=0, concat_axis=0, tiled=True),
    )
    held = kv_own[None]
    for bit in range(group.bit_length() - 1):
        partner = partner_2(held, "ctx", bit)
        lower = member >> bit & 1 == 0
        held = jnp.where(
            lower,
            jnp.concatenate([held, partner], axis=0),
            jnp.concatenate([partner, held], axis=0),
        )
    kv_heads = held.transpose(1, 0, 2, 3).reshape(held.shape[1], BLOCK, 2 * HEAD_SIZE)
    idx = lax.dynamic_index_in_dim(key_blocks[0], head, 0, keepdims=False)
    cnt = lax.dynamic_index_in_dim(block_counts[0], head, 0, keepdims=False)
    attn, query_gradient, kv_part = attend_local(query_heads, kv_heads, output_grad_heads, idx, cnt)
    attn_back = lax.all_to_all(attn, "ctx", split_axis=0, concat_axis=0, tiled=True)
    attn_tok = from_source(attn_back, group, rows_sub)
    output = jnp.dot(attn_tok, weight_full, preferred_element_type=jnp.float32).astype(jnp.bfloat16)
    weight_term = lax.dot_general(
        attn_tok, tok_grad, (((0,), (0,)), ((), ())), preferred_element_type=jnp.float32
    )
    grad_weight = lax.psum_scatter(weight_term, ("dp", "ctx"), scatter_dimension=0, tiled=True)
    q_back, kv_back = (
        lax.all_to_all(query_gradient, "ctx", split_axis=0, concat_axis=0, tiled=True),
        lax.all_to_all(kv_part, "ctx", split_axis=0, concat_axis=0, tiled=True),
    )
    grad_queries = from_source(q_back, group, rows_sub)
    summed = jnp.sum(
        kv_back.reshape(HEADS, group, BLOCK, 2 * HEAD_SIZE).astype(jnp.float32), axis=1
    )
    summed = summed.transpose(1, 0, 2)
    grad_keys = summed[..., :HEAD_SIZE].reshape(BLOCK, HEADS * HEAD_SIZE).astype(jnp.bfloat16)
    grad_values = summed[..., HEAD_SIZE:].reshape(BLOCK, HEADS * HEAD_SIZE).astype(jnp.bfloat16)
    return (output[None], grad_queries[None], grad_keys[None], grad_values[None], grad_weight)


def solution(mesh):
    placed = (
        P("dp", "ctx", None),
        P("dp", "ctx", None),
        P("dp", "ctx", None),
        P("dp", None),
        P("dp", "ctx", None),
        P("dp", None, None, None),
        P("dp", None, None),
    )
    return jax.shard_map(
        local,
        mesh=mesh,
        in_specs=placed,
        out_specs=(
            P("dp", "ctx", None),
            P("dp", "ctx", None),
            P("dp", "ctx", None),
            P("dp", "ctx", None),
            P(("dp", "ctx"), None),
        ),
        check_vma=False,
    )
```

profile of v0, /device:TPU:0, one launch (start us, length us, event | category | flops | bytes accessed | tf_op | source)
XLA Modules:
  0.0 251.5 jit_solution(9450957250715556877)
XLA Ops:
  7.2 1.0 copy.38
  8.3 1.0 copy.39
  9.5 21.7 %all_to_all.30 = bf16[16,64,256]{2,1,0:T(8,128)(2,1)S(1)} all-to-all(bf16[16,64,256]{2,1,0:T(8,128)(2,1)S(1)} %bitcast.158), channel_id=1, replica_groups=mesh['dp'=2,'ctx'=16] {'ctx'}, dimensions={0} | all-to-all | bytes 1048576 | tf_op jit(solution)/shard_map/all_to_all | solution.py:143
  31.2 0.8 copy.30
  32.0 4.4 %all-to-all-start.1 = ((bf16[16,64,128]{2,1,0:T(8,128)(2,1)}), bf16[16,64,128]{2,1,0:T(8,128)(2,1)}, u32[]{:S(2)}, u32[]{:S(2)}) async-start(bf16[16,64,128]{2,1,0:T(8,128)(2,1)} %bitcast.12), calls=%async_computation.1 | async-start | bytes 524288 | tf_op jit(solution)/shard_map/all_to_all | solution.py:142
  36.4 0.7 dynamic-slice_bitcast_fusion.1
  37.1 0.7 dynamic-slice_bitcast_fusion
  37.9 8.6 %all-to-all-done.1 = bf16[16,64,128]{2,1,0:T(8,128)(2,1)} async-done(((bf16[16,64,128]{2,1,0:T(8,128)(2,1)}), bf16[16,64,128]{2,1,0:T(8,128)(2,1)}, u32[]{:S(2)}, u32[]{:S(2)}) %all-to-all-start.1) | async-done | bytes 262176 | tf_op jit(solution)/shard_map/all_to_all | solution.py:142
  46.5 10.9 %while.37 = (s32[]{:T(128)}, f32[2,16,64,128]{3,2,1,0:T(8,128)}, s32[2]{0:T(128)S(1)}, s32[16,2]{0,1:T(2,128)S(1)}, bf16[16,128,256]{2,1,0:T(8,128)(2,1)S(1)}, /*index=5*/bf16[16,64,128]{2,1,0:T(8,128)(2,1)}) while((s32[]{:T(128)}, f32[2,16,64,128]{3,2,1,0:T(8,128)}, s32[2]{0:T(128)S(1)}, s32[16,2]{0,1:T(2,128)S(1)}, ...), condition=%wide.region_1.3_spmd.clone, body=%wide.region_0.2_spmd.sunk.clone | while | flops 33948772 | bytes 3412883 | solution.py:50
  49.1 0.6 gather_fusion
  49.7 2.3 fusion.75
  54.5 0.6 gather_fusion
  55.2 2.3 fusion.75
  57.4 1.6 select_reduce_fusion
  59.1 1.7 fusion.24
  60.7 1.6 fusion.32
  62.3 1.8 all-gather.2.cloned.1.call-done
  64.1 2.4 fusion.22
  66.6 0.8 copy.32
  67.4 5.7 %all-to-all-start.3 = ((bf16[16,64,128]{2,1,0:T(8,128)(2,1)}), bf16[16,64,128]{2,1,0:T(8,128)(2,1)}, u32[]{:S(2)}, u32[]{:S(2)}) async-start(bf16[16,64,128]{2,1,0:T(8,128)(2,1)} %bitcast.19), calls=%async_computation.3 | async-start | bytes 524288 | tf_op jit(solution)/shard_map/all_to_all | solution.py:144
  73.1 9.1 %while.38 = (s32[]{:T(128)}, f32[16,64,128]{2,1,0:T(8,128)S(1)}, s32[2]{0:T(128)S(1)}, bf16[2,16,64,128]{3,2,1,0:T(8,128)(2,1)}, s32[16,2]{0,1:T(2,128)S(1)}, /*index=5*/bf16[16,128,256]{2,1,0:T(8,128)(2,1)S(1)}) while((s32[]{:T(128)}, f32[16,64,128]{2,1,0:T(8,128)S(1)}, s32[2]{0:T(128)S(1)}, ...), condition=%wide.region_5.7_spmd.clone.clone, body=%wide.region_4.6_spmd.clone.sunk.clone | while | flops 34079844 | bytes 3937181 | solution.py:72
  73.1 0.6 dynamic_slice.83
  75.7 0.6 gather_fusion.1
  76.3 1.3 convolution_add_fusion.6
  77.7 0.6 dynamic_slice.83
  80.2 0.6 gather_fusion.1
  80.8 1.3 convolution_add_fusion.6
  82.2 1.0 all-to-all-done.3
  83.2 1.2 multiply_reduce_fusion
  84.3 14.8 %all_to_all.31 = bf16[16,64,128]{2,1,0:T(8,128)(2,1)S(1)} all-to-all(bf16[16,64,128]{2,1,0:T(8,128)(2,1)S(1)} %get-tuple-element.247), channel_id=1, replica_groups=mesh['dp'=2,'ctx'=16] {'ctx'}, dimensions={0} | all-to-all | bytes 524288 | tf_op jit(solution)/shard_map/all_to_all | solution.py:159
  99.4 0.7 copy-done.4
  100.0 2.7 %fusion.25 = f32[1024,1024]{1,0:T(8,128)} fusion(bf16[1,128,1024]{2,1,0:T(8,128)(2,1)S(1)} %copy-done, bf16[16,8,8,128]{3,2,1,0:T(8,128)(2,1)S(1)} %bitcast.153), kind=kOutput, calls=%fused_computation.62 | convolution fusion | flops 268435456 | bytes 4718592 | tf_op jit(solution)/shard_map/dot_general | solution.py:162
  102.8 1.6 broadcast_in_dim.55
  104.3 34.5 %while.39 = (s32[]{:T(128)}, f32[16,64,128]{2,1,0:T(8,128)}, f32[16,128,256]{2,1,0:T(8,128)}, s32[2]{0:T(128)S(1)}, f32[2,16,64,128]{3,2,1,0:T(8,128)}, /*index=...) while((s32[]{:T(128)}, f32[16,64,128]{2,1,0:T(8,128)}, ...), condition=%wide.region_9.11_spmd.clone.clone, body=%wide.region_7.10_spmd.clone.sunk.clone | while | flops 136447120 | bytes 25440924 | solution.py:114
  106.9 0.6 gather_fusion.2
  107.7 1.6 fusion.85
  109.3 1.1 convolution_add_fusion.7
  110.4 1.3 fusion.88
  111.7 1.4 fusion.87
  113.1 1.5 pad_maximum_fusion.4
  114.6 1.9 copy.55
  116.6 4.6 %scatter_fusion = f32[16,128,256]{2,1,0:T(8,128)} fusion(f32[16,128,256]{2,1,0:T(8,128)} %get-tuple-element.518, s32[16]{0:T(128)S(1)} %fusion.86, f32[16,128,256]{2,1,0:T(8,128)S(1)} %copy.55), kind=kCustom, calls=%fused_computation.3.clone.clone.1.clone | custom fusion | flops 524288 | bytes 6291520 | tf_op jit(solution)/shard_map/while/body/eval_jaxpr/scatter-add | solution.py:105
  123.8 0.6 gather_fusion.2
  124.6 1.6 fusion.85
  126.2 2.1 convolution_add_fusion.7
  128.3 1.3 fusion.88
  129.6 1.4 fusion.87
  131.0 1.5 pad_maximum_fusion.4
  132.5 1.9 copy.55
  134.4 4.4 %scatter_fusion = f32[16,128,256]{2,1,0:T(8,128)} fusion(f32[16,128,256]{2,1,0:T(8,128)} %get-tuple-element.518, s32[16]{0:T(128)S(1)} %fusion.86, f32[16,128,256]{2,1,0:T(8,128)S(1)} %copy.55), kind=kCustom, calls=%fused_computation.3.clone.clone.1.clone | custom fusion | flops 524288 | bytes 6291520 | tf_op jit(solution)/shard_map/while/body/eval_jaxpr/scatter-add | solution.py:105
  138.8 2.0 multiply_convert_fusion.1
  140.8 3.5 %all-to-all-start.4 = ((bf16[16,64,128]{2,1,0:T(8,128)(2,1)}), bf16[16,64,128]{2,1,0:T(8,128)(2,1)S(1)}, u32[]{:S(2)}, u32[]{:S(2)}) async-start(bf16[16,64,128]{2,1,0:T(8,128)(2,1)} %multiply_convert_fusion.1), calls=%async_computation.4 | async-start | bytes 524288 | tf_op jit(solution)/shard_map/all_to_all | solution.py:167
  144.3 1.3 slice.57
  145.8 1.1 pad_maximum_fusion.1
  146.9 7.7 %all-to-all-done.4 = bf16[16,64,128]{2,1,0:T(8,128)(2,1)S(1)} async-done(((bf16[16,64,128]{2,1,0:T(8,128)(2,1)}), bf16[16,64,128]{2,1,0:T(8,128)(2,1)S(1)}, u32[]{:S(2)}, u32[]{:S(2)}) %all-to-all-start.4) | async-done | bytes 262176 | tf_op jit(solution)/shard_map/all_to_all | solution.py:167
  154.6 0.7 copy-done.5
  155.3 4.1 %all-to-all-start.5 = ((bf16[16,128,256]{2,1,0:T(8,128)(2,1)}), bf16[16,128,256]{2,1,0:T(8,128)(2,1)S(1)}, u32[]{:S(2)}, u32[]{:S(2)}) async-start(bf16[16,128,256]{2,1,0:T(8,128)(2,1)} %pad_maximum_fusion.1), calls=%async_computation.5 | async-start | bytes 2097152 | tf_op jit(solution)/shard_map/all_to_all | solution.py:168
  159.4 1.8 copy.52
  161.2 1.8 broadcast_in_dim_reshape.3
  163.0 2.1 fusion.21
  165.1 20.8 %all-to-all-done.5 = bf16[16,128,256]{2,1,0:T(8,128)(2,1)S(1)} async-done(((bf16[16,128,256]{2,1,0:T(8,128)(2,1)}), bf16[16,128,256]{2,1,0:T(8,128)(2,1)S(1)}, u32[]{:S(2)}, u32[]{:S(2)}) %all-to-all-start.5) | async-done | bytes 1048608 | tf_op jit(solution)/shard_map/all_to_all | solution.py:168
  186.3 0.9 copy.37
  187.4 0.9 copy.36
  188.2 56.5 %reduce-scatter.2.cloned.1.call-done = f32[32,1024]{1,0:T(8,128)} async-done(((f32[1024,1024]{1,0:T(8,128)}), f32[32,1024]{1,0:T(8,128)}) %reduce-scatter.2.cloned.1.call-update) | async-done | bytes 131088 | tf_op jit(solution)/shard_map/reduce_scatter | solution.py:165
  (57 shorter events, 4.3 us)
Async XLA Ops:
  7.2 57.0 %copy-start = (bf16[1,128,1024]{2,1,0:T(8,128)(2,1)S(1)}, bf16[1,128,1024]{2,1,0:T(8,128)(2,1)}, u32[]{:S(2)}) copy-start(bf16[1,128,1024]{2,1,0:T(8,128)(2,1)} %param.19) | copy-start | bytes 786436
  7.2 56.9 %all-gather.2.cloned.1.call-start = ((), (), s32[]{:S(2)}) async-start(), calls=%async_computation.7 | async-start | bytes 3145728 | tf_op jit(solution)/shard_map/all_gather | solution.py:129
  9.3 21.9 %copy-start.6 = (bf16[1,128,1024]{2,1,0:T(8,128)(2,1)S(1)}, bf16[1,128,1024]{2,1,0:T(8,128)(2,1)}, u32[]{:S(2)}) copy-start(bf16[1,128,1024]{2,1,0:T(8,128)(2,1)} %param.15) | copy-start | bytes 786436
  31.1 6.7 %collective-permute-start = (bf16[1,16,64,256]{3,2,0,1:T(8,128)(2,1)S(1)}, bf16[1,16,64,256]{3,2,0,1:T(8,128)(2,1)S(1)}, u32[]{:S(2)}, u32[]{:S(2)}) collective-permute-start(bf16[1,16,64,256]{3,2,0,1:T(8,128)(2,1)S(1)} %bitcast.155), channel_id=1, source_target_pairs={{0,1},{1,0},{2,3},{3,2},{4,5},{5,4},{6,7},{7,6},{8,9},{9,8},{10,11... | collective-permute-start | bytes 1572872 | tf_op jit(solution)/shard_map/ppermute | solution.py:19
  32.0 14.5 %all-to-all-start.1 = ((bf16[16,64,128]{2,1,0:T(8,128)(2,1)}), bf16[16,64,128]{2,1,0:T(8,128)(2,1)}, u32[]{:S(2)}, u32[]{:S(2)}) async-start(bf16[16,64,128]{2,1,0:T(8,128)(2,1)} %bitcast.12), calls=%async_computation.1 | async-start | bytes 524288 | tf_op jit(solution)/shard_map/all_to_all | solution.py:142
  57.4 3.3 %copy-start.2 = (f32[2,16,64,128]{3,2,1,0:T(8,128)S(1)}, f32[2,16,64,128]{3,2,1,0:T(8,128)}, u32[]{:S(2)}) copy-start(f32[2,16,64,128]{3,2,1,0:T(8,128)} %get-tuple-element.128) | copy-start | bytes 3145732
  67.4 15.8 %all-to-all-start.3 = ((bf16[16,64,128]{2,1,0:T(8,128)(2,1)}), bf16[16,64,128]{2,1,0:T(8,128)(2,1)}, u32[]{:S(2)}, u32[]{:S(2)}) async-start(bf16[16,64,128]{2,1,0:T(8,128)(2,1)} %bitcast.19), calls=%async_computation.3 | async-start | bytes 524288 | tf_op jit(solution)/shard_map/all_to_all | solution.py:144
  73.1 171.6 %reduce-scatter.2.cloned.1.call-start = ((), (), s32[]{:S(2)}) async-start(), calls=%async_computation.8 | async-start | bytes 4325376 | tf_op jit(solution)/shard_map/reduce_scatter | solution.py:165
  99.3 0.7 copy-start.4
  138.8 6.8 %copy-start.1 = (f32[16,128,256]{2,1,0:T(8,128)S(1)}, f32[16,128,256]{2,1,0:T(8,128)}, u32[]{:S(2)}) copy-start(f32[16,128,256]{2,1,0:T(8,128)} %get-tuple-element.131) | copy-start | bytes 6291460
  140.8 13.9 %all-to-all-start.4 = ((bf16[16,64,128]{2,1,0:T(8,128)(2,1)}), bf16[16,64,128]{2,1,0:T(8,128)(2,1)S(1)}, u32[]{:S(2)}, u32[]{:S(2)}) async-start(bf16[16,64,128]{2,1,0:T(8,128)(2,1)} %multiply_convert_fusion.1), calls=%async_computation.4 | async-start | bytes 524288 | tf_op jit(solution)/shard_map/all_to_all | solution.py:167
  146.9 16.1 %copy-start.3 = (bf16[1024,1024]{1,0:T(8,128)(2,1)S(1)}, bf16[1024,1024]{1,0:T(8,128)(2,1)}, u32[]{:S(2)}) copy-start(bf16[1024,1024]{1,0:T(8,128)(2,1)} %all-gather.2.cloned.1.call-done) | copy-start | bytes 6291460
  154.6 0.7 copy-start.5
  155.3 30.5 %all-to-all-start.5 = ((bf16[16,128,256]{2,1,0:T(8,128)(2,1)}), bf16[16,128,256]{2,1,0:T(8,128)(2,1)S(1)}, u32[]{:S(2)}, u32[]{:S(2)}) async-start(bf16[16,128,256]{2,1,0:T(8,128)(2,1)} %pad_maximum_fusion.1), calls=%async_computation.5 | async-start | bytes 2097152 | tf_op jit(solution)/shard_map/all_to_all | solution.py:168
Sparse Core Ops, SparseCore 0:
  31.3 32.8 all-gather.1
  102.9 141.7 reduce-scatter.1
where the time goes:
time: 253 us; the launch traced here: 252 us
  waiting for transfers between devices  96.3 us (38%)
  blocking collectives  36.5 us (14%)
  local copies, waits for them, and re-layouts  26.5 us (10%)
  matrix products  26.2 us (10%)
  other arithmetic  22 us (9%)
  starting transfers between devices  17.8 us (7%)
  between operations  14.3 us (6%)
  loops' own time  11.9 us (5%)
    reduce_scatter x1, waiting for transfers between devices, local(): lax.psum_scatter(weight_term, ('dp', 'ctx'), scatter_dimension=0, tiled=T...  56.5 us
    all_to_all x1, blocking collectives, local(): lax.all_to_all(kv_piece, 'ctx', split_axis=0, concat_axis=0, tiled=True)  21.7 us
    all_to_all x1, waiting for transfers between devices, local(): lax.all_to_all(kv_part, 'ctx', split_axis=0, concat_axis=0, tiled=True)  20.8 us
    all_to_all x1, blocking collectives, local(): lax.all_to_all(attn, 'ctx', split_axis=0, concat_axis=0, tiled=True)  14.8 us
    scatter-add x2, other arithmetic, back_step(): kv_acc.at[idx[:, slot_index]]  8.98 us
    all_to_all x1, waiting for transfers between devices, local(): lax.all_to_all(q_send, 'ctx', split_axis=0, concat_axis=0, tiled=True)  8.57 us
    all_to_all x1, waiting for transfers between devices, local(): lax.all_to_all(query_gradient, 'ctx', split_axis=0, concat_axis=0, tiled=...  7.69 us
    all_to_all x1, starting transfers between devices, local(): lax.all_to_all(do_send, 'ctx', split_axis=0, concat_axis=0, tiled=True)  5.66 us
  transfers between devices with their start and end apart: 7, of which 6 were waited for; matrix products, arithmetic and copies ran while one was open for 25% of the time, Pallas kernels for 0%

commit v1 on v0

v1 whole, which is shorter than its diff:
```python
import functools

import jax
import jax.numpy as jnp
from jax import lax
from jax.experimental import pallas as pl
from jax.experimental.pallas import tpu as pltpu
from jax.sharding import PartitionSpec as P

HEADS = 8
HEAD_SIZE = 128
BLOCK = 128
SCALE = HEAD_SIZE ** (-0.5)
F32 = jnp.float32
BF16 = jnp.bfloat16
VMEM = pl.BlockSpec(memory_space=pltpu.VMEM)
SMEM = pl.BlockSpec(memory_space=pltpu.SMEM)
NN = (((1,), (0,)), ((), ()))
NT = (((1,), (1,)), ((), ()))
TN = (((0,), (0,)), ((), ()))


def dot(a, b, dims):
    return lax.dot_general(a, b, dims, preferred_element_type=F32)


def call(body, outs, scratch=(), n_smem=0, n_vmem=0, flops=0, moved=0, exps=0, name=None):
    many = isinstance(outs, (list, tuple))
    return pl.pallas_call(
        body,
        out_shape=outs,
        in_specs=[SMEM] * n_smem + [VMEM] * n_vmem,
        out_specs=[VMEM] * len(outs) if many else VMEM,
        scratch_shapes=list(scratch),
        compiler_params=pltpu.CompilerParams(vmem_limit_bytes=32 * 2**20),
        cost_estimate=pl.CostEstimate(flops=flops, bytes_accessed=moved, transcendentals=exps),
        name=name,
    )


def shape(dims, dtype=BF16):
    return jax.ShapeDtypeStruct(dims, dtype)


def head_lanes(h):
    return slice(h * HEAD_SIZE, (h + 1) * HEAD_SIZE)


def pack_body(q_ref, k_ref, v_ref, send_ref):
    for h in range(HEADS):
        for part, ref in enumerate((q_ref, k_ref, v_ref)):
            send_ref[h, part * BLOCK : (part + 1) * BLOCK, :] = ref[0, :, head_lanes(h)]


def unpack_body(recv_ref, q_ref, k_ref, v_ref):
    for h in range(HEADS):
        for part, ref in enumerate((q_ref, k_ref, v_ref)):
            ref[0, :, head_lanes(h)] = recv_ref[h, part * BLOCK : (part + 1) * BLOCK, :]


def d_out_body(ids_ref, grad_ref, near_ref, far_ref, d_out_ref):
    half = HEADS // 2
    for side, ref in enumerate((near_ref, far_ref)):
        for i in range(half):
            d_out_ref[(ids_ref[2] ^ side) * half + i] = dot(
                grad_ref[0], ref[i * HEAD_SIZE : (i + 1) * HEAD_SIZE, :], NT
            ).astype(BF16)


def output_body(ids_ref, *refs):
    *attn_refs, near_ref, far_ref, out_ref = refs
    half = HEADS // 2
    total = jnp.zeros(out_ref.shape[1:], F32)
    for side, ref in enumerate((near_ref, far_ref)):
        for i in range(half):
            total += dot(
                attn_refs[0][(ids_ref[2] ^ side) * half + i, BLOCK:, :],
                ref[i * HEAD_SIZE : (i + 1) * HEAD_SIZE, :],
                NN,
            )
    out_ref[0] = total.astype(BF16)


def gather_kv(own_ref, other_ref, kv_ref):
    kv_ref[0] = own_ref[:, BLOCK:, :]
    for r in range(other_ref.shape[0]):
        kv_ref[r + 1] = other_ref[r]


def second_block(ids_ref, kb_ref, j, group):
    block = kb_ref[0, ids_ref[0], j * group + ids_ref[1], 1]
    return (block % group) ^ ids_ref[1], block // group


def forward_body(group, ids_ref, kb_ref, cnt_ref, own_ref, other_ref, d_out_ref, send_ref, probs_ref, kv_ref):
    gather_kv(own_ref, other_ref, kv_ref)
    for h in range(HEADS):
        send_ref[h, :BLOCK, :] = d_out_ref[h]
    for j in range(HEADS):
        r, jb = second_block(ids_ref, kb_ref, j, group)
        both = cnt_ref[0, ids_ref[0], j * group + ids_ref[1]] > 1
        q = own_ref[j, :BLOCK, :]
        s0 = dot(q, kv_ref[0, j, :BLOCK, :], NT) * SCALE
        s1 = dot(q, kv_ref[r, jb, :BLOCK, :], NT) * SCALE
        s1 = jnp.where(both, s1, -jnp.inf)
        top = jnp.max(jnp.maximum(s0, s1), axis=-1, keepdims=True)
        e0 = jnp.exp(s0 - top)
        e1 = jnp.exp(s1 - top)
        inverse = 1.0 / jnp.sum(e0 + e1, axis=-1, keepdims=True)
        p0 = e0 * inverse
        p1 = e1 * inverse
        probs_ref[j, :, :BLOCK] = p0
        probs_ref[j, :, BLOCK:] = p1
        send_ref[j, BLOCK:, :] = (
            dot(p0.astype(BF16), kv_ref[0, j, BLOCK:, :], NN)
            + dot(p1.astype(BF16), kv_ref[r, jb, BLOCK:, :], NN)
        ).astype(BF16)


def backward_body(
    group, ids_ref, kb_ref, own_ref, other_ref, sent_ref, recv_ref, probs_ref,
    dq_ref, near_ref, far_ref, kv_ref, acc_ref,
):
    gather_kv(own_ref, other_ref, kv_ref)
    for r in range(1, group):
        acc_ref[r] = jnp.zeros(acc_ref.shape[1:], F32)
    second = []
    for j in range(HEADS):
        r, jb = second_block(ids_ref, kb_ref, j, group)
        q = own_ref[j, :BLOCK, :]
        do = recv_ref[j, :BLOCK, :]
        delta = jnp.sum(
            do.astype(F32) * sent_ref[j, BLOCK:, :].astype(F32), axis=-1, keepdims=True
        )
        p0 = probs_ref[j, :, :BLOCK]
        p1 = probs_ref[j, :, BLOCK:]
        ds0 = (p0 * (dot(do, kv_ref[0, j, BLOCK:, :], NT) - delta)).astype(BF16)
        ds1 = (p1 * (dot(do, kv_ref[r, jb, BLOCK:, :], NT) - delta)).astype(BF16)
        dq_ref[j] = (
            (dot(ds0, kv_ref[0, j, :BLOCK, :], NN) + dot(ds1, kv_ref[r, jb, :BLOCK, :], NN)) * SCALE
        ).astype(BF16)
        acc_ref[0, j, :BLOCK, :] = dot(ds0, q, TN)
        acc_ref[0, j, BLOCK:, :] = dot(p0.astype(BF16), do, TN)
        second.append((r, jb, dot(ds1, q, TN), dot(p1.astype(BF16), do, TN)))
    for r, jb, dk, dv in second:
        acc_ref[r, jb, :BLOCK, :] += dk
        acc_ref[r, jb, BLOCK:, :] += dv
    near_ref[:, :BLOCK, :] = acc_ref[0, :, :BLOCK, :] * SCALE
    near_ref[:, BLOCK:, :] = acc_ref[0, :, BLOCK:, :]
    for r in range(1, group):
        far_ref[r - 1, :, :BLOCK, :] = (acc_ref[r, :, :BLOCK, :] * SCALE).astype(BF16)
        far_ref[r - 1, :, BLOCK:, :] = acc_ref[r, :, BLOCK:, :].astype(BF16)


def combine_body(dq_ref, near_ref, arrived_ref, send_ref):
    send_ref[:, :BLOCK, :] = dq_ref[...]
    total = near_ref[...]
    for r in range(arrived_ref.shape[0]):
        total += arrived_ref[r].astype(F32)
    send_ref[:, BLOCK:, :] = total.astype(BF16)


def grad_weight_body(
    ids_ref, mine_ref, pair_ref, grad_ref, pair_grad_ref,
    a_keep_ref, a_send_ref, b_keep_ref, b_send_ref, rows_ref, both_ref,
):
    rows_ref[:BLOCK] = grad_ref[0]
    rows_ref[BLOCK:] = pair_grad_ref[0]
    d, z, y, c = ids_ref[2], ids_ref[3], ids_ref[4], ids_ref[5]
    for zr in range(4):
        for dr in range(2):
            h = (dr ^ d) * 4 + (zr ^ z)
            attn = jnp.concatenate([mine_ref[h, BLOCK:, :], pair_ref[h, BLOCK:, :]], axis=0)
            slot = zr * 2 + dr
            both_ref[slot] = dot(attn, rows_ref[...], TN)
            for yr in range(2):
                first = pl.multiple_of((yr ^ y) * 64 + c * 32, 32)
                piece = both_ref[slot, pl.ds(first, 32), :].astype(BF16)
                if zr < 2:
                    (a_send_ref if dr else a_keep_ref)[zr, yr] = piece
                else:
                    (b_send_ref if yr else b_keep_ref)[dr, zr - 2] = piece


def ctx_swap(x, mask):
    n = lax.axis_size("ctx")
    return lax.ppermute(x, "ctx", [(i, i ^ mask) for i in range(n)])


def dp_swap(x):
    return lax.ppermute(x, "dp", [(0, 1), (1, 0)])


def members(x, group):
    return jnp.stack([ctx_swap(x, r) for r in range(1, group)])


def reduce_small_mesh(ids, back, out_grad):
    columns = out_grad.shape[-1]
    pair = ctx_swap(back, 1)
    pair_grad = ctx_swap(out_grad, 1)
    piece = shape((2, 2, 32, columns))
    a_keep, a_send, b_keep, b_send = call(
        grad_weight_body,
        [piece] * 4,
        scratch=[
            pltpu.VMEM((2 * BLOCK, columns), BF16),
            pltpu.VMEM((HEADS, HEAD_SIZE, columns), F32),
        ],
        n_smem=1, n_vmem=4, flops=2**29, moved=3 * 2**20, name="grad_weight",
    )(ids, back, pair, out_grad, pair_grad)
    a = a_keep.astype(F32) + dp_swap(a_send).astype(F32)
    b = b_keep.astype(F32) + ctx_swap(b_send, 2).astype(F32)
    a = a[:, 0] + ctx_swap(a[:, 1].astype(BF16), 2).astype(F32)
    b = b[0] + dp_swap(b[1].astype(BF16)).astype(F32)
    return (
        a[0]
        + ctx_swap(a[1].astype(BF16), 4).astype(F32)
        + ctx_swap(b[0].astype(BF16), 8).astype(F32)
        + ctx_swap(b[1].astype(BF16), 12).astype(F32)
    )


def local(queries, keys, values, out_weight, out_grad, key_blocks, block_counts):
    ctx_count = lax.axis_size("ctx")
    dp_count = lax.axis_size("dp")
    group = ctx_count // HEADS
    position = lax.axis_index("ctx")
    small = dp_count == 2 and ctx_count == 16
    rank = lax.axis_index("dp") if dp_count == 2 else 0
    ids = jnp.stack(
        [position // group, position % group, rank, position >> 2, position >> 1 & 1, position & 1]
    ).astype(jnp.int32)
    columns = out_grad.shape[-1]
    peers = [[j * group + m for j in range(HEADS)] for m in range(group)]

    def exchange(x):
        return lax.all_to_all(x, "ctx", 0, 0, tiled=True, axis_index_groups=peers)

    if dp_count == 2:
        near, far = out_weight, dp_swap(out_weight)
    else:
        near, far = jnp.split(lax.all_gather(out_weight, "dp", axis=0, tiled=True), 2)

    sent = call(
        pack_body, shape((HEADS, 3 * BLOCK, HEAD_SIZE)), n_vmem=3, moved=3 * 2**19, name="pack"
    )(queries, keys, values)
    own = exchange(sent)
    d_out = call(
        d_out_body, shape((HEADS, BLOCK, HEAD_SIZE)), n_smem=1, n_vmem=3,
        flops=2**28, moved=3 * 2**20, name="d_out",
    )(ids, out_grad, near, far)
    other = members(own[:, BLOCK:, :], group)
    kv_scratch = pltpu.VMEM((group, HEADS, 2 * BLOCK, HEAD_SIZE), BF16)
    send, probs = call(
        functools.partial(forward_body, group),
        [shape((HEADS, 2 * BLOCK, HEAD_SIZE)), shape((HEADS, BLOCK, 2 * BLOCK), F32)],
        scratch=[kv_scratch], n_smem=3, n_vmem=3,
        flops=2**27, moved=3 * 2**20, exps=2**18, name="forward",
    )(ids, key_blocks, block_counts, own, other, d_out)
    back = exchange(send)
    dq, near_kv, far_kv = call(
        functools.partial(backward_body, group),
        [
            shape((HEADS, BLOCK, HEAD_SIZE)),
            shape((HEADS, 2 * BLOCK, HEAD_SIZE), F32),
            shape((group - 1, HEADS, 2 * BLOCK, HEAD_SIZE)),
        ],
        scratch=[kv_scratch, pltpu.VMEM((group, HEADS, 2 * BLOCK, HEAD_SIZE), F32)],
        n_smem=2, n_vmem=5, flops=2**28, moved=2**22, name="backward",
    )(ids, key_blocks, own, other, send, back, probs)
    arrived = jnp.stack([ctx_swap(far_kv[r - 1], r) for r in range(1, group)])
    grads = exchange(
        call(
            combine_body, shape((HEADS, 3 * BLOCK, HEAD_SIZE)), n_vmem=3, moved=3 * 2**20, name="combine"
        )(dq, near_kv, arrived)
    )
    tokens = shape((1, BLOCK, HEADS * HEAD_SIZE))
    grad_queries, grad_keys, grad_values = call(
        unpack_body, [tokens] * 3, n_vmem=1, moved=3 * 2**19, name="unpack"
    )(grads)
    if small:
        grad_weight = reduce_small_mesh(ids, back, out_grad)
    else:
        attn = back[:, BLOCK:, :].transpose(1, 0, 2).reshape(BLOCK, HEADS * HEAD_SIZE)
        grad_weight = lax.psum_scatter(
            dot(attn, out_grad[0], TN), ("dp", "ctx"), scatter_dimension=0, tiled=True
        )
    output = call(
        output_body, shape((1, BLOCK, columns)), n_smem=1, n_vmem=3,
        flops=2**28, moved=3 * 2**20, name="output",
    )(ids, back, near, far)
    return (output, grad_queries, grad_keys, grad_values, grad_weight)


def solution(mesh):
    tokens = P("dp", "ctx", None)
    return jax.shard_map(
        local,
        mesh=mesh,
        in_specs=(
            tokens, tokens, tokens, P("dp", None), tokens,
            P("dp", None, None, None), P("dp", None, None),
        ),
        out_specs=(tokens, tokens, tokens, tokens, P(("dp", "ctx"), None)),
        check_vma=False,
    )
```

time: 253 us -> 106 us (0.42)
  waiting for transfers between devices: 96.3 us -> 33.6 us
  matrix products: 26.2 us -> 0 us
  other arithmetic: 22 us -> 1.81 us
  blocking collectives: 36.5 us -> 18.6 us
  local copies, waits for them, and re-layouts: 26.5 us -> 9.61 us
  Pallas kernels: 0 us -> 16.1 us
  between operations: 14.3 us -> 0.85 us
  loops' own time: 11.9 us -> 0 us
  starting transfers between devices: 17.8 us -> 24.5 us
    reduce_scatter x1 -> x0, waiting for transfers between devices: 56.5 us -> none  [local(): lax.psum_scatter(weight_term, ('dp', 'ctx'), scatter_dimension=0, tiled=T...]
    dot_general x15 -> x0, matrix products: 26.2 us -> none  [the longest x2 4.56 us: scores_at(): jnp.einsum('lqo,lco->lqc', query_heads, selected_entries[..., :HEAD_SIZE]...]
    all_to_all x4 -> x2, waiting for transfers between devices: 38 us -> 18.6 us  [exchange(): return lax.all_to_all(x, 'ctx', 0, 0, tiled=True, axis_index_groups=peers)]
    all_to_all x2 -> x1, blocking collectives: 36.5 us -> 18.6 us  [exchange(): return lax.all_to_all(x, 'ctx', 0, 0, tiled=True, axis_index_groups=peers)]
    pallas_call x0 -> x8, Pallas kernels: none -> 16.1 us  [the longest x1 4.64 us: local(): call(functools.partial(forward_body, group), [shape((HEADS, 2 * BLOCK, HE...]
    ppermute x1 -> x12, waiting for transfers between devices: 0.01 us -> 15 us  [the longest x9 7.55 us: ctx_swap(): return lax.ppermute(x, 'ctx', [(i, i ^ mask) for i in range(n)])]
    ppermute x1 -> x12, starting transfers between devices: 0.02 us -> 13.5 us  [the longest x9 8.89 us: ctx_swap(): return lax.ppermute(x, 'ctx', [(i, i ^ mask) for i in range(n)])]
    another operation x3 -> x0, loops' own time: 11.9 us -> none  [the longest x1 4.02 us: attend_local(): (query_gradient, kv_acc), _ = lax.scan(back_step, start, jnp.arange(SLOTS))]
  transfers between devices with their start and end apart: 7 -> 14, of which waited for: 6 -> 6; matrix products, arithmetic and copies ran while one was open for 25% -> 4% of each run, Pallas kernels for 0% -> 9%
where the time goes in v1:
time: 106 us; the launch traced here: 105 us
  waiting for transfers between devices  33.6 us (32%)
  starting transfers between devices  24.5 us (23%)
  blocking collectives  18.6 us (18%)
  Pallas kernels  16.1 us (15%)
  local copies, waits for them, and re-layouts  9.61 us (9%)
  other arithmetic  1.81 us (2%)
    all_to_all x2, waiting for transfers between devices, exchange(): return lax.all_to_all(x, 'ctx', 0, 0, tiled=True, axis_index_groups=peers)  18.6 us
    all_to_all x1, blocking collectives, exchange(): return lax.all_to_all(x, 'ctx', 0, 0, tiled=True, axis_index_groups=peers)  18.6 us
    all_to_all x2, starting transfers between devices, exchange(): return lax.all_to_all(x, 'ctx', 0, 0, tiled=True, axis_index_groups=peers)  11 us
    ppermute x9, starting transfers between devices, ctx_swap(): return lax.ppermute(x, 'ctx', [(i, i ^ mask) for i in range(n)])  8.89 us
    unnamed x33, local copies, waits for them, and re-layouts  7.63 us
    ppermute x9, waiting for transfers between devices, ctx_swap(): return lax.ppermute(x, 'ctx', [(i, i ^ mask) for i in range(n)])  7.55 us
    ppermute x3, waiting for transfers between devices, dp_swap(): return lax.ppermute(x, 'dp', [(0, 1), (1, 0)])  7.4 us
    ppermute x3, starting transfers between devices, dp_swap(): return lax.ppermute(x, 'dp', [(0, 1), (1, 0)])  4.66 us
  transfers between devices with their start and end apart: 14, of which 6 were waited for; matrix products, arithmetic and copies ran while one was open for 4% of the time, Pallas kernels for 9%

profile of v1, /device:TPU:0, one launch (start us, length us, event | category | flops | bytes accessed | tf_op | source)
XLA Modules:
  0.0 105.0 jit_solution(11245955919890496660)
XLA Ops:
  0.6 0.0 copy-start.5
  0.6 0.9 copy-done.5
  1.6 0.9 copy-done.6
  2.5 0.9 copy-done.7
  3.5 1.0 pack.1
  4.5 7.4 %all-to-all-start = ((bf16[8,384,128]{2,1,0:T(8,128)(2,1)}), bf16[8,384,128]{2,1,0:T(8,128)(2,1)S(1)}, u32[]{:S(2)}, u32[]{:S(2)}) async-start(bf16[8,384,128]{2,1,0:T(8,128)(2,1)} %pack.1), calls=%async_computation | async-start | bytes 1572864 | tf_op jit(solution)/shard_map/all_to_all | solution.py:238
  11.9 0.0 copy-done
  11.9 1.6 %collective-permute-start.1 = (bf16[512,1024]{1,0:T(8,128)(2,1)S(1)}, bf16[512,1024]{1,0:T(8,128)(2,1)S(1)}, u32[]{:S(2)}, u32[]{:S(2)}) collective-permute-start(bf16[512,1024]{1,0:T(8,128)(2,1)S(1)} %copy-done), channel_id=1, source_target_pairs={{0,16},{16,0},{1,17},{17,1},{2,18},{18,2},{3,19},{19,3},{4,20},{20... | collective-permute-start | bytes 3145736 | tf_op jit(solution)/shard_map/ppermute | solution.py:191
  13.5 18.6 %all-to-all-done.own_ref = bf16[8,384,128]{2,1,0:T(8,128)(2,1)S(1)} async-done(((bf16[8,384,128]{2,1,0:T(8,128)(2,1)}), bf16[8,384,128]{2,1,0:T(8,128)(2,1)S(1)}, u32[]{:S(2)}, u32[]{:S(2)}) %all-to-all-start) | async-done | bytes 786464 | tf_op jit(solution)/shard_map/all_to_all | solution.py:238
  32.1 0.8 slice.41
  32.9 0.0 collective-permute-start
  32.9 0.7 copy-done.15
  33.6 0.1 copy.12.kb_ref
  33.8 0.1 stack.33.ids_ref
  33.9 2.8 %collective-permute-done.1.far_ref.refs_2_ = bf16[512,1024]{1,0:T(8,128)(2,1)S(1)} collective-permute-done((bf16[512,1024]{1,0:T(8,128)(2,1)S(1)}, bf16[512,1024]{1,0:T(8,128)(2,1)S(1)}, u32[]{:S(2)}, u32[]{:S(2)}) %collective-permute-start.1) | collective-permute-done | bytes 1048608 | tf_op jit(solution)/shard_map/ppermute | solution.py:191
  36.6 0.9 copy-done.12
  37.6 1.2 %d_out.1.d_out_ref = bf16[8,128,128]{2,1,0:T(8,128)(2,1)S(1)} custom-call(s32[6]{0:T(128)S(1)} %stack.33.ids_ref, bf16[1,128,1024]{2,1,0:T(8,128)(2,1)S(1)} %copy-done.12, bf16[512,1024]{1,0:T(8,128)(2,1)S(1)} %copy-done, bf16[512,1024]{1,0:T(8,128)(2,1)S(1)} %collective-permute-done.1.far_ref.refs_2_), custom_call_target="tpu_custom_call" | custom-call | flops 268435456 | bytes 3145728 | tf_op jit(solution)/shard_map/d_out/pallas_call | solution.py:249
  38.8 0.0 collective-permute-done
  38.8 0.0 copy-start.2
  38.8 0.0 copy-done.14
  38.9 4.6 %forward.1 = (bf16[8,256,128]{2,1,0:T(8,128)(2,1)S(1)}, f32[8,128,256]{2,1,0:T(8,128)S(1)}) custom-call(s32[6]{0:T(128)S(1)} %stack.33.ids_ref, s32[1,8,16,2]{3,2,1,0:T(8,128)S(1)} %copy.12.kb_ref, s32[1,8,16]{2,1,0:T(8,128)S(1)} %copy-done.14, bf16[8,384,128]{2,1,0:T(8,128)(2,1)S(1)} %all-to-all-done.own_ref, bf16[1,8,256,128]{3,2,1,0:T(8,128)(2,1)S(1)} %bitcast.37, ...), custom_call_target="tpu_custom_call" | custom-call | flops 134217728 | bytes 3145728 | tf_op jit(solution)/shard_map/forward/pallas_call | solution.py:255
  43.5 0.0 copy-done.2
  43.5 0.0 copy-start.13
  43.5 0.0 copy-start.3
  43.5 18.6 %all_to_all.15.refs_0_.recv_ref.mine_ref = bf16[8,256,128]{2,1,0:T(8,128)(2,1)S(1)} all-to-all(bf16[8,256,128]{2,1,0:T(8,128)(2,1)S(1)} %get-tuple-element.17.sent_ref), channel_id=1, replica_groups={{0,2,4,6,8,10,12,14},{1,3,5,7,9,11,13,15},{16,18,20,22,24,26,28,30},{17..., dimensions={0} | all-to-all | bytes 1048576 | tf_op jit(solution)/shard_map/all_to_all | solution.py:238
  62.1 0.0 collective-permute-start.3
  62.1 0.0 copy-done.13
  62.1 0.5 collective-permute-start.4
  62.6 4.0 %backward.1 = (bf16[8,128,128]{2,1,0:T(8,128)(2,1)S(1)}, f32[8,256,128]{2,1,0:T(8,128)S(1)}, bf16[1,8,256,128]{3,2,1,0:T(8,128)(2,1)S(1)}) custom-call(s32[6]{0:T(128)S(1)} %stack.33.ids_ref, s32[1,8,16,2]{3,2,1,0:T(8,128)S(1)} %copy.12.kb_ref, bf16[8,384,128]{2,1,0:T(8,128)(2,1)S(1)} %all-to-all-done.own_ref, bf16[1,8,256,128]{3,2,1,0:T(8,128)(2,1)S(1)} %bitcast.38, ...), custom_call_target="tpu_custom_call" | custom-call | flops 268435456 | bytes 4194304 | tf_op jit(solution)/shard_map/backward/pallas_call | solution.py:262
  66.7 0.1 collective-permute-start.2
  66.7 0.0 collective-permute-done.4.pair_grad_ref
  66.7 0.0 collective-permute-done.3.pair_ref
  66.8 2.0 %grad_weight.1 = (bf16[2,2,32,1024]{3,2,1,0:T(8,128)(2,1)S(1)}, bf16[2,2,32,1024]{3,2,1,0:T(8,128)(2,1)S(1)}, bf16[2,2,32,1024]{3,2,1,0:T(8,128)(2,1)S(1)}, bf16[2,2,32,1024]{3,2,1,0:T(8,128)(2,1)}) custom-call(s32[6]{0:T(128)S(1)} %stack.33.ids_ref, bf16[8,256,128]{2,1,0:T(8,128)(2,1)S(1)} %all_to_all.15.refs_0_.recv_ref.mine_ref, ...), custom_call_target="tpu_custom_call" | custom-call | flops 536870912 | bytes 3145728 | tf_op jit(solution)/shard_map/grad_weight/pallas_call | solution.py:203
  68.8 0.7 copy-done.4
  69.5 0.7 copy-done.8
  70.2 0.7 copy-done.10
  70.9 1.5 %collective-permute-start.8 = (bf16[2,2,32,1024]{3,2,1,0:T(8,128)(2,1)}, bf16[2,2,32,1024]{3,2,1,0:T(8,128)(2,1)}, u32[]{:S(2)}, u32[]{:S(2)}) collective-permute-start(bf16[2,2,32,1024]{3,2,1,0:T(8,128)(2,1)} %get-tuple-element.28), channel_id=1, source_target_pairs={{0,2},{1,3},{2,0},{3,1},{4,6},{5,7},{6,4},{7,5},{8,10},{9,11},{10,... | collective-permute-start | bytes 786440 | tf_op jit(solution)/shard_map/ppermute | solution.py:187
  72.3 0.0 collective-permute-done.2
  72.4 0.1 combine.1
  72.5 0.9 copy-done.1
  73.3 3.5 %all-to-all-start.2 = ((bf16[8,384,128]{2,1,0:T(8,128)(2,1)}), bf16[8,384,128]{2,1,0:T(8,128)(2,1)S(1)}, u32[]{:S(2)}, u32[]{:S(2)}) async-start(bf16[8,384,128]{2,1,0:T(8,128)(2,1)} %copy-done.1), calls=%async_computation.2 | async-start | bytes 1572864 | tf_op jit(solution)/shard_map/all_to_all | solution.py:238
  76.9 0.0 copy-start.11
  76.9 1.0 copy.15
  77.9 1.6 %collective-permute-start.5 = (bf16[2,2,32,1024]{3,2,0,1:T(8,128)(2,1)S(1)}, bf16[2,2,32,1024]{3,2,0,1:T(8,128)(2,1)S(1)}, u32[]{:S(2)}, u32[]{:S(2)}) collective-permute-start(bf16[2,2,32,1024]{3,2,0,1:T(8,128)(2,1)S(1)} %copy.15), channel_id=1, source_target_pairs={{0,16},{16,0},{1,17},{17,1},{2,18},{18,2},{3,19},{19,3},{4,20},{20... | collective-permute-start | bytes 786440 | tf_op jit(solution)/shard_map/ppermute | solution.py:191
  79.5 0.4 collective-permute-done.8
  79.9 1.0 convert_add_fusion
  80.9 0.0 copy-start.9
  80.9 1.6 %collective-permute-start.9 = (bf16[2,32,1024]{2,1,0:T(8,128)(2,1)S(1)}, bf16[2,32,1024]{2,1,0:T(8,128)(2,1)S(1)}, u32[]{:S(2)}, u32[]{:S(2)}) collective-permute-start(bf16[2,32,1024]{2,1,0:T(8,128)(2,1)S(1)} %fusion.4), channel_id=1, source_target_pairs={{0,16},{16,0},{1,17},{17,1},{2,18},{18,2},{3,19},{19,3},{4,20},{20... | collective-permute-start | bytes 393224 | tf_op jit(solution)/shard_map/ppermute | solution.py:191
  82.5 4.6 %collective-permute-done.5 = bf16[2,2,32,1024]{3,2,0,1:T(8,128)(2,1)S(1)} collective-permute-done((bf16[2,2,32,1024]{3,2,0,1:T(8,128)(2,1)S(1)}, bf16[2,2,32,1024]{3,2,0,1:T(8,128)(2,1)S(1)}, u32[]{:S(2)}, u32[]{:S(2)}) %collective-permute-start.5) | collective-permute-done | bytes 262176 | tf_op jit(solution)/shard_map/ppermute | solution.py:191
  87.1 0.0 copy-done.9
  87.1 0.1 convert_add_fusion.1
  87.2 2.0 %collective-permute-start.6 = (bf16[2,32,1024]{2,1,0:T(8,128)(2,1)S(1)}, bf16[2,32,1024]{2,1,0:T(8,128)(2,1)S(1)}, u32[]{:S(2)}, u32[]{:S(2)}) collective-permute-start(bf16[2,32,1024]{2,1,0:T(8,128)(2,1)S(1)} %fusion.3), channel_id=1, source_target_pairs={{0,2},{1,3},{2,0},{3,1},{4,6},{5,7},{6,4},{7,5},{8,10},{9,11},{10,... | collective-permute-start | bytes 393224 | tf_op jit(solution)/shard_map/ppermute | solution.py:187
  89.2 0.0 collective-permute-done.9
  89.3 3.5 %collective-permute-start.11 = (bf16[32,1024]{1,0:T(8,128)(2,1)S(1)}, bf16[32,1024]{1,0:T(8,128)(2,1)S(1)}, u32[]{:S(2)}, u32[]{:S(2)}) collective-permute-start(bf16[32,1024]{1,0:T(8,128)(2,1)S(1)} %get-tuple-element.30), channel_id=1, source_target_pairs={{0,12},{1,13},{2,14},{3,15},{4,8},{5,9},{6,10},{7,11},{8,4},{9,5},... | collective-permute-start | bytes 196616 | tf_op jit(solution)/shard_map/ppermute | solution.py:187
  92.8 0.0 collective-permute-start.10
  92.8 1.3 %collective-permute-done.6 = bf16[2,32,1024]{2,1,0:T(8,128)(2,1)S(1)} collective-permute-done((bf16[2,32,1024]{2,1,0:T(8,128)(2,1)S(1)}, bf16[2,32,1024]{2,1,0:T(8,128)(2,1)S(1)}, u32[]{:S(2)}, u32[]{:S(2)}) %collective-permute-start.6) | collective-permute-done | bytes 131104 | tf_op jit(solution)/shard_map/ppermute | solution.py:187
  94.1 1.3 %collective-permute-start.7 = (bf16[32,1024]{1,0:T(8,128)(2,1)S(1)}, bf16[32,1024]{1,0:T(8,128)(2,1)S(1)}, u32[]{:S(2)}, u32[]{:S(2)}) collective-permute-start(bf16[32,1024]{1,0:T(8,128)(2,1)S(1)} %fusion.8), channel_id=1, source_target_pairs={{0,4},{1,5},{2,6},{3,7},{4,0},{5,1},{6,2},{7,3},{8,12},{9,13},{10,... | collective-permute-start | bytes 196616 | tf_op jit(solution)/shard_map/ppermute | solution.py:187
  95.4 1.9 %output.1 = bf16[1,128,1024]{2,1,0:T(8,128)(2,1)} custom-call(s32[6]{0:T(128)S(1)} %stack.33.ids_ref, bf16[8,256,128]{2,1,0:T(8,128)(2,1)S(1)} %all_to_all.15.refs_0_.recv_ref.mine_ref, bf16[512,1024]{1,0:T(8,128)(2,1)S(1)} %copy-done, bf16[512,1024]{1,0:T(8,128)(2,1)S(1)} %collective-permute-done.1.far_ref.refs_2_), custom_call_target="tpu_custom_call" | custom-call | flops 268435456 | bytes 3145728 | tf_op jit(solution)/shard_map/output/pallas_call | solution.py:289
  97.4 0.0 collective-permute-done.11
  97.4 5.8 %collective-permute-done.10 = bf16[32,1024]{1,0:T(8,128)(2,1)S(1)} collective-permute-done((bf16[32,1024]{1,0:T(8,128)(2,1)S(1)}, bf16[32,1024]{1,0:T(8,128)(2,1)S(1)}, u32[]{:S(2)}, u32[]{:S(2)}) %collective-permute-start.10) | collective-permute-done | bytes 65568 | tf_op jit(solution)/shard_map/ppermute | solution.py:187
  103.2 0.0 collective-permute-done.7
  103.2 0.7 fusion.7
  103.9 0.0 all-to-all-done.2.recv_ref
  103.9 1.1 %unpack.1 = (bf16[1,128,1024]{2,1,0:T(8,128)(2,1)}, bf16[1,128,1024]{2,1,0:T(8,128)(2,1)}, bf16[1,128,1024]{2,1,0:T(8,128)(2,1)}) custom-call(bf16[8,384,128]{2,1,0:T(8,128)(2,1)S(1)} %all-to-all-done.2.recv_ref), custom_call_target="tpu_custom_call" | custom-call | bytes 1572864 | tf_op jit(solution)/shard_map/unpack/pallas_call | solution.py:279
  (18 shorter events, 0.1 us)
Async XLA Ops:
  0.6 1.0 copy-start.5
  1.6 0.9 copy-start.6
  2.5 0.9 copy-start.7
  4.5 7.4 %copy-start = (bf16[512,1024]{1,0:T(8,128)(2,1)S(1)}, bf16[512,1024]{1,0:T(8,128)(2,1)}, u32[]{:S(2)}) copy-start(bf16[512,1024]{1,0:T(8,128)(2,1)} %refs_1_.1) | copy-start | bytes 3145732
  4.5 27.6 %all-to-all-start = ((bf16[8,384,128]{2,1,0:T(8,128)(2,1)}), bf16[8,384,128]{2,1,0:T(8,128)(2,1)S(1)}, u32[]{:S(2)}, u32[]{:S(2)}) async-start(bf16[8,384,128]{2,1,0:T(8,128)(2,1)} %pack.1), calls=%async_computation | async-start | bytes 1572864 | tf_op jit(solution)/shard_map/all_to_all | solution.py:238
  11.9 24.7 %collective-permute-start.1 = (bf16[512,1024]{1,0:T(8,128)(2,1)S(1)}, bf16[512,1024]{1,0:T(8,128)(2,1)S(1)}, u32[]{:S(2)}, u32[]{:S(2)}) collective-permute-start(bf16[512,1024]{1,0:T(8,128)(2,1)S(1)} %copy-done), channel_id=1, source_target_pairs={{0,16},{16,0},{1,17},{17,1},{2,18},{18,2},{3,19},{19,3},{4,20},{20... | collective-permute-start | bytes 3145736 | tf_op jit(solution)/shard_map/ppermute | solution.py:191
  32.9 5.9 %collective-permute-start = (bf16[8,256,128]{2,1,0:T(8,128)(2,1)}, bf16[8,256,128]{2,1,0:T(8,128)(2,1)S(1)}, u32[]{:S(2)}, u32[]{:S(2)}) collective-permute-start(bf16[8,256,128]{2,1,0:T(8,128)(2,1)} %slice.41), channel_id=1, source_target_pairs={{0,1},{1,0},{2,3},{3,2},{4,5},{5,4},{6,7},{7,6},{8,9},{9,8},{10,11... | collective-permute-start | bytes 1572872 | tf_op jit(solution)/shard_map/ppermute | solution.py:187
  32.9 0.7 copy-start.15
  36.6 1.0 copy-start.12
  37.6 1.3 %copy-start.14 = (s32[1,8,16]{2,1,0:T(8,128)S(1)}, s32[1,8,16]{2,1,0:T(8,128)}, u32[]{:S(2)}) copy-start(s32[1,8,16]{2,1,0:T(8,128)} %cnt_ref.1) | copy-start | bytes 1540
  38.8 4.7 %copy-start.2 = (bf16[8,256,128]{2,1,0:T(8,128)(2,1)}, bf16[8,256,128]{2,1,0:T(8,128)(2,1)S(1)}, u32[]{:S(2)}) copy-start(bf16[8,256,128]{2,1,0:T(8,128)(2,1)S(1)} %collective-permute-done) | copy-start | bytes 1572868
  43.5 18.6 %copy-start.13 = (bf16[1,128,1024]{2,1,0:T(8,128)(2,1)S(1)}, bf16[1,128,1024]{2,1,0:T(8,128)(2,1)}, u32[]{:S(2)}) copy-start(bf16[1,128,1024]{2,1,0:T(8,128)(2,1)} %grad_ref.3) | copy-start | bytes 786436
  43.5 19.1 %copy-start.3 = (bf16[8,256,128]{2,1,0:T(8,128)(2,1)S(1)}, bf16[8,256,128]{2,1,0:T(8,128)(2,1)}, u32[]{:S(2)}) copy-start(bf16[8,256,128]{2,1,0:T(8,128)(2,1)} %copy-done.2) | copy-start | bytes 1572868
  62.1 4.6 %collective-permute-start.3 = (bf16[8,256,128]{2,1,0:T(8,128)(2,1)S(1)}, bf16[8,256,128]{2,1,0:T(8,128)(2,1)S(1)}, u32[]{:S(2)}, u32[]{:S(2)}) collective-permute-start(bf16[8,256,128]{2,1,0:T(8,128)(2,1)S(1)} %all_to_all.15.refs_0_.recv_ref.mine_ref), channel_id=1, source_target_pairs={{0,1},{1,0},{2,3},{3,2},{4,5},{5,4},{6,7},{7,6},{8,9},{9,8},{10,11... | collective-permute-start | bytes 1572872 | tf_op jit(solution)/shard_map/ppermute | solution.py:187
  62.1 4.6 %collective-permute-start.4 = (bf16[1,128,1024]{2,1,0:T(8,128)(2,1)S(1)}, bf16[1,128,1024]{2,1,0:T(8,128)(2,1)S(1)}, u32[]{:S(2)}, u32[]{:S(2)}) collective-permute-start(bf16[1,128,1024]{2,1,0:T(8,128)(2,1)S(1)} %copy-done.13), channel_id=1, source_target_pairs={{0,1},{1,0},{2,3},{3,2},{4,5},{5,4},{6,7},{7,6},{8,9},{9,8},{10,11... | collective-permute-start | bytes 786440 | tf_op jit(solution)/shard_map/ppermute | solution.py:187
  66.7 5.7 %collective-permute-start.2 = (bf16[8,256,128]{2,1,0:T(8,128)(2,1)S(1)}, bf16[8,256,128]{2,1,0:T(8,128)(2,1)S(1)}, u32[]{:S(2)}, u32[]{:S(2)}) collective-permute-start(bf16[8,256,128]{2,1,0:T(8,128)(2,1)S(1)} %bitcast.40), channel_id=1, source_target_pairs={{0,1},{1,0},{2,3},{3,2},{4,5},{5,4},{6,7},{7,6},{8,9},{9,8},{10,11... | collective-permute-start | bytes 1572872 | tf_op jit(solution)/shard_map/ppermute | solution.py:187
  68.8 0.7 copy-start.4
  69.5 0.7 copy-start.8
  70.2 0.7 copy-start.10
  70.9 9.0 %collective-permute-start.8 = (bf16[2,2,32,1024]{3,2,1,0:T(8,128)(2,1)}, bf16[2,2,32,1024]{3,2,1,0:T(8,128)(2,1)}, u32[]{:S(2)}, u32[]{:S(2)}) collective-permute-start(bf16[2,2,32,1024]{3,2,1,0:T(8,128)(2,1)} %get-tuple-element.28), channel_id=1, source_target_pairs={{0,2},{1,3},{2,0},{3,1},{4,6},{5,7},{6,4},{7,5},{8,10},{9,11},{10,... | collective-permute-start | bytes 786440 | tf_op jit(solution)/shard_map/ppermute | solution.py:187
  72.5 0.9 copy-start.1
  73.3 30.6 %all-to-all-start.2 = ((bf16[8,384,128]{2,1,0:T(8,128)(2,1)}), bf16[8,384,128]{2,1,0:T(8,128)(2,1)S(1)}, u32[]{:S(2)}, u32[]{:S(2)}) async-start(bf16[8,384,128]{2,1,0:T(8,128)(2,1)} %copy-done.1), calls=%async_computation.2 | async-start | bytes 1572864 | tf_op jit(solution)/shard_map/all_to_all | solution.py:238
  76.9 3.0 %copy-start.11 = (bf16[2,2,32,1024]{3,2,1,0:T(8,128)(2,1)S(1)}, bf16[2,2,32,1024]{3,2,1,0:T(8,128)(2,1)}, u32[]{:S(2)}) copy-start(bf16[2,2,32,1024]{3,2,1,0:T(8,128)(2,1)} %copy-done.10) | copy-start | bytes 786436
  77.9 9.2 %collective-permute-start.5 = (bf16[2,2,32,1024]{3,2,0,1:T(8,128)(2,1)S(1)}, bf16[2,2,32,1024]{3,2,0,1:T(8,128)(2,1)S(1)}, u32[]{:S(2)}, u32[]{:S(2)}) collective-permute-start(bf16[2,2,32,1024]{3,2,0,1:T(8,128)(2,1)S(1)} %copy.15), channel_id=1, source_target_pairs={{0,16},{16,0},{1,17},{17,1},{2,18},{18,2},{3,19},{19,3},{4,20},{20... | collective-permute-start | bytes 786440 | tf_op jit(solution)/shard_map/ppermute | solution.py:191
  80.9 6.2 %copy-start.9 = (bf16[2,2,32,1024]{3,2,1,0:T(8,128)(2,1)S(1)}, bf16[2,2,32,1024]{3,2,1,0:T(8,128)(2,1)}, u32[]{:S(2)}) copy-start(bf16[2,2,32,1024]{3,2,1,0:T(8,128)(2,1)} %copy-done.8) | copy-start | bytes 786436
  80.9 8.3 %collective-permute-start.9 = (bf16[2,32,1024]{2,1,0:T(8,128)(2,1)S(1)}, bf16[2,32,1024]{2,1,0:T(8,128)(2,1)S(1)}, u32[]{:S(2)}, u32[]{:S(2)}) collective-permute-start(bf16[2,32,1024]{2,1,0:T(8,128)(2,1)S(1)} %fusion.4), channel_id=1, source_target_pairs={{0,16},{16,0},{1,17},{17,1},{2,18},{18,2},{3,19},{19,3},{4,20},{20... | collective-permute-start | bytes 393224 | tf_op jit(solution)/shard_map/ppermute | solution.py:191
  87.2 6.8 %collective-permute-start.6 = (bf16[2,32,1024]{2,1,0:T(8,128)(2,1)S(1)}, bf16[2,32,1024]{2,1,0:T(8,128)(2,1)S(1)}, u32[]{:S(2)}, u32[]{:S(2)}) collective-permute-start(bf16[2,32,1024]{2,1,0:T(8,128)(2,1)S(1)} %fusion.3), channel_id=1, source_target_pairs={{0,2},{1,3},{2,0},{3,1},{4,6},{5,7},{6,4},{7,5},{8,10},{9,11},{10,... | collective-permute-start | bytes 393224 | tf_op jit(solution)/shard_map/ppermute | solution.py:187
  89.3 8.1 %collective-permute-start.11 = (bf16[32,1024]{1,0:T(8,128)(2,1)S(1)}, bf16[32,1024]{1,0:T(8,128)(2,1)S(1)}, u32[]{:S(2)}, u32[]{:S(2)}) collective-permute-start(bf16[32,1024]{1,0:T(8,128)(2,1)S(1)} %get-tuple-element.30), channel_id=1, source_target_pairs={{0,12},{1,13},{2,14},{3,15},{4,8},{5,9},{6,10},{7,11},{8,4},{9,5},... | collective-permute-start | bytes 196616 | tf_op jit(solution)/shard_map/ppermute | solution.py:187
  92.8 10.4 %collective-permute-start.10 = (bf16[32,1024]{1,0:T(8,128)(2,1)S(1)}, bf16[32,1024]{1,0:T(8,128)(2,1)S(1)}, u32[]{:S(2)}, u32[]{:S(2)}) collective-permute-start(bf16[32,1024]{1,0:T(8,128)(2,1)S(1)} %get-tuple-element.29), channel_id=1, source_target_pairs={{0,8},{1,9},{2,10},{3,11},{4,12},{5,13},{6,14},{7,15},{8,0},{9,1},... | collective-permute-start | bytes 196616 | tf_op jit(solution)/shard_map/ppermute | solution.py:187
  94.1 9.1 %collective-permute-start.7 = (bf16[32,1024]{1,0:T(8,128)(2,1)S(1)}, bf16[32,1024]{1,0:T(8,128)(2,1)S(1)}, u32[]{:S(2)}, u32[]{:S(2)}) collective-permute-start(bf16[32,1024]{1,0:T(8,128)(2,1)S(1)} %fusion.8), channel_id=1, source_target_pairs={{0,4},{1,5},{2,6},{3,7},{4,0},{5,1},{6,2},{7,3},{8,12},{9,13},{10,... | collective-permute-start | bytes 196616 | tf_op jit(solution)/shard_map/ppermute | solution.py:187

commit v2 on v1

v2 whole, which is shorter than its diff:
```python
import functools

import jax
import jax.numpy as jnp
from jax import lax
from jax.experimental import pallas as pl
from jax.experimental.pallas import tpu as pltpu
from jax.sharding import PartitionSpec as P

HEADS = 8
HEAD_SIZE = 128
BLOCK = 128
SCALE = HEAD_SIZE ** (-0.5)
F32 = jnp.float32
BF16 = jnp.bfloat16
VMEM = pl.BlockSpec(memory_space=pltpu.VMEM)
HBM = pl.BlockSpec(memory_space=pltpu.HBM)
SMEM = pl.BlockSpec(memory_space=pltpu.SMEM)
NN = (((1,), (0,)), ((), ()))
NT = (((1,), (1,)), ((), ()))
TN = (((0,), (0,)), ((), ()))


def dot(a, b, dims):
    return lax.dot_general(a, b, dims, preferred_element_type=F32)


def call(body, outs, scratch=(), n_smem=0, n_vmem=0, n_hbm=0, out_specs=None, vmem=16, alias=None, flops=0, name=None):
    many = isinstance(outs, (list, tuple))
    return pl.pallas_call(
        body,
        out_shape=outs,
        in_specs=[SMEM] * n_smem + [VMEM] * n_vmem + [HBM] * n_hbm,
        out_specs=out_specs or ([VMEM] * len(outs) if many else VMEM),
        scratch_shapes=list(scratch),
        input_output_aliases=alias or {},
        compiler_params=pltpu.CompilerParams(vmem_limit_bytes=vmem * 2**20),
        cost_estimate=pl.CostEstimate(flops=flops, bytes_accessed=0, transcendentals=0),
        name=name,
    )


def shape(dims, dtype=BF16):
    return jax.ShapeDtypeStruct(dims, dtype)


def head_lanes(h):
    return slice(h * HEAD_SIZE, (h + 1) * HEAD_SIZE)


def pack_body(q_ref, k_ref, v_ref, send_ref, wide_ref, tall_ref, in_sems, out_sems):
    inward = [
        pltpu.make_async_copy(ref.at[0], wide_ref.at[part], in_sems.at[part])
        for part, ref in enumerate((q_ref, k_ref, v_ref))
    ]
    outward = [
        pltpu.make_async_copy(
            tall_ref.at[part], send_ref.at[:, pl.ds(part * BLOCK, BLOCK), :], out_sems.at[part]
        )
        for part in range(3)
    ]
    for copy in inward:
        copy.start()
    for part in range(3):
        inward[part].wait()
        for h in range(HEADS):
            tall_ref[part, h] = wide_ref[part, :, head_lanes(h)]
        outward[part].start()
    for copy in outward:
        copy.wait()


def pack(*arrays):
    width = arrays[0].shape[-1]
    return pl.pallas_call(
        pack_body,
        out_shape=shape((HEADS, 3 * BLOCK, HEAD_SIZE)),
        in_specs=[HBM] * 3,
        out_specs=HBM,
        scratch_shapes=[
            pltpu.VMEM((3, BLOCK, width), BF16),
            pltpu.VMEM((3, HEADS, BLOCK, HEAD_SIZE), BF16),
            pltpu.SemaphoreType.DMA((3,)),
            pltpu.SemaphoreType.DMA((3,)),
        ],
        compiler_params=pltpu.CompilerParams(vmem_limit_bytes=60 * 2**20),
        cost_estimate=pl.CostEstimate(flops=2**35, bytes_accessed=0, transcendentals=0),
        name="pack",
    )(*arrays)


def unpack_body(recv_ref, q_ref, k_ref, v_ref):
    for part, ref in enumerate((q_ref, k_ref, v_ref)):
        for h in range(HEADS):
            ref[0, :, head_lanes(h)] = recv_ref[h, part * BLOCK : (part + 1) * BLOCK, :]


def weight_rows(ids_ref, refs, place):
    half, quarter = HEADS // 2, HEADS // 4
    i = place % quarter
    near_ref, *far_refs = refs
    if place < half:
        return ids_ref[2] * half + place, near_ref[place * HEAD_SIZE : (place + 1) * HEAD_SIZE, :]
    part = (place - half) // quarter
    h = (ids_ref[2] ^ 1) * half + (part ^ ids_ref[6]) * quarter + i
    return h, far_refs[part][i * HEAD_SIZE : (i + 1) * HEAD_SIZE, :]


def d_out_body(ids_ref, grad_ref, *refs):
    *weight_refs, send_ref, tile_ref, sem = refs
    for place in range(HEADS):
        h, weight = weight_rows(ids_ref, weight_refs, place)
        tile_ref[h] = dot(grad_ref[0], weight, NT).astype(BF16)
    copy = pltpu.make_async_copy(tile_ref, send_ref.at[:, pl.ds(0, BLOCK), :], sem)
    copy.start()
    copy.wait()


def output_body(ids_ref, back_ref, *refs):
    *weight_refs, out_ref = refs
    total = jnp.zeros(out_ref.shape[1:], F32)
    for place in range(HEADS):
        h, weight = weight_rows(ids_ref, weight_refs, place)
        total += dot(back_ref[h, BLOCK:, :], weight, TN)
    out_ref[0] = total.astype(BF16)


def second_block(ids_ref, kb_ref, j, group):
    block = kb_ref[0, ids_ref[0], j * group + ids_ref[1], 1]
    return (block % group) ^ ids_ref[1], block // group


def forward_body(group, ids_ref, kb_ref, cnt_ref, *refs):
    own_ref, *other_refs = refs[:group]
    _, send_ref, probs_ref, kv_ref, s_ref, p_ref, t_ref, sems = refs[group:]
    kv_ref[0] = own_ref[:, BLOCK:, :]
    for r, ref in enumerate(other_refs):
        kv_ref[r + 1] = ref[:, BLOCK:, :]
    picks = [second_block(ids_ref, kb_ref, j, group) for j in range(HEADS)]
    copies = []
    for j in range(HEADS):
        q = own_ref[j, :BLOCK, :]
        both = cnt_ref[0, ids_ref[0], j * group + ids_ref[1]] > 1
        s_ref[j, :, :BLOCK] = dot(q, kv_ref[0, j, :BLOCK, :], NT) * SCALE
        s1 = dot(q, kv_ref[picks[j][0], picks[j][1], :BLOCK, :], NT) * SCALE
        s_ref[j, :, BLOCK:] = jnp.where(both, s1, -jnp.inf)
    for j in range(HEADS):
        s = s_ref[j]
        e = jnp.exp(s - jnp.max(s, axis=-1, keepdims=True))
        p = e * (1.0 / jnp.sum(e, axis=-1, keepdims=True))
        p_ref[j] = p.astype(BF16)
    copies.append(pltpu.make_async_copy(p_ref, probs_ref, sems.at[0]))
    copies[-1].start()
    for j in range(HEADS):
        attn = dot(p_ref[j, :, :BLOCK], kv_ref[0, j, BLOCK:, :], NN) + dot(
            p_ref[j, :, BLOCK:], kv_ref[picks[j][0], picks[j][1], BLOCK:, :], NN
        )
        t_ref[j] = attn.T.astype(BF16)
    copies.append(pltpu.make_async_copy(t_ref, send_ref.at[:, pl.ds(BLOCK, BLOCK), :], sems.at[1]))
    copies[-1].start()
    for copy in copies:
        copy.wait()


def backward_body(group, ids_ref, kb_ref, back_ref, *refs):
    own_ref, *other_refs = refs[:group]
    probs_ref, dq_ref, near_ref, *far_refs = refs[group:-7]
    q_ref, kv_ref, p_ref, dp_ref, ds_ref, acc_ref, sems = refs[-7:]
    loads = [pltpu.make_async_copy(own_ref.at[:, pl.ds(BLOCK, 2 * BLOCK), :], kv_ref.at[0], sems.at[0])]
    for r, ref in enumerate(other_refs):
        loads.append(
            pltpu.make_async_copy(ref.at[:, pl.ds(BLOCK, 2 * BLOCK), :], kv_ref.at[r + 1], sems.at[r + 1])
        )
    loads.append(pltpu.make_async_copy(probs_ref, p_ref, sems.at[group]))
    loads.append(pltpu.make_async_copy(own_ref.at[:, pl.ds(0, BLOCK), :], q_ref, sems.at[group + 1]))
    for copy in loads:
        copy.start()
    picks = [second_block(ids_ref, kb_ref, j, group) for j in range(HEADS)]
    for r in range(1, group):
        acc_ref[r] = jnp.zeros(acc_ref.shape[1:], F32)
    for copy in loads[:group]:
        copy.wait()
    for j in range(HEADS):
        do = back_ref[j, :BLOCK, :]
        dp_ref[j, :, :BLOCK] = dot(do, kv_ref[0, j, BLOCK:, :], NT)
        dp_ref[j, :, BLOCK:] = dot(do, kv_ref[picks[j][0], picks[j][1], BLOCK:, :], NT)
    for copy in loads[group:]:
        copy.wait()
    for j in range(HEADS):
        p = p_ref[j].astype(F32)
        dp = dp_ref[j]
        delta = jnp.sum(p * dp, axis=-1, keepdims=True)
        ds_ref[j] = (p * (dp - delta)).astype(BF16)
    second = []
    for j in range(HEADS):
        dk = dot(ds_ref[j], q_ref[j], TN)
        dv = dot(p_ref[j], back_ref[j, :BLOCK, :], TN)
        acc_ref[0, j, :BLOCK, :] = dk[:BLOCK]
        acc_ref[0, j, BLOCK:, :] = dv[:BLOCK]
        dp_ref[j, :, :BLOCK] = dk[BLOCK:]
        dp_ref[j, :, BLOCK:] = dv[BLOCK:]
    for j in range(HEADS):
        r, jb = picks[j]
        acc_ref[r, jb, :BLOCK, :] += dp_ref[j, :, :BLOCK]
        acc_ref[r, jb, BLOCK:, :] += dp_ref[j, :, BLOCK:]
    for j in range(HEADS):
        dq_ref[j] = (
            (
                dot(ds_ref[j, :, :BLOCK], kv_ref[0, j, :BLOCK, :], NN)
                + dot(ds_ref[j, :, BLOCK:], kv_ref[picks[j][0], picks[j][1], :BLOCK, :], NN)
            )
            * SCALE
        ).astype(BF16)
    for r, ref in enumerate((near_ref, *far_refs)):
        ref[:, :BLOCK, :] = (acc_ref[r, :, :BLOCK, :] * SCALE).astype(BF16)
        ref[:, BLOCK:, :] = acc_ref[r, :, BLOCK:, :].astype(BF16)


def combine_body(dq_ref, near_ref, *refs):
    *arrived_refs, send_ref = refs
    send_ref[:, :BLOCK, :] = dq_ref[...]
    total = near_ref[...].astype(F32)
    for ref in arrived_refs:
        total += ref[...].astype(F32)
    send_ref[:, BLOCK:, :] = total.astype(BF16)


def feature_body(ids_ref, mine_ref, pair_ref, *out_refs):
    d, z, y, c = ids_ref[2], ids_ref[3], ids_ref[4], ids_ref[5]
    for yr, ref in enumerate(out_refs):
        first = pl.multiple_of(BLOCK + (yr ^ y) * 64 + c * 32, 32)
        for place in range(HEADS):
            h = ((place >> 2) ^ d) * 4 + ((place & 3) ^ z)
            rows = slice(place * 32, (place + 1) * 32)
            ref[rows, :BLOCK] = mine_ref[h, pl.ds(first, 32), :]
            ref[rows, BLOCK:] = pair_ref[h, pl.ds(first, 32), :]


def grad_weight_body(*refs):
    attn_refs, grad_refs = refs[:2], refs[2:6]
    keep_ref, send_ref, rows_ref, sems = refs[6:]
    loads = [
        pltpu.make_async_copy(ref.at[0], rows_ref.at[i], sems.at[i]) for i, ref in enumerate(grad_refs)
    ]
    for copy in loads:
        copy.start()
    for copy in loads:
        copy.wait()
    half = keep_ref.shape[0]
    for place, ref in ((1, send_ref), (0, keep_ref)):
        rows = slice(place * half, (place + 1) * half)
        total = jnp.zeros(ref.shape, F32)
        for i, attn_ref in enumerate(attn_refs):
            total += dot(attn_ref[rows, :BLOCK], rows_ref[i], NN)
            total += dot(attn_ref[rows, BLOCK:], rows_ref[i + 2], NN)
        ref[...] = total.astype(ref.dtype)


def ctx_swap(x, mask):
    n = lax.axis_size("ctx")
    return lax.ppermute(x, "ctx", [(i, i ^ mask) for i in range(n)])


def dp_swap(x):
    return lax.ppermute(x, "dp", [(0, 1), (1, 0)])


def together(*values):
    return lax.optimization_barrier(values)


def own_features(ids, back):
    return call(
        feature_body, [shape((HEADS * 32, 2 * BLOCK))] * 2, n_smem=1, n_vmem=2, name="features"
    )(ids, back, ctx_swap(back, 1))


def reduce_weight(features, rows):
    columns = rows[0].shape[-1]
    keep, send = call(
        grad_weight_body,
        [shape((4 * 32, columns), F32), shape((4 * 32, columns))],
        [pltpu.VMEM((4, BLOCK, columns), BF16), pltpu.SemaphoreType.DMA((4,))],
        n_vmem=2, n_hbm=4, vmem=16, flops=2**35, name="grad_weight",
    )(features[0], ctx_swap(features[1], 2), *rows)
    total = (keep + dp_swap(send).astype(F32)).reshape(4, 32, columns)
    parts = [ctx_swap(total[zr].astype(BF16), 4 * zr) for zr in range(1, 4)]
    return total[0] + sum(part.astype(F32) for part in parts)


def local(queries, keys, values, out_weight, out_grad, key_blocks, block_counts):
    ctx_count = lax.axis_size("ctx")
    dp_count = lax.axis_size("dp")
    group = ctx_count // HEADS
    position = lax.axis_index("ctx")
    small = dp_count == 2 and ctx_count == 16
    rank = lax.axis_index("dp") if dp_count == 2 else 0
    ids = jnp.stack(
        [position // group, position % group, rank, position >> 2, position >> 1 & 1, position & 1,
         position & 1 if dp_count == 2 else 0]
    ).astype(jnp.int32)
    columns = out_grad.shape[-1]
    peers = [[j * group + m for j in range(HEADS)] for m in range(group)]

    def exchange(x):
        return lax.all_to_all(x, "ctx", 0, 0, tiled=True, axis_index_groups=peers)

    if dp_count == 2:
        near, rows = out_weight, out_weight.shape[0] // 2
        half = dp_swap(lax.dynamic_slice_in_dim(near, (position & 1) * rows, rows, 0))
    if small:
        same, cross = [out_grad, ctx_swap(out_grad, 2)], [ctx_swap(out_grad, 1)]
        cross.append(ctx_swap(same[1], 1))
    if dp_count == 2:
        far = [half, ctx_swap(half, 1)]
    else:
        near, *far = jnp.split(
            lax.all_gather(out_weight, "dp", axis=0, tiled=True), (HEADS * 64, HEADS * 96)
        )

    own = exchange(pack(queries, keys, values))
    pair = shape((HEADS, 2 * BLOCK, HEAD_SIZE))
    tile = shape((HEADS, BLOCK, HEAD_SIZE))
    tile_scratch = pltpu.VMEM(tile.shape, BF16)
    score = (HEADS, BLOCK, 2 * BLOCK)
    if small:
        own, same[1], *rest = together(own, same[1], *cross, *far)
        cross, far = rest[:2], rest[2:]
    send = call(
        d_out_body, pair, [tile_scratch, pltpu.SemaphoreType.DMA],
        n_smem=1, n_vmem=4, out_specs=HBM, vmem=60, flops=2**33, name="d_out",
    )(ids, out_grad, near, *far)
    others = [ctx_swap(own, r) for r in range(1, group)]
    vmem = 16 if group == 2 else 40
    kv_scratch = pltpu.VMEM((group, HEADS, 2 * BLOCK, HEAD_SIZE), BF16)
    send, probs = call(
        functools.partial(forward_body, group),
        [pair, shape(score)],
        [kv_scratch, pltpu.VMEM(score, F32), pltpu.VMEM(score, BF16), tile_scratch, pltpu.SemaphoreType.DMA((2,))],
        n_smem=3, n_vmem=group, n_hbm=1, out_specs=[HBM] * 2, vmem=60, alias={3 + group: 0}, name="forward",
    )(ids, key_blocks, block_counts, own, *others, send)
    back = exchange(send)
    dq, near_kv, *far_kv = call(
        functools.partial(backward_body, group),
        [tile, pair] + [pair] * (group - 1),
        [
            tile_scratch, kv_scratch, pltpu.VMEM(score, BF16), pltpu.VMEM(score, F32), pltpu.VMEM(score, BF16),
            pltpu.VMEM((group, HEADS, 2 * BLOCK, HEAD_SIZE), F32), pltpu.SemaphoreType.DMA((group + 2,)),
        ],
        n_smem=2, n_vmem=1, n_hbm=group + 1, vmem=vmem, name="backward",
    )(ids, key_blocks, back, own, *others, probs)
    arrived = [ctx_swap(part, r + 1) for r, part in enumerate(far_kv)]
    if small:
        dq, *features = together(dq, *own_features(ids, back))
    grads = exchange(
        call(
            combine_body, shape((HEADS, 3 * BLOCK, HEAD_SIZE)), n_vmem=group + 1,
            vmem=vmem, flops=2**33, name="combine",
        )(dq, near_kv, *arrived)
    )
    tokens = shape((1, BLOCK, HEADS * HEAD_SIZE))
    grad_queries, grad_keys, grad_values = call(unpack_body, [tokens] * 3, n_vmem=1, name="unpack")(grads)
    if small:
        grad_weight = reduce_weight(features, same + cross)
    else:
        grad_weight = lax.psum_scatter(
            dot(back[:, BLOCK:, :].reshape(HEADS * HEAD_SIZE, BLOCK), out_grad[0], NN),
            ("dp", "ctx"), scatter_dimension=0, tiled=True,
        )
    output = call(
        output_body, shape((1, BLOCK, columns)), n_smem=1, n_vmem=4, vmem=60, name="output",
    )(ids, back, near, *far)
    return (output, grad_queries, grad_keys, grad_values, grad_weight)


def solution(mesh):
    tokens = P("dp", "ctx", None)
    return jax.shard_map(
        local,
        mesh=mesh,
        in_specs=(
            tokens, tokens, tokens, P("dp", None), tokens,
            P("dp", None, None, None), P("dp", None, None),
        ),
        out_specs=(tokens, tokens, tokens, tokens, P(("dp", "ctx"), None)),
        check_vma=False,
    )
```

time: 106 us -> 98.7 us (0.931)
  local copies, waits for them, and re-layouts: 9.61 us -> 5.87 us
  waiting for transfers between devices: 33.6 us -> 30.3 us
  Pallas kernels: 16.1 us -> 18.7 us
  starting transfers between devices: 24.5 us -> 22.7 us
    all_to_all x2, waiting for transfers between devices: 18.6 us -> 2.17 us  [exchange(): return lax.all_to_all(x, 'ctx', 0, 0, tiled=True, axis_index_groups=peers)]
    ppermute x3 -> x2, waiting for transfers between devices: 7.4 us -> 16.9 us  [dp_swap(): return lax.ppermute(x, 'dp', [(0, 1), (1, 0)])]
    ppermute x9 -> x11, waiting for transfers between devices: 7.55 us -> 11.2 us  [ctx_swap(): return lax.ppermute(x, 'ctx', [(i, i ^ mask) for i in range(n)])]
    pallas_call x8 -> x9, Pallas kernels: 16.1 us -> 18.7 us  [the longest x1 3.52 us: local(): call(functools.partial(forward_body, group), [pair, shape(score)], [kv_sc...]
    unnamed x33 -> x29, local copies, waits for them, and re-layouts: 7.63 us -> 5.18 us
    ppermute x3 -> x2, starting transfers between devices: 4.66 us -> 2.99 us  [dp_swap(): return lax.ppermute(x, 'dp', [(0, 1), (1, 0)])]
    add x4 -> x1, other arithmetic: 1.78 us -> 0.69 us  [reduce_weight(): return total[0] + sum((part.astype(F32) for part in parts))]
    ppermute x9 -> x11, starting transfers between devices: 8.89 us -> 8.59 us  [ctx_swap(): return lax.ppermute(x, 'ctx', [(i, i ^ mask) for i in range(n)])]
  transfers between devices with their start and end apart: 14 -> 15, of which waited for: 6 -> 6; matrix products, arithmetic and copies ran while one was open for 4% -> 2% of each run, Pallas kernels for 9% -> 12%
where the time goes in v2:
time: 98.7 us; the launch traced here: 98.1 us
  waiting for transfers between devices  30.3 us (31%)
  starting transfers between devices  22.7 us (23%)
  blocking collectives  18.8 us (19%)
  Pallas kernels  18.7 us (19%)
  local copies, waits for them, and re-layouts  5.87 us (6%)
    all_to_all x1, blocking collectives, exchange(): return lax.all_to_all(x, 'ctx', 0, 0, tiled=True, axis_index_groups=peers)  18.8 us
    ppermute x2, waiting for transfers between devices, dp_swap(): return lax.ppermute(x, 'dp', [(0, 1), (1, 0)])  16.9 us
    ppermute x11, waiting for transfers between devices, ctx_swap(): return lax.ppermute(x, 'ctx', [(i, i ^ mask) for i in range(n)])  11.2 us
    all_to_all x2, starting transfers between devices, exchange(): return lax.all_to_all(x, 'ctx', 0, 0, tiled=True, axis_index_groups=peers)  11.1 us
    ppermute x11, starting transfers between devices, ctx_swap(): return lax.ppermute(x, 'ctx', [(i, i ^ mask) for i in range(n)])  8.59 us
    unnamed x29, local copies, waits for them, and re-layouts  5.18 us
    pallas_call x1, Pallas kernels, local(): call(functools.partial(forward_body, group), [pair, shape(score)], [kv_sc...  3.52 us
    pallas_call x1, Pallas kernels, local(): call(functools.partial(backward_body, group), [tile, pair] + [pair] * (gr...  3.34 us
  transfers between devices with their start and end apart: 15, of which 6 were waited for; matrix products, arithmetic and copies ran while one was open for 2% of the time, Pallas kernels for 12%

profile of v2, /device:TPU:0, one launch (start us, length us, event | category | flops | bytes accessed | tf_op | source)
XLA Modules:
  0.0 98.1 jit_solution(1881390131148787542)
XLA Ops:
  0.6 1.9 %pack.1 = bf16[8,384,128]{2,1,0:T(8,128)(2,1)} custom-call(bf16[1,128,1024]{2,1,0:T(8,128)(2,1)} %q_ref.1, bf16[1,128,1024]{2,1,0:T(8,128)(2,1)} %k_ref.1, bf16[1,128,1024]{2,1,0:T(8,128)(2,1)} %v_ref.1), custom_call_target="tpu_custom_call" | custom-call | flops 34359738368 | tf_op jit(solution)/shard_map/pack/pallas_call | solution.py:75
  2.6 0.0 copy-start.10
  2.6 7.4 %all-to-all-start = ((bf16[8,384,128]{2,1,0:T(8,128)(2,1)}), bf16[8,384,128]{2,1,0:T(8,128)(2,1)S(1)}, u32[]{:S(2)}, u32[]{:S(2)}) async-start(bf16[8,384,128]{2,1,0:T(8,128)(2,1)} %pack.1), calls=%async_computation | async-start | bytes 1572864 | tf_op jit(solution)/shard_map/all_to_all | solution.py:306
  10.0 0.0 copy-done.10
  10.0 0.0 copy-start.8
  10.1 1.6 %collective-permute-start.3 = (bf16[256,1024]{1,0:T(8,128)(2,1)S(1)}, bf16[256,1024]{1,0:T(8,128)(2,1)S(1)}, u32[]{:S(2)}, u32[]{:S(2)}) collective-permute-start(bf16[256,1024]{1,0:T(8,128)(2,1)S(1)} %constant_dynamic-slice_fusion), channel_id=1, source_target_pairs={{0,16},{16,0},{1,17},{17,1},{2,18},{18,2},{3,19},{19,3},{4,20},{20... | collective-permute-start | bytes 1572872 | tf_op jit(solution)/shard_map/ppermute | solution.py:265
  11.6 0.0 copy-done.8
  11.6 2.0 %collective-permute-start = (bf16[1,128,1024]{2,1,0:T(8,128)(2,1)S(1)}, bf16[1,128,1024]{2,1,0:T(8,128)(2,1)S(1)}, u32[]{:S(2)}, u32[]{:S(2)}) collective-permute-start(bf16[1,128,1024]{2,1,0:T(8,128)(2,1)S(1)} %copy-done.8), channel_id=1, source_target_pairs={{0,2},{1,3},{2,0},{3,1},{4,6},{5,7},{6,4},{7,5},{8,10},{9,11},{10,... | collective-permute-start | bytes 786440 | tf_op jit(solution)/shard_map/ppermute | solution.py:261
  13.6 9.9 %collective-permute-done.3.refs_1_ = bf16[256,1024]{1,0:T(8,128)(2,1)S(1)} collective-permute-done((bf16[256,1024]{1,0:T(8,128)(2,1)S(1)}, bf16[256,1024]{1,0:T(8,128)(2,1)S(1)}, u32[]{:S(2)}, u32[]{:S(2)}) %collective-permute-start.3) | collective-permute-done | bytes 524320 | tf_op jit(solution)/shard_map/ppermute | solution.py:265
  23.5 0.0 collective-permute-start.4
  23.5 0.5 collective-permute-start.1
  24.0 1.9 %collective-permute-done.refs_3_ = bf16[1,128,1024]{2,1,0:T(8,128)(2,1)S(1)} collective-permute-done((bf16[1,128,1024]{2,1,0:T(8,128)(2,1)S(1)}, bf16[1,128,1024]{2,1,0:T(8,128)(2,1)S(1)}, u32[]{:S(2)}, u32[]{:S(2)}) %collective-permute-start) | collective-permute-done | bytes 262176 | tf_op jit(solution)/shard_map/ppermute | solution.py:261
  25.9 0.0 collective-permute-start.2
  25.9 0.7 copy-done.13
  26.6 0.8 copy.13.kb_ref
  27.4 0.6 stack.28.ids_ref
  28.0 0.0 collective-permute-done.1.refs_4_
  28.0 0.0 collective-permute-done.2.refs_5_
  28.0 0.0 collective-permute-done.4.refs_2_
  28.0 0.0 copy-start.12
  28.0 2.2 %all-to-all-done.refs_0_ = bf16[8,384,128]{2,1,0:T(8,128)(2,1)S(1)} async-done(((bf16[8,384,128]{2,1,0:T(8,128)(2,1)}), bf16[8,384,128]{2,1,0:T(8,128)(2,1)S(1)}, u32[]{:S(2)}, u32[]{:S(2)}) %all-to-all-start) | async-done | bytes 786464 | tf_op jit(solution)/shard_map/all_to_all | solution.py:306
  30.2 0.0 collective-permute-start.5
  30.2 0.0 copy-done.11
  30.2 0.0 copy-done.12
  30.2 3.3 %d_out.1.refs_2_ = bf16[8,256,128]{2,1,0:T(8,128)(2,1)} custom-call(s32[7]{0:T(128)} %stack.28.ids_ref, bf16[1,128,1024]{2,1,0:T(8,128)(2,1)} %refs_2_.1, bf16[512,1024]{1,0:T(8,128)(2,1)} %refs_0_.3, bf16[256,1024]{1,0:T(8,128)(2,1)} %copy-done.11, bf16[256,1024]{1,0:T(8,128)(2,1)} %copy-done.12), custom_call_target="tpu_custom_call" | custom-call | flops 8589934592 | tf_op jit(solution)/shard_map/d_out/pallas_call | solution.py:329
  33.5 0.0 copy-done.1
  33.6 0.0 collective-permute-done.5.refs_1_
  33.6 0.0 copy-start.3
  33.6 0.9 copy-done.3
  34.5 3.5 %forward.1 = (bf16[8,256,128]{2,1,0:T(8,128)(2,1)}, bf16[8,128,256]{2,1,0:T(8,128)(2,1)}) custom-call(s32[7]{0:T(128)} %stack.28.ids_ref, s32[1,8,16,2]{3,2,1,0:T(8,128)} %copy.13.kb_ref, s32[1,8,16]{2,1,0:T(8,128)} %cnt_ref.1, bf16[8,384,128]{2,1,0:T(8,128)(2,1)} %copy-done.1, bf16[8,384,128]{2,1,0:T(8,128)(2,1)} %copy-done.3, ...), custom_call_target="tpu_custom_call", output_to_operand_aliasing={{0}: (5, {})} | custom-call | tf_op jit(solution)/shard_map/forward/pallas_call | solution.py:336
  38.0 0.0 copy-start.2
  38.0 0.0 copy-start.5
  38.0 18.8 %all_to_all.15.back_ref.mine_ref = bf16[8,256,128]{2,1,0:T(8,128)(2,1)S(1)} all-to-all(bf16[8,256,128]{2,1,0:T(8,128)(2,1)} %get-tuple-element.29), channel_id=1, replica_groups={{0,2,4,6,8,10,12,14},{1,3,5,7,9,11,13,15},{16,18,20,22,24,26,28,30},{17..., dimensions={0} | all-to-all | bytes 1048576 | tf_op jit(solution)/shard_map/all_to_all | solution.py:306
  56.8 0.0 collective-permute-start.6
  56.8 0.0 copy-done.2
  56.8 0.0 copy-done.5
  56.8 0.6 copy-done.7
  57.5 1.1 %copy-done.4 = bf16[8,384,128]{2,1,0:T(8,128)(2,1)S(1)} copy-done((bf16[8,384,128]{2,1,0:T(8,128)(2,1)S(1)}, bf16[8,384,128]{2,1,0:T(8,128)(2,1)}, u32[]{:S(2)}) %copy-start.4) | copy-done | bytes 786456
  58.6 1.0 %copy-done.6 = bf16[8,128,256]{2,1,0:T(8,128)(2,1)S(1)} copy-done((bf16[8,128,256]{2,1,0:T(8,128)(2,1)S(1)}, bf16[8,128,256]{2,1,0:T(8,128)(2,1)}, u32[]{:S(2)}) %copy-start.6) | copy-done | bytes 524312
  59.6 3.3 %backward.1 = (bf16[8,128,128]{2,1,0:T(8,128)(2,1)S(1)}, bf16[8,256,128]{2,1,0:T(8,128)(2,1)S(1)}, bf16[8,256,128]{2,1,0:T(8,128)(2,1)S(1)}) custom-call(s32[7]{0:T(128)S(1)} %copy-done.7, s32[1,8,16,2]{3,2,1,0:T(8,128)S(1)} %copy-done.5, bf16[8,256,128]{2,1,0:T(8,128)(2,1)S(1)} %all_to_all.15.back_ref.mine_ref, bf16[8,384,128]{2,1,0:T(8,128)(2,1)S(1)} %copy-done.2, ...), custom_call_target="tpu_custom_call" | custom-call | tf_op jit(solution)/shard_map/backward/pallas_call | solution.py:343
  63.0 0.1 collective-permute-start.7
  63.1 0.0 collective-permute-done.6.pair_ref
  63.1 0.0 copy-done
  63.1 0.6 features.1
  63.7 1.5 %collective-permute-start.8 = (bf16[256,256]{1,0:T(8,128)(2,1)S(1)}, bf16[256,256]{1,0:T(8,128)(2,1)S(1)}, u32[]{:S(2)}, u32[]{:S(2)}) collective-permute-start(bf16[256,256]{1,0:T(8,128)(2,1)S(1)} %get-tuple-element.41), channel_id=1, source_target_pairs={{0,2},{1,3},{2,0},{3,1},{4,6},{5,7},{6,4},{7,5},{8,10},{9,11},{10,... | collective-permute-start | bytes 393224 | tf_op jit(solution)/shard_map/ppermute | solution.py:261
  65.2 0.0 collective-permute-done.7.refs_0_
  65.2 1.0 %combine.1 = bf16[8,384,128]{2,1,0:T(8,128)(2,1)} custom-call(bf16[8,128,128]{2,1,0:T(8,128)(2,1)S(1)} %get-tuple-element.34.dq_ref, bf16[8,256,128]{2,1,0:T(8,128)(2,1)S(1)} %get-tuple-element.35.near_ref, bf16[8,256,128]{2,1,0:T(8,128)(2,1)S(1)} %collective-permute-done.7.refs_0_), custom_call_target="tpu_custom_call" | custom-call | flops 8589934592 | tf_op jit(solution)/shard_map/combine/pallas_call | solution.py:356
  66.3 3.7 %all-to-all-start.2 = ((bf16[8,384,128]{2,1,0:T(8,128)(2,1)}), bf16[8,384,128]{2,1,0:T(8,128)(2,1)S(1)}, u32[]{:S(2)}, u32[]{:S(2)}) async-start(bf16[8,384,128]{2,1,0:T(8,128)(2,1)} %combine.1), calls=%async_computation.2 | async-start | bytes 1572864 | tf_op jit(solution)/shard_map/all_to_all | solution.py:306
  70.0 0.0 collective-permute-done.8.refs_1_
  70.0 0.0 copy-done.9
  70.0 0.8 grad_weight.1
  70.8 1.4 %collective-permute-start.9 = (bf16[128,1024]{1,0:T(8,128)(2,1)S(1)}, bf16[128,1024]{1,0:T(8,128)(2,1)S(1)}, u32[]{:S(2)}, u32[]{:S(2)}) collective-permute-start(bf16[128,1024]{1,0:T(8,128)(2,1)S(1)} %get-tuple-element.46), channel_id=1, source_target_pairs={{0,16},{16,0},{1,17},{17,1},{2,18},{18,2},{3,19},{19,3},{4,20},{20... | collective-permute-start | bytes 786440 | tf_op jit(solution)/shard_map/ppermute | solution.py:265
  72.2 7.1 %collective-permute-done.9 = bf16[128,1024]{1,0:T(8,128)(2,1)S(1)} collective-permute-done((bf16[128,1024]{1,0:T(8,128)(2,1)S(1)}, bf16[128,1024]{1,0:T(8,128)(2,1)S(1)}, u32[]{:S(2)}, u32[]{:S(2)}) %collective-permute-start.9) | collective-permute-done | bytes 262176 | tf_op jit(solution)/shard_map/ppermute | solution.py:265
  79.3 0.1 fusion
  79.4 3.5 %collective-permute-start.12 = (bf16[32,1024]{1,0:T(8,128)(2,1)S(1)}, bf16[32,1024]{1,0:T(8,128)(2,1)S(1)}, u32[]{:S(2)}, u32[]{:S(2)}) collective-permute-start(bf16[32,1024]{1,0:T(8,128)(2,1)S(1)} %get-tuple-element.50), channel_id=1, source_target_pairs={{0,12},{1,13},{2,14},{3,15},{4,8},{5,9},{6,10},{7,11},{8,4},{9,5},... | collective-permute-start | bytes 196616 | tf_op jit(solution)/shard_map/ppermute | solution.py:261
  82.9 0.0 collective-permute-start.11
  82.9 0.9 collective-permute-start.10
  83.8 3.1 %output.1 = bf16[1,128,1024]{2,1,0:T(8,128)(2,1)} custom-call(s32[7]{0:T(128)} %stack.28.ids_ref, bf16[8,256,128]{2,1,0:T(8,128)(2,1)} %copy-done, bf16[512,1024]{1,0:T(8,128)(2,1)} %refs_0_.3, bf16[256,1024]{1,0:T(8,128)(2,1)} %copy-done.11, bf16[256,1024]{1,0:T(8,128)(2,1)} %copy-done.12), custom_call_target="tpu_custom_call" | custom-call | tf_op jit(solution)/shard_map/output/pallas_call | solution.py:370
  87.0 2.6 %collective-permute-done.12 = bf16[32,1024]{1,0:T(8,128)(2,1)S(1)} collective-permute-done((bf16[32,1024]{1,0:T(8,128)(2,1)S(1)}, bf16[32,1024]{1,0:T(8,128)(2,1)S(1)}, u32[]{:S(2)}, u32[]{:S(2)}) %collective-permute-start.12) | collective-permute-done | bytes 65568 | tf_op jit(solution)/shard_map/ppermute | solution.py:261
  89.6 6.7 %collective-permute-done.11 = bf16[32,1024]{1,0:T(8,128)(2,1)S(1)} collective-permute-done((bf16[32,1024]{1,0:T(8,128)(2,1)S(1)}, bf16[32,1024]{1,0:T(8,128)(2,1)S(1)}, u32[]{:S(2)}, u32[]{:S(2)}) %collective-permute-start.11) | collective-permute-done | bytes 65568 | tf_op jit(solution)/shard_map/ppermute | solution.py:261
  96.3 0.0 collective-permute-done.10
  96.3 0.7 slice_add_fusion
  97.0 0.0 all-to-all-done.2.recv_ref
  97.0 1.1 %unpack.1 = (bf16[1,128,1024]{2,1,0:T(8,128)(2,1)}, bf16[1,128,1024]{2,1,0:T(8,128)(2,1)}, bf16[1,128,1024]{2,1,0:T(8,128)(2,1)}) custom-call(bf16[8,384,128]{2,1,0:T(8,128)(2,1)S(1)} %all-to-all-done.2.recv_ref), custom_call_target="tpu_custom_call" | custom-call | tf_op jit(solution)/shard_map/unpack/pallas_call | solution.py:362
  (10 shorter events, 0.1 us)
Async XLA Ops:
  2.6 7.4 %copy-start.10 = (bf16[512,1024]{1,0:T(8,128)(2,1)S(1)}, bf16[512,1024]{1,0:T(8,128)(2,1)}, u32[]{:S(2)}) copy-start(bf16[512,1024]{1,0:T(8,128)(2,1)} %refs_0_.3) | copy-start | bytes 3145732
  2.6 27.6 %all-to-all-start = ((bf16[8,384,128]{2,1,0:T(8,128)(2,1)}), bf16[8,384,128]{2,1,0:T(8,128)(2,1)S(1)}, u32[]{:S(2)}, u32[]{:S(2)}) async-start(bf16[8,384,128]{2,1,0:T(8,128)(2,1)} %pack.1), calls=%async_computation | async-start | bytes 1572864 | tf_op jit(solution)/shard_map/all_to_all | solution.py:306
  10.0 1.6 %copy-start.8 = (bf16[1,128,1024]{2,1,0:T(8,128)(2,1)S(1)}, bf16[1,128,1024]{2,1,0:T(8,128)(2,1)}, u32[]{:S(2)}) copy-start(bf16[1,128,1024]{2,1,0:T(8,128)(2,1)} %refs_2_.1) | copy-start | bytes 786436
  10.1 13.4 %collective-permute-start.3 = (bf16[256,1024]{1,0:T(8,128)(2,1)S(1)}, bf16[256,1024]{1,0:T(8,128)(2,1)S(1)}, u32[]{:S(2)}, u32[]{:S(2)}) collective-permute-start(bf16[256,1024]{1,0:T(8,128)(2,1)S(1)} %constant_dynamic-slice_fusion), channel_id=1, source_target_pairs={{0,16},{16,0},{1,17},{17,1},{2,18},{18,2},{3,19},{19,3},{4,20},{20... | collective-permute-start | bytes 1572872 | tf_op jit(solution)/shard_map/ppermute | solution.py:265
  11.6 14.3 %collective-permute-start = (bf16[1,128,1024]{2,1,0:T(8,128)(2,1)S(1)}, bf16[1,128,1024]{2,1,0:T(8,128)(2,1)S(1)}, u32[]{:S(2)}, u32[]{:S(2)}) collective-permute-start(bf16[1,128,1024]{2,1,0:T(8,128)(2,1)S(1)} %copy-done.8), channel_id=1, source_target_pairs={{0,2},{1,3},{2,0},{3,1},{4,6},{5,7},{6,4},{7,5},{8,10},{9,11},{10,... | collective-permute-start | bytes 786440 | tf_op jit(solution)/shard_map/ppermute | solution.py:261
  23.5 6.7 %copy-start.11 = (bf16[256,1024]{1,0:T(8,128)(2,1)}, bf16[256,1024]{1,0:T(8,128)(2,1)S(1)}, u32[]{:S(2)}) copy-start(bf16[256,1024]{1,0:T(8,128)(2,1)S(1)} %collective-permute-done.3.refs_1_) | copy-start | bytes 1572868
  23.5 4.5 %collective-permute-start.4 = (bf16[256,1024]{1,0:T(8,128)(2,1)S(1)}, bf16[256,1024]{1,0:T(8,128)(2,1)S(1)}, u32[]{:S(2)}, u32[]{:S(2)}) collective-permute-start(bf16[256,1024]{1,0:T(8,128)(2,1)S(1)} %collective-permute-done.3.refs_1_), channel_id=1, source_target_pairs={{0,1},{1,0},{2,3},{3,2},{4,5},{5,4},{6,7},{7,6},{8,9},{9,8},{10,11... | collective-permute-start | bytes 1572872 | tf_op jit(solution)/shard_map/ppermute | solution.py:261
  23.5 4.5 %collective-permute-start.1 = (bf16[1,128,1024]{2,1,0:T(8,128)(2,1)S(1)}, bf16[1,128,1024]{2,1,0:T(8,128)(2,1)S(1)}, u32[]{:S(2)}, u32[]{:S(2)}) collective-permute-start(bf16[1,128,1024]{2,1,0:T(8,128)(2,1)S(1)} %copy-done.8), channel_id=1, source_target_pairs={{0,1},{1,0},{2,3},{3,2},{4,5},{5,4},{6,7},{7,6},{8,9},{9,8},{10,11... | collective-permute-start | bytes 786440 | tf_op jit(solution)/shard_map/ppermute | solution.py:261
  25.9 2.1 %collective-permute-start.2 = (bf16[1,128,1024]{2,1,0:T(8,128)(2,1)S(1)}, bf16[1,128,1024]{2,1,0:T(8,128)(2,1)S(1)}, u32[]{:S(2)}, u32[]{:S(2)}) collective-permute-start(bf16[1,128,1024]{2,1,0:T(8,128)(2,1)S(1)} %collective-permute-done.refs_3_), channel_id=1, source_target_pairs={{0,1},{1,0},{2,3},{3,2},{4,5},{5,4},{6,7},{7,6},{8,9},{9,8},{10,11... | collective-permute-start | bytes 786440 | tf_op jit(solution)/shard_map/ppermute | solution.py:261
  25.9 0.7 copy-start.13
  28.0 2.2 %copy-start.12 = (bf16[256,1024]{1,0:T(8,128)(2,1)}, bf16[256,1024]{1,0:T(8,128)(2,1)S(1)}, u32[]{:S(2)}) copy-start(bf16[256,1024]{1,0:T(8,128)(2,1)S(1)} %collective-permute-done.4.refs_2_) | copy-start | bytes 1572868
  30.2 3.4 %copy-start.1 = (bf16[8,384,128]{2,1,0:T(8,128)(2,1)}, bf16[8,384,128]{2,1,0:T(8,128)(2,1)S(1)}, u32[]{:S(2)}) copy-start(bf16[8,384,128]{2,1,0:T(8,128)(2,1)S(1)} %all-to-all-done.refs_0_) | copy-start | bytes 2359300
  30.2 3.4 %collective-permute-start.5 = (bf16[8,384,128]{2,1,0:T(8,128)(2,1)S(1)}, bf16[8,384,128]{2,1,0:T(8,128)(2,1)S(1)}, u32[]{:S(2)}, u32[]{:S(2)}) collective-permute-start(bf16[8,384,128]{2,1,0:T(8,128)(2,1)S(1)} %all-to-all-done.refs_0_), channel_id=1, source_target_pairs={{0,1},{1,0},{2,3},{3,2},{4,5},{5,4},{6,7},{7,6},{8,9},{9,8},{10,11... | collective-permute-start | bytes 2359304 | tf_op jit(solution)/shard_map/ppermute | solution.py:261
  33.6 0.9 copy-start.3
  38.0 18.8 %copy-start.2 = (bf16[8,384,128]{2,1,0:T(8,128)(2,1)S(1)}, bf16[8,384,128]{2,1,0:T(8,128)(2,1)}, u32[]{:S(2)}) copy-start(bf16[8,384,128]{2,1,0:T(8,128)(2,1)} %copy-done.1) | copy-start | bytes 2359300
  38.0 18.8 %copy-start.5 = (s32[1,8,16,2]{3,2,1,0:T(8,128)S(1)}, s32[1,8,16,2]{3,2,1,0:T(8,128)}, u32[]{:S(2)}) copy-start(s32[1,8,16,2]{3,2,1,0:T(8,128)} %copy.13.kb_ref) | copy-start | bytes 3076
  56.8 6.3 %copy-start = (bf16[8,256,128]{2,1,0:T(8,128)(2,1)}, bf16[8,256,128]{2,1,0:T(8,128)(2,1)S(1)}, u32[]{:S(2)}) copy-start(bf16[8,256,128]{2,1,0:T(8,128)(2,1)S(1)} %all_to_all.15.back_ref.mine_ref) | copy-start | bytes 1572868
  56.8 0.6 copy-start.7
  56.8 6.2 %collective-permute-start.6 = (bf16[8,256,128]{2,1,0:T(8,128)(2,1)S(1)}, bf16[8,256,128]{2,1,0:T(8,128)(2,1)S(1)}, u32[]{:S(2)}, u32[]{:S(2)}) collective-permute-start(bf16[8,256,128]{2,1,0:T(8,128)(2,1)S(1)} %all_to_all.15.back_ref.mine_ref), channel_id=1, source_target_pairs={{0,1},{1,0},{2,3},{3,2},{4,5},{5,4},{6,7},{7,6},{8,9},{9,8},{10,11... | collective-permute-start | bytes 1572872 | tf_op jit(solution)/shard_map/ppermute | solution.py:261
  57.5 1.1 %copy-start.4 = (bf16[8,384,128]{2,1,0:T(8,128)(2,1)S(1)}, bf16[8,384,128]{2,1,0:T(8,128)(2,1)}, u32[]{:S(2)}) copy-start(bf16[8,384,128]{2,1,0:T(8,128)(2,1)} %copy-done.3) | copy-start | bytes 2359300
  58.6 1.0 %copy-start.6 = (bf16[8,128,256]{2,1,0:T(8,128)(2,1)S(1)}, bf16[8,128,256]{2,1,0:T(8,128)(2,1)}, u32[]{:S(2)}) copy-start(bf16[8,128,256]{2,1,0:T(8,128)(2,1)} %get-tuple-element.30.refs_2_) | copy-start | bytes 1572868
  63.0 2.3 %collective-permute-start.7 = (bf16[8,256,128]{2,1,0:T(8,128)(2,1)S(1)}, bf16[8,256,128]{2,1,0:T(8,128)(2,1)S(1)}, u32[]{:S(2)}, u32[]{:S(2)}) collective-permute-start(bf16[8,256,128]{2,1,0:T(8,128)(2,1)S(1)} %get-tuple-element.36), channel_id=1, source_target_pairs={{0,1},{1,0},{2,3},{3,2},{4,5},{5,4},{6,7},{7,6},{8,9},{9,8},{10,11... | collective-permute-start | bytes 1572872 | tf_op jit(solution)/shard_map/ppermute | solution.py:261
  63.7 6.3 %collective-permute-start.8 = (bf16[256,256]{1,0:T(8,128)(2,1)S(1)}, bf16[256,256]{1,0:T(8,128)(2,1)S(1)}, u32[]{:S(2)}, u32[]{:S(2)}) collective-permute-start(bf16[256,256]{1,0:T(8,128)(2,1)S(1)} %get-tuple-element.41), channel_id=1, source_target_pairs={{0,2},{1,3},{2,0},{3,1},{4,6},{5,7},{6,4},{7,5},{8,10},{9,11},{10,... | collective-permute-start | bytes 393224 | tf_op jit(solution)/shard_map/ppermute | solution.py:261
  66.3 3.7 %copy-start.9 = (bf16[1,128,1024]{2,1,0:T(8,128)(2,1)S(1)}, bf16[1,128,1024]{2,1,0:T(8,128)(2,1)}, u32[]{:S(2)}) copy-start(bf16[1,128,1024]{2,1,0:T(8,128)(2,1)} %refs_2_.1) | copy-start | bytes 786436
  66.3 30.7 %all-to-all-start.2 = ((bf16[8,384,128]{2,1,0:T(8,128)(2,1)}), bf16[8,384,128]{2,1,0:T(8,128)(2,1)S(1)}, u32[]{:S(2)}, u32[]{:S(2)}) async-start(bf16[8,384,128]{2,1,0:T(8,128)(2,1)} %combine.1), calls=%async_computation.2 | async-start | bytes 1572864 | tf_op jit(solution)/shard_map/all_to_all | solution.py:306
  70.8 8.5 %collective-permute-start.9 = (bf16[128,1024]{1,0:T(8,128)(2,1)S(1)}, bf16[128,1024]{1,0:T(8,128)(2,1)S(1)}, u32[]{:S(2)}, u32[]{:S(2)}) collective-permute-start(bf16[128,1024]{1,0:T(8,128)(2,1)S(1)} %get-tuple-element.46), channel_id=1, source_target_pairs={{0,16},{16,0},{1,17},{17,1},{2,18},{18,2},{3,19},{19,3},{4,20},{20... | collective-permute-start | bytes 786440 | tf_op jit(solution)/shard_map/ppermute | solution.py:265
  79.4 10.2 %collective-permute-start.12 = (bf16[32,1024]{1,0:T(8,128)(2,1)S(1)}, bf16[32,1024]{1,0:T(8,128)(2,1)S(1)}, u32[]{:S(2)}, u32[]{:S(2)}) collective-permute-start(bf16[32,1024]{1,0:T(8,128)(2,1)S(1)} %get-tuple-element.50), channel_id=1, source_target_pairs={{0,12},{1,13},{2,14},{3,15},{4,8},{5,9},{6,10},{7,11},{8,4},{9,5},... | collective-permute-start | bytes 196616 | tf_op jit(solution)/shard_map/ppermute | solution.py:261
  82.9 13.4 %collective-permute-start.11 = (bf16[32,1024]{1,0:T(8,128)(2,1)S(1)}, bf16[32,1024]{1,0:T(8,128)(2,1)S(1)}, u32[]{:S(2)}, u32[]{:S(2)}) collective-permute-start(bf16[32,1024]{1,0:T(8,128)(2,1)S(1)} %get-tuple-element.51), channel_id=1, source_target_pairs={{0,8},{1,9},{2,10},{3,11},{4,12},{5,13},{6,14},{7,15},{8,0},{9,1},... | collective-permute-start | bytes 196616 | tf_op jit(solution)/shard_map/ppermute | solution.py:261
  82.9 13.4 %collective-permute-start.10 = (bf16[32,1024]{1,0:T(8,128)(2,1)S(1)}, bf16[32,1024]{1,0:T(8,128)(2,1)S(1)}, u32[]{:S(2)}, u32[]{:S(2)}) collective-permute-start(bf16[32,1024]{1,0:T(8,128)(2,1)S(1)} %get-tuple-element.49), channel_id=1, source_target_pairs={{0,4},{1,5},{2,6},{3,7},{4,0},{5,1},{6,2},{7,3},{8,12},{9,13},{10,... | collective-permute-start | bytes 196616 | tf_op jit(solution)/shard_map/ppermute | solution.py:261

commit v3 on v2

--- a/solution.py
+++ b/solution.py
@@ -107,13 +107,13 @@
 
 
 def d_out_body(ids_ref, grad_ref, *refs):
-    *weight_refs, send_ref, tile_ref, sem = refs
+    *weight_refs, tile_ref = refs[: -HEADS - 1] + refs[-1:]
+    piece_refs = refs[-HEADS - 1 : -1]
     for place in range(HEADS):
         h, weight = weight_rows(ids_ref, weight_refs, place)
         tile_ref[h] = dot(grad_ref[0], weight, NT).astype(BF16)
-    copy = pltpu.make_async_copy(tile_ref, send_ref.at[:, pl.ds(0, BLOCK), :], sem)
-    copy.start()
-    copy.wait()
+    for k, ref in enumerate(piece_refs):
+        ref[...] = tile_ref[ids_ref[0] ^ k]
 
 
 def output_body(ids_ref, back_ref, *refs):
@@ -121,7 +121,7 @@
     total = jnp.zeros(out_ref.shape[1:], F32)
     for place in range(HEADS):
         h, weight = weight_rows(ids_ref, weight_refs, place)
-        total += dot(back_ref[h, BLOCK:, :], weight, TN)
+        total += dot(back_ref[h], weight, TN)
     out_ref[0] = total.astype(BF16)
 
 
@@ -132,7 +132,7 @@
 
 def forward_body(group, ids_ref, kb_ref, cnt_ref, *refs):
     own_ref, *other_refs = refs[:group]
-    _, send_ref, probs_ref, kv_ref, s_ref, p_ref, t_ref, sems = refs[group:]
+    send_ref, probs_ref, kv_ref, s_ref, p_ref, t_ref, sems = refs[group:]
     kv_ref[0] = own_ref[:, BLOCK:, :]
     for r, ref in enumerate(other_refs):
         kv_ref[r + 1] = ref[:, BLOCK:, :]
@@ -156,16 +156,17 @@
             p_ref[j, :, BLOCK:], kv_ref[picks[j][0], picks[j][1], BLOCK:, :], NN
         )
         t_ref[j] = attn.T.astype(BF16)
-    copies.append(pltpu.make_async_copy(t_ref, send_ref.at[:, pl.ds(BLOCK, BLOCK), :], sems.at[1]))
+    copies.append(pltpu.make_async_copy(t_ref, send_ref, sems.at[1]))
     copies[-1].start()
     for copy in copies:
         copy.wait()
 
 
-def backward_body(group, ids_ref, kb_ref, back_ref, *refs):
+def backward_body(group, ids_ref, kb_ref, *refs):
+    piece_refs, refs = refs[:HEADS], refs[HEADS:]
     own_ref, *other_refs = refs[:group]
-    probs_ref, dq_ref, near_ref, *far_refs = refs[group:-7]
-    q_ref, kv_ref, p_ref, dp_ref, ds_ref, acc_ref, sems = refs[-7:]
+    probs_ref, dq_ref, near_ref, *far_refs = refs[group:-8]
+    q_ref, kv_ref, do_ref, p_ref, dp_ref, ds_ref, acc_ref, sems = refs[-8:]
     loads = [pltpu.make_async_copy(own_ref.at[:, pl.ds(BLOCK, 2 * BLOCK), :], kv_ref.at[0], sems.at[0])]
     for r, ref in enumerate(other_refs):
         loads.append(
@@ -175,13 +176,15 @@
     loads.append(pltpu.make_async_copy(own_ref.at[:, pl.ds(0, BLOCK), :], q_ref, sems.at[group + 1]))
     for copy in loads:
         copy.start()
+    for k, ref in enumerate(piece_refs):
+        do_ref[ids_ref[0] ^ k] = ref[...]
     picks = [second_block(ids_ref, kb_ref, j, group) for j in range(HEADS)]
     for r in range(1, group):
         acc_ref[r] = jnp.zeros(acc_ref.shape[1:], F32)
     for copy in loads[:group]:
         copy.wait()
     for j in range(HEADS):
-        do = back_ref[j, :BLOCK, :]
+        do = do_ref[j]
         dp_ref[j, :, :BLOCK] = dot(do, kv_ref[0, j, BLOCK:, :], NT)
         dp_ref[j, :, BLOCK:] = dot(do, kv_ref[picks[j][0], picks[j][1], BLOCK:, :], NT)
     for copy in loads[group:]:
@@ -194,7 +197,7 @@
     second = []
     for j in range(HEADS):
         dk = dot(ds_ref[j], q_ref[j], TN)
-        dv = dot(p_ref[j], back_ref[j, :BLOCK, :], TN)
+        dv = dot(p_ref[j], do_ref[j], TN)
         acc_ref[0, j, :BLOCK, :] = dk[:BLOCK]
         acc_ref[0, j, BLOCK:, :] = dv[:BLOCK]
         dp_ref[j, :, :BLOCK] = dk[BLOCK:]
@@ -228,7 +231,7 @@
 def feature_body(ids_ref, mine_ref, pair_ref, *out_refs):
     d, z, y, c = ids_ref[2], ids_ref[3], ids_ref[4], ids_ref[5]
     for yr, ref in enumerate(out_refs):
-        first = pl.multiple_of(BLOCK + (yr ^ y) * 64 + c * 32, 32)
+        first = pl.multiple_of((yr ^ y) * 64 + c * 32, 32)
         for place in range(HEADS):
             h = ((place >> 2) ^ d) * 4 + ((place & 3) ^ z)
             rows = slice(place * 32, (place + 1) * 32)
@@ -286,6 +289,9 @@
     total = (keep + dp_swap(send).astype(F32)).reshape(4, 32, columns)
     parts = [ctx_swap(total[zr].astype(BF16), 4 * zr) for zr in range(1, 4)]
     return total[0] + sum(part.astype(F32) for part in parts)
+
+
+D_OUT_FLOPS = 2**32
 
 
 def local(queries, keys, values, out_weight, out_grad, key_blocks, block_counts):
@@ -309,8 +315,7 @@
         near, rows = out_weight, out_weight.shape[0] // 2
         half = dp_swap(lax.dynamic_slice_in_dim(near, (position & 1) * rows, rows, 0))
     if small:
-        same, cross = [out_grad, ctx_swap(out_grad, 2)], [ctx_swap(out_grad, 1)]
-        cross.append(ctx_swap(same[1], 1))
+        cross = [ctx_swap(out_grad, 1)]
     if dp_count == 2:
         far = [half, ctx_swap(half, 1)]
     else:
@@ -323,35 +328,42 @@
     tile = shape((HEADS, BLOCK, HEAD_SIZE))
     tile_scratch = pltpu.VMEM(tile.shape, BF16)
     score = (HEADS, BLOCK, 2 * BLOCK)
-    if small:
-        own, same[1], *rest = together(own, same[1], *cross, *far)
-        cross, far = rest[:2], rest[2:]
-    send = call(
-        d_out_body, pair, [tile_scratch, pltpu.SemaphoreType.DMA],
-        n_smem=1, n_vmem=4, out_specs=HBM, vmem=60, flops=2**33, name="d_out",
+    pieces = call(
+        d_out_body, [shape((BLOCK, HEAD_SIZE))] * HEADS, [tile_scratch],
+        n_smem=1, n_vmem=4, flops=D_OUT_FLOPS, name="d_out",
     )(ids, out_grad, near, *far)
+    pieces = [pieces[0]] + [ctx_swap(pieces[k], k * group) for k in range(1, HEADS)]
+    if small:
+        own, cross[0], *pieces = together(own, cross[0], *pieces)
+    else:
+        own, *pieces = together(own, *pieces)
     others = [ctx_swap(own, r) for r in range(1, group)]
     vmem = 16 if group == 2 else 40
     kv_scratch = pltpu.VMEM((group, HEADS, 2 * BLOCK, HEAD_SIZE), BF16)
     send, probs = call(
         functools.partial(forward_body, group),
-        [pair, shape(score)],
+        [tile, shape(score)],
         [kv_scratch, pltpu.VMEM(score, F32), pltpu.VMEM(score, BF16), tile_scratch, pltpu.SemaphoreType.DMA((2,))],
-        n_smem=3, n_vmem=group, n_hbm=1, out_specs=[HBM] * 2, vmem=60, alias={3 + group: 0}, name="forward",
-    )(ids, key_blocks, block_counts, own, *others, send)
+        n_smem=3, n_vmem=group, out_specs=[HBM] * 2, vmem=vmem, name="forward",
+    )(ids, key_blocks, block_counts, own, *others)
     back = exchange(send)
+    if small:
+        same = [out_grad, ctx_swap(out_grad, 2)]
+        cross.append(ctx_swap(same[1], 1))
+        back, same[1], cross[1] = together(back, same[1], cross[1])
     dq, near_kv, *far_kv = call(
         functools.partial(backward_body, group),
         [tile, pair] + [pair] * (group - 1),
         [
-            tile_scratch, kv_scratch, pltpu.VMEM(score, BF16), pltpu.VMEM(score, F32), pltpu.VMEM(score, BF16),
+            tile_scratch, kv_scratch, tile_scratch, pltpu.VMEM(score, BF16), pltpu.VMEM(score, F32),
+            pltpu.VMEM(score, BF16),
             pltpu.VMEM((group, HEADS, 2 * BLOCK, HEAD_SIZE), F32), pltpu.SemaphoreType.DMA((group + 2,)),
         ],
-        n_smem=2, n_vmem=1, n_hbm=group + 1, vmem=vmem, name="backward",
-    )(ids, key_blocks, back, own, *others, probs)
+        n_smem=2, n_vmem=HEADS, n_hbm=group + 1, vmem=vmem, name="backward",
+    )(ids, key_blocks, *pieces, own, *others, probs)
     arrived = [ctx_swap(part, r + 1) for r, part in enumerate(far_kv)]
     if small:
-        dq, *features = together(dq, *own_features(ids, back))
+        features = own_features(ids, back)
     grads = exchange(
         call(
             combine_body, shape((HEADS, 3 * BLOCK, HEAD_SIZE)), n_vmem=group + 1,
@@ -364,7 +376,7 @@
         grad_weight = reduce_weight(features, same + cross)
     else:
         grad_weight = lax.psum_scatter(
-            dot(back[:, BLOCK:, :].reshape(HEADS * HEAD_SIZE, BLOCK), out_grad[0], NN),
+            dot(back.reshape(HEADS * HEAD_SIZE, BLOCK), out_grad[0], NN),
             ("dp", "ctx"), scatter_dimension=0, tiled=True,
         )
     output = call(

time: 98.7 us -> 95.5 us (0.968)
  blocking collectives: 18.8 us -> 0 us
  starting transfers between devices: 22.7 us -> 36.3 us
  waiting for transfers between devices: 30.3 us -> 33.7 us
    all_to_all x1 -> x0, blocking collectives: 18.8 us -> none  [exchange(): return lax.all_to_all(x, 'ctx', 0, 0, tiled=True, axis_index_groups=peers)]
    ppermute x11 -> x18, starting transfers between devices: 8.59 us -> 18.8 us  [ctx_swap(): return lax.ppermute(x, 'ctx', [(i, i ^ mask) for i in range(n)])]
    ppermute x11 -> x18, waiting for transfers between devices: 11.2 us -> 20.6 us  [ctx_swap(): return lax.ppermute(x, 'ctx', [(i, i ^ mask) for i in range(n)])]
    ppermute x2, waiting for transfers between devices: 16.9 us -> 10.7 us  [dp_swap(): return lax.ppermute(x, 'dp', [(0, 1), (1, 0)])]
    pallas_call x2, Pallas kernels: 6.84 us -> 4.8 us  [the longest x1 3.53 us: local(): call(functools.partial(forward_body, group), [tile, shape(score)], [kv_sc...]
    all_to_all x2 -> x3, starting transfers between devices: 11.1 us -> 13.1 us  [exchange(): return lax.all_to_all(x, 'ctx', 0, 0, tiled=True, axis_index_groups=peers)]
    ppermute x2, starting transfers between devices: 2.99 us -> 4.45 us  [dp_swap(): return lax.ppermute(x, 'dp', [(0, 1), (1, 0)])]
    unnamed x29 -> x33, local copies, waits for them, and re-layouts: 5.18 us -> 4.03 us
  transfers between devices with their start and end apart: 15 -> 23, of which waited for: 6 -> 11; matrix products, arithmetic and copies ran while one was open for 2% -> 1% of each run, Pallas kernels for 12% -> 18%
where the time goes in v3:
time: 95.5 us; the launch traced here: 95 us
  starting transfers between devices  36.3 us (38%)
  waiting for transfers between devices  33.7 us (35%)
  Pallas kernels  18.1 us (19%)
  local copies, waits for them, and re-layouts  5.21 us (5%)
    ppermute x18, waiting for transfers between devices, ctx_swap(): return lax.ppermute(x, 'ctx', [(i, i ^ mask) for i in range(n)])  20.6 us
    ppermute x18, starting transfers between devices, ctx_swap(): return lax.ppermute(x, 'ctx', [(i, i ^ mask) for i in range(n)])  18.8 us
    all_to_all x3, starting transfers between devices, exchange(): return lax.all_to_all(x, 'ctx', 0, 0, tiled=True, axis_index_groups=peers)  13.1 us
    ppermute x2, waiting for transfers between devices, dp_swap(): return lax.ppermute(x, 'dp', [(0, 1), (1, 0)])  10.7 us
    ppermute x2, starting transfers between devices, dp_swap(): return lax.ppermute(x, 'dp', [(0, 1), (1, 0)])  4.45 us
    pallas_call x1, Pallas kernels, local(): call(functools.partial(backward_body, group), [tile, pair] + [pair] * (gr...  4.11 us
    unnamed x33, local copies, waits for them, and re-layouts  4.03 us
    pallas_call x1, Pallas kernels, local(): call(functools.partial(forward_body, group), [tile, shape(score)], [kv_sc...  3.53 us
  transfers between devices with their start and end apart: 23, of which 11 were waited for; matrix products, arithmetic and copies ran while one was open for 1% of the time, Pallas kernels for 18%

profile of v3, /device:TPU:0, one launch (start us, length us, event | category | flops | bytes accessed | tf_op | source)
XLA Modules:
  0.0 95.0 jit_solution(16840430433385485468)
XLA Ops:
  0.6 1.1 %constant_dynamic-slice_fusion = bf16[256,1024]{1,0:T(8,128)(2,1)S(1)} fusion(bf16[512,1024]{1,0:T(8,128)(2,1)} %refs_0_.3, s32[]{:T(128)S(6)} %select_n.16), kind=kLoop, calls=%fused_computation.2 | loop fusion | bytes 1048580 | tf_op jit(solution)/shard_map/dynamic_slice | solution.py:316
  1.7 3.0 %collective-permute-start.1 = (bf16[256,1024]{1,0:T(8,128)(2,1)S(1)}, bf16[256,1024]{1,0:T(8,128)(2,1)S(1)}, u32[]{:S(2)}, u32[]{:S(2)}) collective-permute-start(bf16[256,1024]{1,0:T(8,128)(2,1)S(1)} %constant_dynamic-slice_fusion), channel_id=1, source_target_pairs={{0,16},{16,0},{1,17},{17,1},{2,18},{18,2},{3,19},{19,3},{4,20},{20... | collective-permute-start | bytes 1572872 | tf_op jit(solution)/shard_map/ppermute | solution.py:268
  4.7 1.9 %pack.1 = bf16[8,384,128]{2,1,0:T(8,128)(2,1)} custom-call(bf16[1,128,1024]{2,1,0:T(8,128)(2,1)} %q_ref.1, bf16[1,128,1024]{2,1,0:T(8,128)(2,1)} %k_ref.1, bf16[1,128,1024]{2,1,0:T(8,128)(2,1)} %v_ref.1), custom_call_target="tpu_custom_call" | custom-call | flops 34359738368 | tf_op jit(solution)/shard_map/pack/pallas_call | solution.py:75
  6.7 0.0 copy-start.8
  6.7 0.0 copy-start
  6.7 6.0 %all-to-all-start = ((bf16[8,384,128]{2,1,0:T(8,128)(2,1)}), bf16[8,384,128]{2,1,0:T(8,128)(2,1)S(1)}, u32[]{:S(2)}, u32[]{:S(2)}) async-start(bf16[8,384,128]{2,1,0:T(8,128)(2,1)} %pack.1), calls=%async_computation | async-start | bytes 1572864 | tf_op jit(solution)/shard_map/all_to_all | solution.py:312
  12.7 4.0 %collective-permute-done.1.refs_1_ = bf16[256,1024]{1,0:T(8,128)(2,1)S(1)} collective-permute-done((bf16[256,1024]{1,0:T(8,128)(2,1)S(1)}, bf16[256,1024]{1,0:T(8,128)(2,1)S(1)}, u32[]{:S(2)}, u32[]{:S(2)}) %collective-permute-start.1) | collective-permute-done | bytes 524320 | tf_op jit(solution)/shard_map/ppermute | solution.py:268
  16.7 0.0 collective-permute-start.2
  16.7 0.5 collective-permute-start
  17.2 0.1 stack.28.ids_ref
  17.3 1.3 %collective-permute-done.2.refs_2_ = bf16[256,1024]{1,0:T(8,128)(2,1)S(1)} collective-permute-done((bf16[256,1024]{1,0:T(8,128)(2,1)S(1)}, bf16[256,1024]{1,0:T(8,128)(2,1)S(1)}, u32[]{:S(2)}, u32[]{:S(2)}) %collective-permute-start.2) | collective-permute-done | bytes 524320 | tf_op jit(solution)/shard_map/ppermute | solution.py:264
  18.6 1.3 %d_out.1 = (bf16[128,128]{1,0:T(8,128)(2,1)S(1)}, bf16[128,128]{1,0:T(8,128)(2,1)S(1)}, bf16[128,128]{1,0:T(8,128)(2,1)S(1)}, bf16[128,128]{1,0:T(8,128)(2,1)S(1...) custom-call(s32[7]{0:T(128)S(1)} %stack.28.ids_ref, ...), custom_call_target="tpu_custom_call" | custom-call | flops 4294967296 | tf_op jit(solution)/shard_map/d_out/pallas_call | solution.py:331
  19.9 0.0 copy-start.15
  19.9 1.8 %collective-permute-start.3 = (bf16[128,128]{1,0:T(8,128)(2,1)S(1)}, bf16[128,128]{1,0:T(8,128)(2,1)S(1)}, u32[]{:S(2)}, u32[]{:S(2)}) collective-permute-start(bf16[128,128]{1,0:T(8,128)(2,1)S(1)} %get-tuple-element.39), channel_id=1, source_target_pairs={{0,2},{1,3},{2,0},{3,1},{4,6},{5,7},{6,4},{7,5},{8,10},{9,11},{10,... | collective-permute-start | bytes 98312 | tf_op jit(solution)/shard_map/ppermute | solution.py:264
  21.7 1.6 %collective-permute-start.4 = (bf16[128,128]{1,0:T(8,128)(2,1)S(1)}, bf16[128,128]{1,0:T(8,128)(2,1)S(1)}, u32[]{:S(2)}, u32[]{:S(2)}) collective-permute-start(bf16[128,128]{1,0:T(8,128)(2,1)S(1)} %get-tuple-element.40), channel_id=1, source_target_pairs={{0,4},{1,5},{2,6},{3,7},{4,0},{5,1},{6,2},{7,3},{8,12},{9,13},{10,... | collective-permute-start | bytes 98312 | tf_op jit(solution)/shard_map/ppermute | solution.py:264
  23.3 0.1 collective-permute-start.5
  23.4 2.8 %collective-permute-start.6 = (bf16[128,128]{1,0:T(8,128)(2,1)S(1)}, bf16[128,128]{1,0:T(8,128)(2,1)S(1)}, u32[]{:S(2)}, u32[]{:S(2)}) collective-permute-start(bf16[128,128]{1,0:T(8,128)(2,1)S(1)} %get-tuple-element.42), channel_id=1, source_target_pairs={{0,8},{1,9},{2,10},{3,11},{4,12},{5,13},{6,14},{7,15},{8,0},{9,1},... | collective-permute-start | bytes 98312 | tf_op jit(solution)/shard_map/ppermute | solution.py:264
  26.3 0.0 collective-permute-done.refs_4_
  26.3 0.7 copy-done.9
  27.0 1.3 %collective-permute-start.7 = (bf16[128,128]{1,0:T(8,128)(2,1)S(1)}, bf16[128,128]{1,0:T(8,128)(2,1)S(1)}, u32[]{:S(2)}, u32[]{:S(2)}) collective-permute-start(bf16[128,128]{1,0:T(8,128)(2,1)S(1)} %get-tuple-element.43), channel_id=1, source_target_pairs={{0,10},{1,11},{2,8},{3,9},{4,14},{5,15},{6,12},{7,13},{8,2},{9,3},... | collective-permute-start | bytes 98312 | tf_op jit(solution)/shard_map/ppermute | solution.py:264
  28.3 0.0 collective-permute-done.3.refs_1_
  28.3 3.6 %collective-permute-start.8 = (bf16[128,128]{1,0:T(8,128)(2,1)S(1)}, bf16[128,128]{1,0:T(8,128)(2,1)S(1)}, u32[]{:S(2)}, u32[]{:S(2)}) collective-permute-start(bf16[128,128]{1,0:T(8,128)(2,1)S(1)} %get-tuple-element.44), channel_id=1, source_target_pairs={{0,12},{1,13},{2,14},{3,15},{4,8},{5,9},{6,10},{7,11},{8,4},{9,5},... | collective-permute-start | bytes 98312 | tf_op jit(solution)/shard_map/ppermute | solution.py:264
  31.9 0.0 collective-permute-done.4.refs_2_
  31.9 0.0 collective-permute-start.9
  31.9 0.0 collective-permute-done.5.refs_3_
  31.9 5.0 %collective-permute-done.6.refs_4_ = bf16[128,128]{1,0:T(8,128)(2,1)S(1)} collective-permute-done((bf16[128,128]{1,0:T(8,128)(2,1)S(1)}, bf16[128,128]{1,0:T(8,128)(2,1)S(1)}, u32[]{:S(2)}, u32[]{:S(2)}) %collective-permute-start.6) | collective-permute-done | bytes 32800 | tf_op jit(solution)/shard_map/ppermute | solution.py:264
  36.9 1.1 %collective-permute-done.7.refs_5_ = bf16[128,128]{1,0:T(8,128)(2,1)S(1)} collective-permute-done((bf16[128,128]{1,0:T(8,128)(2,1)S(1)}, bf16[128,128]{1,0:T(8,128)(2,1)S(1)}, u32[]{:S(2)}, u32[]{:S(2)}) %collective-permute-start.7) | collective-permute-done | bytes 32800 | tf_op jit(solution)/shard_map/ppermute | solution.py:264
  38.0 0.0 collective-permute-done.8.refs_6_
  38.0 0.6 collective-permute-done.9.refs_7_
  38.6 0.0 all-to-all-done.refs_0_.refs_8_
  38.6 0.0 collective-permute-start.10
  38.6 0.6 collective-permute-start.11
  39.2 0.1 copy.12.kb_ref
  39.3 1.6 %collective-permute-done.10.refs_1_.refs_9_ = bf16[8,384,128]{2,1,0:T(8,128)(2,1)S(1)} collective-permute-done((bf16[8,384,128]{2,1,0:T(8,128)(2,1)S(1)}, bf16[8,384,128]{2,1,0:T(8,128)(2,1)S(1)}, u32[]{:S(2)}, u32[]{:S(2)}) %collective-permute-start.10) | collective-permute-done | bytes 786464 | tf_op jit(solution)/shard_map/ppermute | solution.py:264
  40.9 3.5 %forward.1 = (bf16[8,128,128]{2,1,0:T(8,128)(2,1)}, bf16[8,128,256]{2,1,0:T(8,128)(2,1)S(1)}) custom-call(s32[7]{0:T(128)S(1)} %stack.28.ids_ref, s32[1,8,16,2]{3,2,1,0:T(8,128)S(1)} %copy.12.kb_ref, s32[1,8,16]{2,1,0:T(8,128)S(1)} %copy-done.5, bf16[8,384,128]{2,1,0:T(8,128)(2,1)S(1)} %all-to-all-done.refs_0_.refs_8_, ...), custom_call_target="tpu_custom_call" | custom-call | tf_op jit(solution)/shard_map/forward/pallas_call | solution.py:343
  44.4 3.4 %all-to-all-start.1 = ((bf16[8,128,128]{2,1,0:T(8,128)(2,1)}), bf16[8,128,128]{2,1,0:T(8,128)(2,1)S(1)}, u32[]{:S(2)}, u32[]{:S(2)}) async-start(bf16[8,128,128]{2,1,0:T(8,128)(2,1)} %get-tuple-element.47), calls=%async_computation.1 | async-start | bytes 524288 | tf_op jit(solution)/shard_map/all_to_all | solution.py:312
  47.9 0.2 collective-permute-start.12
  48.1 4.1 %backward.1 = (bf16[8,128,128]{2,1,0:T(8,128)(2,1)S(1)}, bf16[8,256,128]{2,1,0:T(8,128)(2,1)S(1)}, bf16[8,256,128]{2,1,0:T(8,128)(2,1)}) custom-call(s32[7]{0:T(128)S(1)} %stack.28.ids_ref, s32[1,8,16,2]{3,2,1,0:T(8,128)S(1)} %copy.12.kb_ref, bf16[128,128]{1,0:T(8,128)(2,1)S(1)} %get-tuple-element.49.refs_0_, ...), custom_call_target="tpu_custom_call" | custom-call | tf_op jit(solution)/shard_map/backward/pallas_call | solution.py:354
  52.2 0.8 copy-done.6
  53.0 0.7 copy-done.13
  53.7 0.4 collective-permute-start.13
  54.1 0.0 collective-permute-done.12.refs_5_
  54.1 0.7 copy-done.11
  54.8 2.5 %all-to-all-done.1.back_ref.mine_ref = bf16[8,128,128]{2,1,0:T(8,128)(2,1)S(1)} async-done(((bf16[8,128,128]{2,1,0:T(8,128)(2,1)}), bf16[8,128,128]{2,1,0:T(8,128)(2,1)S(1)}, u32[]{:S(2)}, u32[]{:S(2)}) %all-to-all-start.1) | async-done | bytes 262176 | tf_op jit(solution)/shard_map/all_to_all | solution.py:312
  57.3 1.5 %collective-permute-done.14.pair_ref = bf16[8,128,128]{2,1,0:T(8,128)(2,1)S(1)} collective-permute-done((bf16[8,128,128]{2,1,0:T(8,128)(2,1)S(1)}, bf16[8,128,128]{2,1,0:T(8,128)(2,1)S(1)}, u32[]{:S(2)}, u32[]{:S(2)}) %collective-permute-start.14) | collective-permute-done | bytes 262176 | tf_op jit(solution)/shard_map/ppermute | solution.py:264
  58.8 1.3 %features.1 = (bf16[256,256]{1,0:T(8,128)(2,1)S(1)}, bf16[256,256]{1,0:T(8,128)(2,1)}) custom-call(s32[7]{0:T(128)S(1)} %stack.28.ids_ref, bf16[8,128,128]{2,1,0:T(8,128)(2,1)S(1)} %all-to-all-done.1.back_ref.mine_ref, bf16[8,128,128]{2,1,0:T(8,128)(2,1)S(1)} %collective-permute-done.14.pair_ref), custom_call_target="tpu_custom_call" | custom-call | tf_op jit(solution)/shard_map/features/pallas_call | solution.py:276
  60.1 1.4 %collective-permute-start.15 = (bf16[256,256]{1,0:T(8,128)(2,1)}, bf16[256,256]{1,0:T(8,128)(2,1)S(1)}, u32[]{:S(2)}, u32[]{:S(2)}) collective-permute-start(bf16[256,256]{1,0:T(8,128)(2,1)} %get-tuple-element.65), channel_id=1, source_target_pairs={{0,2},{1,3},{2,0},{3,1},{4,6},{5,7},{6,4},{7,5},{8,10},{9,11},{10,... | collective-permute-start | bytes 393224 | tf_op jit(solution)/shard_map/ppermute | solution.py:264
  61.5 0.9 copy-done.14
  62.5 1.0 %combine.1 = bf16[8,384,128]{2,1,0:T(8,128)(2,1)} custom-call(bf16[8,128,128]{2,1,0:T(8,128)(2,1)S(1)} %copy-done.14, bf16[8,256,128]{2,1,0:T(8,128)(2,1)S(1)} %copy-done.7, bf16[8,256,128]{2,1,0:T(8,128)(2,1)S(1)} %collective-permute-done.13.refs_0_), custom_call_target="tpu_custom_call" | custom-call | flops 8589934592 | tf_op jit(solution)/shard_map/combine/pallas_call | solution.py:368
  63.5 3.7 %all-to-all-start.2 = ((bf16[8,384,128]{2,1,0:T(8,128)(2,1)}), bf16[8,384,128]{2,1,0:T(8,128)(2,1)S(1)}, u32[]{:S(2)}, u32[]{:S(2)}) async-start(bf16[8,384,128]{2,1,0:T(8,128)(2,1)} %combine.1), calls=%async_computation.2 | async-start | bytes 1572864 | tf_op jit(solution)/shard_map/all_to_all | solution.py:312
  67.2 0.0 collective-permute-done.15.refs_1_
  67.2 0.8 grad_weight.1
  68.1 1.4 %collective-permute-start.16 = (bf16[128,1024]{1,0:T(8,128)(2,1)S(1)}, bf16[128,1024]{1,0:T(8,128)(2,1)S(1)}, u32[]{:S(2)}, u32[]{:S(2)}) collective-permute-start(bf16[128,1024]{1,0:T(8,128)(2,1)S(1)} %get-tuple-element.70), channel_id=1, source_target_pairs={{0,16},{16,0},{1,17},{17,1},{2,18},{18,2},{3,19},{19,3},{4,20},{20... | collective-permute-start | bytes 786440 | tf_op jit(solution)/shard_map/ppermute | solution.py:268
  69.5 6.7 %collective-permute-done.16 = bf16[128,1024]{1,0:T(8,128)(2,1)S(1)} collective-permute-done((bf16[128,1024]{1,0:T(8,128)(2,1)S(1)}, bf16[128,1024]{1,0:T(8,128)(2,1)S(1)}, u32[]{:S(2)}, u32[]{:S(2)}) %collective-permute-start.16) | collective-permute-done | bytes 262176 | tf_op jit(solution)/shard_map/ppermute | solution.py:268
  76.2 0.1 fusion
  76.3 3.5 %collective-permute-start.19 = (bf16[32,1024]{1,0:T(8,128)(2,1)S(1)}, bf16[32,1024]{1,0:T(8,128)(2,1)S(1)}, u32[]{:S(2)}, u32[]{:S(2)}) collective-permute-start(bf16[32,1024]{1,0:T(8,128)(2,1)S(1)} %get-tuple-element.74), channel_id=1, source_target_pairs={{0,12},{1,13},{2,14},{3,15},{4,8},{5,9},{6,10},{7,11},{8,4},{9,5},... | collective-permute-start | bytes 196616 | tf_op jit(solution)/shard_map/ppermute | solution.py:264
  79.8 0.9 collective-permute-start.17
  80.7 3.0 %output.1 = bf16[1,128,1024]{2,1,0:T(8,128)(2,1)} custom-call(s32[7]{0:T(128)} %copy-done.4, bf16[8,128,128]{2,1,0:T(8,128)(2,1)} %copy-done.1, bf16[512,1024]{1,0:T(8,128)(2,1)} %refs_0_.3, bf16[256,1024]{1,0:T(8,128)(2,1)} %copy-done.2, bf16[256,1024]{1,0:T(8,128)(2,1)} %copy-done.3), custom_call_target="tpu_custom_call" | custom-call | tf_op jit(solution)/shard_map/output/pallas_call | solution.py:382
  83.8 3.0 %collective-permute-done.19 = bf16[32,1024]{1,0:T(8,128)(2,1)S(1)} collective-permute-done((bf16[32,1024]{1,0:T(8,128)(2,1)S(1)}, bf16[32,1024]{1,0:T(8,128)(2,1)S(1)}, u32[]{:S(2)}, u32[]{:S(2)}) %collective-permute-start.19) | collective-permute-done | bytes 65568 | tf_op jit(solution)/shard_map/ppermute | solution.py:264
  86.8 6.4 %collective-permute-done.18 = bf16[32,1024]{1,0:T(8,128)(2,1)S(1)} collective-permute-done((bf16[32,1024]{1,0:T(8,128)(2,1)S(1)}, bf16[32,1024]{1,0:T(8,128)(2,1)S(1)}, u32[]{:S(2)}, u32[]{:S(2)}) %collective-permute-start.18) | collective-permute-done | bytes 65568 | tf_op jit(solution)/shard_map/ppermute | solution.py:264
  93.2 0.0 collective-permute-done.17
  93.2 0.7 slice_add_fusion
  93.9 0.0 all-to-all-done.2.recv_ref
  93.9 1.1 %unpack.1 = (bf16[1,128,1024]{2,1,0:T(8,128)(2,1)}, bf16[1,128,1024]{2,1,0:T(8,128)(2,1)}, bf16[1,128,1024]{2,1,0:T(8,128)(2,1)}) custom-call(bf16[8,384,128]{2,1,0:T(8,128)(2,1)S(1)} %all-to-all-done.2.recv_ref), custom_call_target="tpu_custom_call" | custom-call | tf_op jit(solution)/shard_map/unpack/pallas_call | solution.py:374
  (29 shorter events, 0.1 us)
Async XLA Ops:
  1.7 14.9 %collective-permute-start.1 = (bf16[256,1024]{1,0:T(8,128)(2,1)S(1)}, bf16[256,1024]{1,0:T(8,128)(2,1)S(1)}, u32[]{:S(2)}, u32[]{:S(2)}) collective-permute-start(bf16[256,1024]{1,0:T(8,128)(2,1)S(1)} %constant_dynamic-slice_fusion), channel_id=1, source_target_pairs={{0,16},{16,0},{1,17},{17,1},{2,18},{18,2},{3,19},{19,3},{4,20},{20... | collective-permute-start | bytes 1572872 | tf_op jit(solution)/shard_map/ppermute | solution.py:268
  6.7 10.0 %copy-start.8 = (bf16[1,128,1024]{2,1,0:T(8,128)(2,1)S(1)}, bf16[1,128,1024]{2,1,0:T(8,128)(2,1)}, u32[]{:S(2)}) copy-start(bf16[1,128,1024]{2,1,0:T(8,128)(2,1)} %refs_2_.1) | copy-start | bytes 786436
  6.7 11.9 %copy-start = (bf16[512,1024]{1,0:T(8,128)(2,1)S(1)}, bf16[512,1024]{1,0:T(8,128)(2,1)}, u32[]{:S(2)}) copy-start(bf16[512,1024]{1,0:T(8,128)(2,1)} %refs_0_.3) | copy-start | bytes 3145732
  6.7 31.9 %all-to-all-start = ((bf16[8,384,128]{2,1,0:T(8,128)(2,1)}), bf16[8,384,128]{2,1,0:T(8,128)(2,1)S(1)}, u32[]{:S(2)}, u32[]{:S(2)}) async-start(bf16[8,384,128]{2,1,0:T(8,128)(2,1)} %pack.1), calls=%async_computation | async-start | bytes 1572864 | tf_op jit(solution)/shard_map/all_to_all | solution.py:312
  16.6 3.2 %copy-start.2 = (bf16[256,1024]{1,0:T(8,128)(2,1)}, bf16[256,1024]{1,0:T(8,128)(2,1)S(1)}, u32[]{:S(2)}) copy-start(bf16[256,1024]{1,0:T(8,128)(2,1)S(1)} %collective-permute-done.1.refs_1_) | copy-start | bytes 1572868
  16.7 1.9 %collective-permute-start.2 = (bf16[256,1024]{1,0:T(8,128)(2,1)S(1)}, bf16[256,1024]{1,0:T(8,128)(2,1)S(1)}, u32[]{:S(2)}, u32[]{:S(2)}) collective-permute-start(bf16[256,1024]{1,0:T(8,128)(2,1)S(1)} %collective-permute-done.1.refs_1_), channel_id=1, source_target_pairs={{0,1},{1,0},{2,3},{3,2},{4,5},{5,4},{6,7},{7,6},{8,9},{9,8},{10,11... | collective-permute-start | bytes 1572872 | tf_op jit(solution)/shard_map/ppermute | solution.py:264
  16.7 9.6 %collective-permute-start = (bf16[1,128,1024]{2,1,0:T(8,128)(2,1)S(1)}, bf16[1,128,1024]{2,1,0:T(8,128)(2,1)S(1)}, u32[]{:S(2)}, u32[]{:S(2)}) collective-permute-start(bf16[1,128,1024]{2,1,0:T(8,128)(2,1)S(1)} %copy-done.8), channel_id=1, source_target_pairs={{0,1},{1,0},{2,3},{3,2},{4,5},{5,4},{6,7},{7,6},{8,9},{9,8},{10,11... | collective-permute-start | bytes 786440 | tf_op jit(solution)/shard_map/ppermute | solution.py:264
  17.2 41.6 %copy-start.4 = (s32[7]{0:T(128)}, s32[7]{0:T(128)S(1)}, u32[]{:S(2)}) copy-start(s32[7]{0:T(128)S(1)} %stack.28.ids_ref) | copy-start | bytes 88
  18.6 1.3 %copy-start.3 = (bf16[256,1024]{1,0:T(8,128)(2,1)}, bf16[256,1024]{1,0:T(8,128)(2,1)S(1)}, u32[]{:S(2)}) copy-start(bf16[256,1024]{1,0:T(8,128)(2,1)S(1)} %collective-permute-done.2.refs_2_) | copy-start | bytes 1572868
  19.9 19.3 %copy-start.15 = (s32[1,8,16,2]{2,3,1,0:T(2,128)S(1)}, s32[1,8,16,2]{2,3,1,0:T(2,128)}, u32[]{:S(2)}) copy-start(s32[1,8,16,2]{2,3,1,0:T(2,128)} %param.12) | copy-start | bytes 3076
  19.9 8.4 %collective-permute-start.3 = (bf16[128,128]{1,0:T(8,128)(2,1)S(1)}, bf16[128,128]{1,0:T(8,128)(2,1)S(1)}, u32[]{:S(2)}, u32[]{:S(2)}) collective-permute-start(bf16[128,128]{1,0:T(8,128)(2,1)S(1)} %get-tuple-element.39), channel_id=1, source_target_pairs={{0,2},{1,3},{2,0},{3,1},{4,6},{5,7},{6,4},{7,5},{8,10},{9,11},{10,... | collective-permute-start | bytes 98312 | tf_op jit(solution)/shard_map/ppermute | solution.py:264
  21.7 10.2 %collective-permute-start.4 = (bf16[128,128]{1,0:T(8,128)(2,1)S(1)}, bf16[128,128]{1,0:T(8,128)(2,1)S(1)}, u32[]{:S(2)}, u32[]{:S(2)}) collective-permute-start(bf16[128,128]{1,0:T(8,128)(2,1)S(1)} %get-tuple-element.40), channel_id=1, source_target_pairs={{0,4},{1,5},{2,6},{3,7},{4,0},{5,1},{6,2},{7,3},{8,12},{9,13},{10,... | collective-permute-start | bytes 98312 | tf_op jit(solution)/shard_map/ppermute | solution.py:264
  23.3 8.6 %collective-permute-start.5 = (bf16[128,128]{1,0:T(8,128)(2,1)S(1)}, bf16[128,128]{1,0:T(8,128)(2,1)S(1)}, u32[]{:S(2)}, u32[]{:S(2)}) collective-permute-start(bf16[128,128]{1,0:T(8,128)(2,1)S(1)} %get-tuple-element.41), channel_id=1, source_target_pairs={{0,6},{1,7},{2,4},{3,5},{4,2},{5,3},{6,0},{7,1},{8,14},{9,15},{10,... | collective-permute-start | bytes 98312 | tf_op jit(solution)/shard_map/ppermute | solution.py:264
  23.4 13.4 %collective-permute-start.6 = (bf16[128,128]{1,0:T(8,128)(2,1)S(1)}, bf16[128,128]{1,0:T(8,128)(2,1)S(1)}, u32[]{:S(2)}, u32[]{:S(2)}) collective-permute-start(bf16[128,128]{1,0:T(8,128)(2,1)S(1)} %get-tuple-element.42), channel_id=1, source_target_pairs={{0,8},{1,9},{2,10},{3,11},{4,12},{5,13},{6,14},{7,15},{8,0},{9,1},... | collective-permute-start | bytes 98312 | tf_op jit(solution)/shard_map/ppermute | solution.py:264
  26.3 0.7 copy-start.9
  27.0 11.0 %collective-permute-start.7 = (bf16[128,128]{1,0:T(8,128)(2,1)S(1)}, bf16[128,128]{1,0:T(8,128)(2,1)S(1)}, u32[]{:S(2)}, u32[]{:S(2)}) collective-permute-start(bf16[128,128]{1,0:T(8,128)(2,1)S(1)} %get-tuple-element.43), channel_id=1, source_target_pairs={{0,10},{1,11},{2,8},{3,9},{4,14},{5,15},{6,12},{7,13},{8,2},{9,3},... | collective-permute-start | bytes 98312 | tf_op jit(solution)/shard_map/ppermute | solution.py:264
  28.3 9.7 %collective-permute-start.8 = (bf16[128,128]{1,0:T(8,128)(2,1)S(1)}, bf16[128,128]{1,0:T(8,128)(2,1)S(1)}, u32[]{:S(2)}, u32[]{:S(2)}) collective-permute-start(bf16[128,128]{1,0:T(8,128)(2,1)S(1)} %get-tuple-element.44), channel_id=1, source_target_pairs={{0,12},{1,13},{2,14},{3,15},{4,8},{5,9},{6,10},{7,11},{8,4},{9,5},... | collective-permute-start | bytes 98312 | tf_op jit(solution)/shard_map/ppermute | solution.py:264
  31.9 6.7 %collective-permute-start.9 = (bf16[128,128]{1,0:T(8,128)(2,1)S(1)}, bf16[128,128]{1,0:T(8,128)(2,1)S(1)}, u32[]{:S(2)}, u32[]{:S(2)}) collective-permute-start(bf16[128,128]{1,0:T(8,128)(2,1)S(1)} %get-tuple-element.45), channel_id=1, source_target_pairs={{0,14},{1,15},{2,12},{3,13},{4,10},{5,11},{6,8},{7,9},{8,6},{9,7},... | collective-permute-start | bytes 98312 | tf_op jit(solution)/shard_map/ppermute | solution.py:264
  38.6 2.3 %copy-start.5 = (s32[1,8,16]{2,1,0:T(8,128)S(1)}, s32[1,8,16]{2,1,0:T(8,128)}, u32[]{:S(2)}) copy-start(s32[1,8,16]{2,1,0:T(8,128)} %cnt_ref.1) | copy-start | bytes 1540
  38.6 2.3 %collective-permute-start.10 = (bf16[8,384,128]{2,1,0:T(8,128)(2,1)S(1)}, bf16[8,384,128]{2,1,0:T(8,128)(2,1)S(1)}, u32[]{:S(2)}, u32[]{:S(2)}) collective-permute-start(bf16[8,384,128]{2,1,0:T(8,128)(2,1)S(1)} %all-to-all-done.refs_0_.refs_8_), channel_id=1, source_target_pairs={{0,1},{1,0},{2,3},{3,2},{4,5},{5,4},{6,7},{7,6},{8,9},{9,8},{10,11... | collective-permute-start | bytes 2359304 | tf_op jit(solution)/shard_map/ppermute | solution.py:264
  38.6 9.3 %collective-permute-start.11 = (bf16[1,128,1024]{2,1,0:T(8,128)(2,1)S(1)}, bf16[1,128,1024]{2,1,0:T(8,128)(2,1)S(1)}, u32[]{:S(2)}, u32[]{:S(2)}) collective-permute-start(bf16[1,128,1024]{2,1,0:T(8,128)(2,1)S(1)} %copy-done.8), channel_id=1, source_target_pairs={{0,2},{1,3},{2,0},{3,1},{4,6},{5,7},{6,4},{7,5},{8,10},{9,11},{10,... | collective-permute-start | bytes 786440 | tf_op jit(solution)/shard_map/ppermute | solution.py:264
  44.4 12.9 %all-to-all-start.1 = ((bf16[8,128,128]{2,1,0:T(8,128)(2,1)}), bf16[8,128,128]{2,1,0:T(8,128)(2,1)S(1)}, u32[]{:S(2)}, u32[]{:S(2)}) async-start(bf16[8,128,128]{2,1,0:T(8,128)(2,1)} %get-tuple-element.47), calls=%async_computation.1 | async-start | bytes 524288 | tf_op jit(solution)/shard_map/all_to_all | solution.py:312
  47.9 6.2 %collective-permute-start.12 = (bf16[1,128,1024]{2,1,0:T(8,128)(2,1)S(1)}, bf16[1,128,1024]{2,1,0:T(8,128)(2,1)S(1)}, u32[]{:S(2)}, u32[]{:S(2)}) collective-permute-start(bf16[1,128,1024]{2,1,0:T(8,128)(2,1)S(1)} %collective-permute-done.11.refs_3_), channel_id=1, source_target_pairs={{0,1},{1,0},{2,3},{3,2},{4,5},{5,4},{6,7},{7,6},{8,9},{9,8},{10,11... | collective-permute-start | bytes 786440 | tf_op jit(solution)/shard_map/ppermute | solution.py:264
  52.2 0.8 copy-start.6
  53.0 0.7 copy-start.13
  53.7 7.8 %copy-start.7 = (bf16[8,256,128]{2,1,0:T(8,128)(2,1)S(1)}, bf16[8,256,128]{2,1,0:T(8,128)(2,1)}, u32[]{:S(2)}) copy-start(bf16[8,256,128]{2,1,0:T(8,128)(2,1)} %copy-done.6) | copy-start | bytes 1572868
  53.7 7.8 %collective-permute-start.13 = (bf16[8,256,128]{2,1,0:T(8,128)(2,1)}, bf16[8,256,128]{2,1,0:T(8,128)(2,1)S(1)}, u32[]{:S(2)}, u32[]{:S(2)}) collective-permute-start(bf16[8,256,128]{2,1,0:T(8,128)(2,1)} %get-tuple-element.60), channel_id=1, source_target_pairs={{0,1},{1,0},{2,3},{3,2},{4,5},{5,4},{6,7},{7,6},{8,9},{9,8},{10,11... | collective-permute-start | bytes 1572872 | tf_op jit(solution)/shard_map/ppermute | solution.py:264
  54.1 0.7 copy-start.11
  57.3 2.8 %copy-start.1 = (bf16[8,128,128]{2,1,0:T(8,128)(2,1)}, bf16[8,128,128]{2,1,0:T(8,128)(2,1)S(1)}, u32[]{:S(2)}) copy-start(bf16[8,128,128]{2,1,0:T(8,128)(2,1)S(1)} %all-to-all-done.1.back_ref.mine_ref) | copy-start | bytes 786436
  57.3 1.5 %collective-permute-start.14 = (bf16[8,128,128]{2,1,0:T(8,128)(2,1)S(1)}, bf16[8,128,128]{2,1,0:T(8,128)(2,1)S(1)}, u32[]{:S(2)}, u32[]{:S(2)}) collective-permute-start(bf16[8,128,128]{2,1,0:T(8,128)(2,1)S(1)} %all-to-all-done.1.back_ref.mine_ref), channel_id=1, source_target_pairs={{0,1},{1,0},{2,3},{3,2},{4,5},{5,4},{6,7},{7,6},{8,9},{9,8},{10,11... | collective-permute-start | bytes 786440 | tf_op jit(solution)/shard_map/ppermute | solution.py:264
  60.1 7.1 %collective-permute-start.15 = (bf16[256,256]{1,0:T(8,128)(2,1)}, bf16[256,256]{1,0:T(8,128)(2,1)S(1)}, u32[]{:S(2)}, u32[]{:S(2)}) collective-permute-start(bf16[256,256]{1,0:T(8,128)(2,1)} %get-tuple-element.65), channel_id=1, source_target_pairs={{0,2},{1,3},{2,0},{3,1},{4,6},{5,7},{6,4},{7,5},{8,10},{9,11},{10,... | collective-permute-start | bytes 393224 | tf_op jit(solution)/shard_map/ppermute | solution.py:264
  61.5 1.0 %copy-start.14 = (bf16[8,128,128]{2,1,0:T(8,128)(2,1)S(1)}, bf16[8,128,128]{2,1,0:T(8,128)(2,1)}, u32[]{:S(2)}) copy-start(bf16[8,128,128]{2,1,0:T(8,128)(2,1)} %copy-done.13) | copy-start | bytes 786436
  63.5 3.7 %copy-start.10 = (bf16[1,128,1024]{2,1,0:T(8,128)(2,1)S(1)}, bf16[1,128,1024]{2,1,0:T(8,128)(2,1)}, u32[]{:S(2)}) copy-start(bf16[1,128,1024]{2,1,0:T(8,128)(2,1)} %copy-done.9) | copy-start | bytes 786436
  63.5 3.7 %copy-start.12 = (bf16[1,128,1024]{2,1,0:T(8,128)(2,1)S(1)}, bf16[1,128,1024]{2,1,0:T(8,128)(2,1)}, u32[]{:S(2)}) copy-start(bf16[1,128,1024]{2,1,0:T(8,128)(2,1)} %copy-done.11) | copy-start | bytes 786436
  63.5 30.4 %all-to-all-start.2 = ((bf16[8,384,128]{2,1,0:T(8,128)(2,1)}), bf16[8,384,128]{2,1,0:T(8,128)(2,1)S(1)}, u32[]{:S(2)}, u32[]{:S(2)}) async-start(bf16[8,384,128]{2,1,0:T(8,128)(2,1)} %combine.1), calls=%async_computation.2 | async-start | bytes 1572864 | tf_op jit(solution)/shard_map/all_to_all | solution.py:312
  68.1 8.1 %collective-permute-start.16 = (bf16[128,1024]{1,0:T(8,128)(2,1)S(1)}, bf16[128,1024]{1,0:T(8,128)(2,1)S(1)}, u32[]{:S(2)}, u32[]{:S(2)}) collective-permute-start(bf16[128,1024]{1,0:T(8,128)(2,1)S(1)} %get-tuple-element.70), channel_id=1, source_target_pairs={{0,16},{16,0},{1,17},{17,1},{2,18},{18,2},{3,19},{19,3},{4,20},{20... | collective-permute-start | bytes 786440 | tf_op jit(solution)/shard_map/ppermute | solution.py:268
  76.3 10.5 %collective-permute-start.19 = (bf16[32,1024]{1,0:T(8,128)(2,1)S(1)}, bf16[32,1024]{1,0:T(8,128)(2,1)S(1)}, u32[]{:S(2)}, u32[]{:S(2)}) collective-permute-start(bf16[32,1024]{1,0:T(8,128)(2,1)S(1)} %get-tuple-element.74), channel_id=1, source_target_pairs={{0,12},{1,13},{2,14},{3,15},{4,8},{5,9},{6,10},{7,11},{8,4},{9,5},... | collective-permute-start | bytes 196616 | tf_op jit(solution)/shard_map/ppermute | solution.py:264
  79.8 13.4 %collective-permute-start.18 = (bf16[32,1024]{1,0:T(8,128)(2,1)S(1)}, bf16[32,1024]{1,0:T(8,128)(2,1)S(1)}, u32[]{:S(2)}, u32[]{:S(2)}) collective-permute-start(bf16[32,1024]{1,0:T(8,128)(2,1)S(1)} %get-tuple-element.75), channel_id=1, source_target_pairs={{0,8},{1,9},{2,10},{3,11},{4,12},{5,13},{6,14},{7,15},{8,0},{9,1},... | collective-permute-start | bytes 196616 | tf_op jit(solution)/shard_map/ppermute | solution.py:264
  79.8 13.4 %collective-permute-start.17 = (bf16[32,1024]{1,0:T(8,128)(2,1)S(1)}, bf16[32,1024]{1,0:T(8,128)(2,1)S(1)}, u32[]{:S(2)}, u32[]{:S(2)}) collective-permute-start(bf16[32,1024]{1,0:T(8,128)(2,1)S(1)} %get-tuple-element.73), channel_id=1, source_target_pairs={{0,4},{1,5},{2,6},{3,7},{4,0},{5,1},{6,2},{7,3},{8,12},{9,13},{10,... | collective-permute-start | bytes 196616 | tf_op jit(solution)/shard_map/ppermute | solution.py:264

commit v4 on v3

--- a/solution.py
+++ b/solution.py
@@ -214,18 +214,22 @@
             )
             * SCALE
         ).astype(BF16)
-    for r, ref in enumerate((near_ref, *far_refs)):
-        ref[:, :BLOCK, :] = (acc_ref[r, :, :BLOCK, :] * SCALE).astype(BF16)
-        ref[:, BLOCK:, :] = acc_ref[r, :, BLOCK:, :].astype(BF16)
+    near_ref[:, :BLOCK, :] = (acc_ref[0, :, :BLOCK, :] * SCALE).astype(BF16)
+    near_ref[:, BLOCK:, :] = acc_ref[0, :, BLOCK:, :].astype(BF16)
+    for r in range(1, group):
+        far_refs[2 * r - 2][...] = (acc_ref[r, :, :BLOCK, :] * SCALE).astype(BF16)
+        far_refs[2 * r - 1][...] = acc_ref[r, :, BLOCK:, :].astype(BF16)
 
 
 def combine_body(dq_ref, near_ref, *refs):
     *arrived_refs, send_ref = refs
     send_ref[:, :BLOCK, :] = dq_ref[...]
-    total = near_ref[...].astype(F32)
-    for ref in arrived_refs:
-        total += ref[...].astype(F32)
-    send_ref[:, BLOCK:, :] = total.astype(BF16)
+    for part in range(2):
+        rows = slice(part * BLOCK, (part + 1) * BLOCK)
+        total = near_ref[:, rows, :].astype(F32)
+        for ref in arrived_refs[part::2]:
+            total += ref[...].astype(F32)
+        send_ref[:, BLOCK + part * BLOCK : 2 * BLOCK + part * BLOCK, :] = total.astype(BF16)
 
 
 def feature_body(ids_ref, mine_ref, pair_ref, *out_refs):
@@ -284,7 +288,7 @@
         grad_weight_body,
         [shape((4 * 32, columns), F32), shape((4 * 32, columns))],
         [pltpu.VMEM((4, BLOCK, columns), BF16), pltpu.SemaphoreType.DMA((4,))],
-        n_vmem=2, n_hbm=4, vmem=16, flops=2**35, name="grad_weight",
+        n_vmem=2, n_hbm=4, vmem=16, flops=GW_FLOPS, name="grad_weight",
     )(features[0], ctx_swap(features[1], 2), *rows)
     total = (keep + dp_swap(send).astype(F32)).reshape(4, 32, columns)
     parts = [ctx_swap(total[zr].astype(BF16), 4 * zr) for zr in range(1, 4)]
@@ -292,6 +296,7 @@
 
 
 D_OUT_FLOPS = 2**32
+GW_FLOPS = 2**35
 
 
 def local(queries, keys, values, out_weight, out_grad, key_blocks, block_counts):
@@ -353,7 +358,7 @@
         back, same[1], cross[1] = together(back, same[1], cross[1])
     dq, near_kv, *far_kv = call(
         functools.partial(backward_body, group),
-        [tile, pair] + [pair] * (group - 1),
+        [tile, pair] + [tile] * (2 * group - 2),
         [
             tile_scratch, kv_scratch, tile_scratch, pltpu.VMEM(score, BF16), pltpu.VMEM(score, F32),
             pltpu.VMEM(score, BF16),
@@ -361,19 +366,17 @@
         ],
         n_smem=2, n_vmem=HEADS, n_hbm=group + 1, vmem=vmem, name="backward",
     )(ids, key_blocks, *pieces, own, *others, probs)
-    arrived = [ctx_swap(part, r + 1) for r, part in enumerate(far_kv)]
-    if small:
-        features = own_features(ids, back)
-    grads = exchange(
-        call(
-            combine_body, shape((HEADS, 3 * BLOCK, HEAD_SIZE)), n_vmem=group + 1,
-            vmem=vmem, flops=2**33, name="combine",
-        )(dq, near_kv, *arrived)
-    )
+    arrived = [ctx_swap(part, i // 2 + 1) for i, part in enumerate(far_kv)]
+    send = call(
+        combine_body, shape((HEADS, 3 * BLOCK, HEAD_SIZE)), n_vmem=2 * group, vmem=vmem,
+        name="combine",
+    )(dq, near_kv, *arrived)
+    back, send = together(back, send)
+    grads = exchange(send)
     tokens = shape((1, BLOCK, HEADS * HEAD_SIZE))
     grad_queries, grad_keys, grad_values = call(unpack_body, [tokens] * 3, n_vmem=1, name="unpack")(grads)
     if small:
-        grad_weight = reduce_weight(features, same + cross)
+        grad_weight = reduce_weight(own_features(ids, back), same + cross)
     else:
         grad_weight = lax.psum_scatter(
             dot(back.reshape(HEADS * HEAD_SIZE, BLOCK), out_grad[0], NN),

time: 95.5 us -> 92 us (0.963)
  local copies, waits for them, and re-layouts: 5.21 us -> 2.05 us
  Pallas kernels: 18.1 us -> 16.8 us
  waiting for transfers between devices: 33.7 us -> 34.8 us
    unnamed x33 -> x21, local copies, waits for them, and re-layouts: 4.03 us -> 0.87 us
    ppermute x18 -> x19, waiting for transfers between devices: 20.6 us -> 21.7 us  [ctx_swap(): return lax.ppermute(x, 'ctx', [(i, i ^ mask) for i in range(n)])]
    ppermute x18 -> x19, starting transfers between devices: 18.8 us -> 19 us  [ctx_swap(): return lax.ppermute(x, 'ctx', [(i, i ^ mask) for i in range(n)])]
  transfers between devices with their start and end apart: 23 -> 24, of which waited for: 11 -> 13; matrix products, arithmetic and copies ran while one was open for 1% -> 1% of each run, Pallas kernels for 18% -> 16%
where the time goes in v4:
time: 92 us; the launch traced here: 91.6 us
  starting transfers between devices  36.4 us (40%)
  waiting for transfers between devices  34.8 us (38%)
  Pallas kernels  16.8 us (18%)
  local copies, waits for them, and re-layouts  2.05 us (2%)
    ppermute x19, waiting for transfers between devices, ctx_swap(): return lax.ppermute(x, 'ctx', [(i, i ^ mask) for i in range(n)])  21.7 us
    ppermute x19, starting transfers between devices, ctx_swap(): return lax.ppermute(x, 'ctx', [(i, i ^ mask) for i in range(n)])  19 us
    all_to_all x3, starting transfers between devices, exchange(): return lax.all_to_all(x, 'ctx', 0, 0, tiled=True, axis_index_groups=peers)  12.9 us
    ppermute x2, waiting for transfers between devices, dp_swap(): return lax.ppermute(x, 'dp', [(0, 1), (1, 0)])  10.1 us
    ppermute x2, starting transfers between devices, dp_swap(): return lax.ppermute(x, 'dp', [(0, 1), (1, 0)])  4.45 us
    pallas_call x1, Pallas kernels, local(): call(functools.partial(forward_body, group), [tile, shape(score)], [kv_sc...  3.53 us
    pallas_call x1, Pallas kernels, local(): call(functools.partial(backward_body, group), [tile, pair] + [tile] * (2...  3.44 us
    pallas_call x1, Pallas kernels, local(): call(output_body, shape((1, BLOCK, columns)), n_smem=1, n_vmem=4, vmem=60...  3.04 us
  transfers between devices with their start and end apart: 24, of which 13 were waited for; matrix products, arithmetic and copies ran while one was open for 1% of the time, Pallas kernels for 16%

profile of v4, /device:TPU:0, one launch (start us, length us, event | category | flops | bytes accessed | tf_op | source)
XLA Modules:
  0.0 91.6 jit_solution(1640643124649354987)
XLA Ops:
  0.6 1.1 %constant_dynamic-slice_fusion = bf16[256,1024]{1,0:T(8,128)(2,1)S(1)} fusion(bf16[512,1024]{1,0:T(8,128)(2,1)} %refs_0_.3, s32[]{:T(128)S(6)} %select_n.16), kind=kLoop, calls=%fused_computation.2 | loop fusion | bytes 1048580 | tf_op jit(solution)/shard_map/dynamic_slice | solution.py:321
  1.7 3.0 %collective-permute-start.1 = (bf16[256,1024]{1,0:T(8,128)(2,1)S(1)}, bf16[256,1024]{1,0:T(8,128)(2,1)S(1)}, u32[]{:S(2)}, u32[]{:S(2)}) collective-permute-start(bf16[256,1024]{1,0:T(8,128)(2,1)S(1)} %constant_dynamic-slice_fusion), channel_id=1, source_target_pairs={{0,16},{16,0},{1,17},{17,1},{2,18},{18,2},{3,19},{19,3},{4,20},{20... | collective-permute-start | bytes 1572872 | tf_op jit(solution)/shard_map/ppermute | solution.py:272
  4.7 2.0 %pack.1 = bf16[8,384,128]{2,1,0:T(8,128)(2,1)} custom-call(bf16[1,128,1024]{2,1,0:T(8,128)(2,1)} %q_ref.1, bf16[1,128,1024]{2,1,0:T(8,128)(2,1)} %k_ref.1, bf16[1,128,1024]{2,1,0:T(8,128)(2,1)} %v_ref.1), custom_call_target="tpu_custom_call" | custom-call | flops 34359738368 | tf_op jit(solution)/shard_map/pack/pallas_call | solution.py:75
  6.7 0.0 copy-start.6
  6.7 0.0 copy-start
  6.7 6.0 %all-to-all-start = ((bf16[8,384,128]{2,1,0:T(8,128)(2,1)}), bf16[8,384,128]{2,1,0:T(8,128)(2,1)S(1)}, u32[]{:S(2)}, u32[]{:S(2)}) async-start(bf16[8,384,128]{2,1,0:T(8,128)(2,1)} %pack.1), calls=%async_computation | async-start | bytes 1572864 | tf_op jit(solution)/shard_map/all_to_all | solution.py:317
  12.7 4.0 %collective-permute-done.1.refs_1_ = bf16[256,1024]{1,0:T(8,128)(2,1)S(1)} collective-permute-done((bf16[256,1024]{1,0:T(8,128)(2,1)S(1)}, bf16[256,1024]{1,0:T(8,128)(2,1)S(1)}, u32[]{:S(2)}, u32[]{:S(2)}) %collective-permute-start.1) | collective-permute-done | bytes 524320 | tf_op jit(solution)/shard_map/ppermute | solution.py:272
  16.7 0.0 collective-permute-start.2
  16.7 0.5 collective-permute-start
  17.2 0.1 stack.28.ids_ref
  17.3 1.3 %collective-permute-done.2.refs_2_ = bf16[256,1024]{1,0:T(8,128)(2,1)S(1)} collective-permute-done((bf16[256,1024]{1,0:T(8,128)(2,1)S(1)}, bf16[256,1024]{1,0:T(8,128)(2,1)S(1)}, u32[]{:S(2)}, u32[]{:S(2)}) %collective-permute-start.2) | collective-permute-done | bytes 524320 | tf_op jit(solution)/shard_map/ppermute | solution.py:268
  18.6 1.3 %d_out.1 = (bf16[128,128]{1,0:T(8,128)(2,1)S(1)}, bf16[128,128]{1,0:T(8,128)(2,1)S(1)}, bf16[128,128]{1,0:T(8,128)(2,1)S(1)}, bf16[128,128]{1,0:T(8,128)(2,1)S(1...) custom-call(s32[7]{0:T(128)S(1)} %stack.28.ids_ref, ...), custom_call_target="tpu_custom_call" | custom-call | flops 4294967296 | tf_op jit(solution)/shard_map/d_out/pallas_call | solution.py:336
  19.9 0.0 copy-start.9
  19.9 1.8 %collective-permute-start.3 = (bf16[128,128]{1,0:T(8,128)(2,1)S(1)}, bf16[128,128]{1,0:T(8,128)(2,1)S(1)}, u32[]{:S(2)}, u32[]{:S(2)}) collective-permute-start(bf16[128,128]{1,0:T(8,128)(2,1)S(1)} %get-tuple-element.42), channel_id=1, source_target_pairs={{0,2},{1,3},{2,0},{3,1},{4,6},{5,7},{6,4},{7,5},{8,10},{9,11},{10,... | collective-permute-start | bytes 98312 | tf_op jit(solution)/shard_map/ppermute | solution.py:268
  21.7 1.6 %collective-permute-start.4 = (bf16[128,128]{1,0:T(8,128)(2,1)S(1)}, bf16[128,128]{1,0:T(8,128)(2,1)S(1)}, u32[]{:S(2)}, u32[]{:S(2)}) collective-permute-start(bf16[128,128]{1,0:T(8,128)(2,1)S(1)} %get-tuple-element.43), channel_id=1, source_target_pairs={{0,4},{1,5},{2,6},{3,7},{4,0},{5,1},{6,2},{7,3},{8,12},{9,13},{10,... | collective-permute-start | bytes 98312 | tf_op jit(solution)/shard_map/ppermute | solution.py:268
  23.3 0.1 collective-permute-start.5
  23.4 2.8 %collective-permute-start.6 = (bf16[128,128]{1,0:T(8,128)(2,1)S(1)}, bf16[128,128]{1,0:T(8,128)(2,1)S(1)}, u32[]{:S(2)}, u32[]{:S(2)}) collective-permute-start(bf16[128,128]{1,0:T(8,128)(2,1)S(1)} %get-tuple-element.45), channel_id=1, source_target_pairs={{0,8},{1,9},{2,10},{3,11},{4,12},{5,13},{6,14},{7,15},{8,0},{9,1},... | collective-permute-start | bytes 98312 | tf_op jit(solution)/shard_map/ppermute | solution.py:268
  26.3 0.7 copy-done.7
  27.0 1.3 %collective-permute-start.7 = (bf16[128,128]{1,0:T(8,128)(2,1)S(1)}, bf16[128,128]{1,0:T(8,128)(2,1)S(1)}, u32[]{:S(2)}, u32[]{:S(2)}) collective-permute-start(bf16[128,128]{1,0:T(8,128)(2,1)S(1)} %get-tuple-element.46), channel_id=1, source_target_pairs={{0,10},{1,11},{2,8},{3,9},{4,14},{5,15},{6,12},{7,13},{8,2},{9,3},... | collective-permute-start | bytes 98312 | tf_op jit(solution)/shard_map/ppermute | solution.py:268
  28.3 0.0 collective-permute-done.3.refs_1_
  28.3 3.6 %collective-permute-start.8 = (bf16[128,128]{1,0:T(8,128)(2,1)S(1)}, bf16[128,128]{1,0:T(8,128)(2,1)S(1)}, u32[]{:S(2)}, u32[]{:S(2)}) collective-permute-start(bf16[128,128]{1,0:T(8,128)(2,1)S(1)} %get-tuple-element.47), channel_id=1, source_target_pairs={{0,12},{1,13},{2,14},{3,15},{4,8},{5,9},{6,10},{7,11},{8,4},{9,5},... | collective-permute-start | bytes 98312 | tf_op jit(solution)/shard_map/ppermute | solution.py:268
  31.9 0.0 collective-permute-done.4.refs_2_
  31.9 0.0 collective-permute-start.9
  31.9 0.0 collective-permute-done.5.refs_3_
  31.9 5.0 %collective-permute-done.6.refs_4_ = bf16[128,128]{1,0:T(8,128)(2,1)S(1)} collective-permute-done((bf16[128,128]{1,0:T(8,128)(2,1)S(1)}, bf16[128,128]{1,0:T(8,128)(2,1)S(1)}, u32[]{:S(2)}, u32[]{:S(2)}) %collective-permute-start.6) | collective-permute-done | bytes 32800 | tf_op jit(solution)/shard_map/ppermute | solution.py:268
  36.9 1.1 %collective-permute-done.7.refs_5_ = bf16[128,128]{1,0:T(8,128)(2,1)S(1)} collective-permute-done((bf16[128,128]{1,0:T(8,128)(2,1)S(1)}, bf16[128,128]{1,0:T(8,128)(2,1)S(1)}, u32[]{:S(2)}, u32[]{:S(2)}) %collective-permute-start.7) | collective-permute-done | bytes 32800 | tf_op jit(solution)/shard_map/ppermute | solution.py:268
  38.0 0.6 collective-permute-done.9.refs_7_
  38.6 0.0 all-to-all-done.refs_0_.refs_8_
  38.6 0.0 collective-permute-start.10
  38.6 0.6 collective-permute-start.11
  39.2 0.1 copy.12.kb_ref
  39.3 1.6 %collective-permute-done.10.refs_1_.refs_9_ = bf16[8,384,128]{2,1,0:T(8,128)(2,1)S(1)} collective-permute-done((bf16[8,384,128]{2,1,0:T(8,128)(2,1)S(1)}, bf16[8,384,128]{2,1,0:T(8,128)(2,1)S(1)}, u32[]{:S(2)}, u32[]{:S(2)}) %collective-permute-start.10) | collective-permute-done | bytes 786464 | tf_op jit(solution)/shard_map/ppermute | solution.py:268
  40.9 3.5 %forward.1 = (bf16[8,128,128]{2,1,0:T(8,128)(2,1)}, bf16[8,128,256]{2,1,0:T(8,128)(2,1)S(1)}) custom-call(s32[7]{0:T(128)S(1)} %stack.28.ids_ref, s32[1,8,16,2]{3,2,1,0:T(8,128)S(1)} %copy.12.kb_ref, s32[1,8,16]{2,1,0:T(8,128)S(1)} %copy-done.5, bf16[8,384,128]{2,1,0:T(8,128)(2,1)S(1)} %all-to-all-done.refs_0_.refs_8_, ...), custom_call_target="tpu_custom_call" | custom-call | tf_op jit(solution)/shard_map/forward/pallas_call | solution.py:348
  44.4 3.4 %all-to-all-start.1 = ((bf16[8,128,128]{2,1,0:T(8,128)(2,1)}), bf16[8,128,128]{2,1,0:T(8,128)(2,1)S(1)}, u32[]{:S(2)}, u32[]{:S(2)}) async-start(bf16[8,128,128]{2,1,0:T(8,128)(2,1)} %get-tuple-element.50), calls=%async_computation.1 | async-start | bytes 524288 | tf_op jit(solution)/shard_map/all_to_all | solution.py:317
  47.9 3.4 %backward.1 = (bf16[8,128,128]{2,1,0:T(8,128)(2,1)S(1)}, bf16[8,256,128]{2,1,0:T(8,128)(2,1)S(1)}, bf16[8,128,128]{2,1,0:T(8,128)(2,1)S(1)}, bf16[8,128,128]{2,1,0:T(8,128)(2,1)S(1)}) custom-call(s32[7]{0:T(128)S(1)} %stack.28.ids_ref, s32[1,8,16,2]{3,2,1,0:T(8,128)S(1)} %copy.12.kb_ref, bf16[128,128]{1,0:T(8,128)(2,1)S(1)} %get-tuple-element.52.refs_0_, ...), custom_call_target="tpu_custom_call" | custom-call | tf_op jit(solution)/shard_map/backward/pallas_call | solution.py:359
  51.3 0.2 collective-permute-start.13
  51.5 0.4 collective-permute-start.14
  51.9 0.0 collective-permute-done.11.refs_3_
  51.9 0.1 collective-permute-start.12
  52.0 0.9 collective-permute-done.13.refs_0_
  52.9 0.4 collective-permute-done.14.refs_1_
  53.3 1.0 %combine.1 = bf16[8,384,128]{2,1,0:T(8,128)(2,1)} custom-call(bf16[8,128,128]{2,1,0:T(8,128)(2,1)S(1)} %get-tuple-element.61.dq_ref, bf16[8,256,128]{2,1,0:T(8,128)(2,1)S(1)} %get-tuple-element.62.near_ref, bf16[8,128,128]{2,1,0:T(8,128)(2,1)S(1)} %collective-permute-done.13.refs_0_, bf16[8,128,128]{2,1,0:T(8,128)(2,1)S(1)} %collective-permute-done.14.refs_1_), custom_call_target="tpu_custom_call" | custom-call | tf_op jit(solution)/shard_map/combine/pallas_call | solution.py:370
  54.3 0.0 collective-permute-done.12.refs_5_
  54.3 3.0 %all-to-all-done.1.back_ref.mine_ref = bf16[8,128,128]{2,1,0:T(8,128)(2,1)S(1)} async-done(((bf16[8,128,128]{2,1,0:T(8,128)(2,1)}), bf16[8,128,128]{2,1,0:T(8,128)(2,1)S(1)}, u32[]{:S(2)}, u32[]{:S(2)}) %all-to-all-start.1) | async-done | bytes 262176 | tf_op jit(solution)/shard_map/all_to_all | solution.py:317
  57.3 0.0 collective-permute-start.15
  57.3 1.5 %collective-permute-done.15.pair_ref = bf16[8,128,128]{2,1,0:T(8,128)(2,1)S(1)} collective-permute-done((bf16[8,128,128]{2,1,0:T(8,128)(2,1)S(1)}, bf16[8,128,128]{2,1,0:T(8,128)(2,1)S(1)}, u32[]{:S(2)}, u32[]{:S(2)}) %collective-permute-start.15) | collective-permute-done | bytes 262176 | tf_op jit(solution)/shard_map/ppermute | solution.py:268
  58.9 0.6 features.1
  59.5 0.0 copy-start.8
  59.5 1.5 %collective-permute-start.16 = (bf16[256,256]{1,0:T(8,128)(2,1)S(1)}, bf16[256,256]{1,0:T(8,128)(2,1)S(1)}, u32[]{:S(2)}, u32[]{:S(2)}) collective-permute-start(bf16[256,256]{1,0:T(8,128)(2,1)S(1)} %get-tuple-element.71), channel_id=1, source_target_pairs={{0,2},{1,3},{2,0},{3,1},{4,6},{5,7},{6,4},{7,5},{8,10},{9,11},{10,... | collective-permute-start | bytes 393224 | tf_op jit(solution)/shard_map/ppermute | solution.py:268
  61.0 3.5 %all-to-all-start.2 = ((bf16[8,384,128]{2,1,0:T(8,128)(2,1)}), bf16[8,384,128]{2,1,0:T(8,128)(2,1)S(1)}, u32[]{:S(2)}, u32[]{:S(2)}) async-start(bf16[8,384,128]{2,1,0:T(8,128)(2,1)} %combine.1), calls=%async_computation.2 | async-start | bytes 1572864 | tf_op jit(solution)/shard_map/all_to_all | solution.py:317
  64.5 0.6 collective-permute-done.16.refs_1_
  65.1 0.8 grad_weight.1
  65.9 1.4 %collective-permute-start.17 = (bf16[128,1024]{1,0:T(8,128)(2,1)S(1)}, bf16[128,1024]{1,0:T(8,128)(2,1)S(1)}, u32[]{:S(2)}, u32[]{:S(2)}) collective-permute-start(bf16[128,1024]{1,0:T(8,128)(2,1)S(1)} %get-tuple-element.76), channel_id=1, source_target_pairs={{0,16},{16,0},{1,17},{17,1},{2,18},{18,2},{3,19},{19,3},{4,20},{20... | collective-permute-start | bytes 786440 | tf_op jit(solution)/shard_map/ppermute | solution.py:272
  67.4 6.1 %collective-permute-done.17 = bf16[128,1024]{1,0:T(8,128)(2,1)S(1)} collective-permute-done((bf16[128,1024]{1,0:T(8,128)(2,1)S(1)}, bf16[128,1024]{1,0:T(8,128)(2,1)S(1)}, u32[]{:S(2)}, u32[]{:S(2)}) %collective-permute-start.17) | collective-permute-done | bytes 262176 | tf_op jit(solution)/shard_map/ppermute | solution.py:272
  73.5 0.1 fusion
  73.6 1.7 %collective-permute-start.18 = (bf16[32,1024]{1,0:T(8,128)(2,1)S(1)}, bf16[32,1024]{1,0:T(8,128)(2,1)S(1)}, u32[]{:S(2)}, u32[]{:S(2)}) collective-permute-start(bf16[32,1024]{1,0:T(8,128)(2,1)S(1)} %get-tuple-element.79), channel_id=1, source_target_pairs={{0,4},{1,5},{2,6},{3,7},{4,0},{5,1},{6,2},{7,3},{8,12},{9,13},{10,... | collective-permute-start | bytes 196616 | tf_op jit(solution)/shard_map/ppermute | solution.py:268
  75.3 2.4 %collective-permute-start.19 = (bf16[32,1024]{1,0:T(8,128)(2,1)S(1)}, bf16[32,1024]{1,0:T(8,128)(2,1)S(1)}, u32[]{:S(2)}, u32[]{:S(2)}) collective-permute-start(bf16[32,1024]{1,0:T(8,128)(2,1)S(1)} %get-tuple-element.81), channel_id=1, source_target_pairs={{0,8},{1,9},{2,10},{3,11},{4,12},{5,13},{6,14},{7,15},{8,0},{9,1},... | collective-permute-start | bytes 196616 | tf_op jit(solution)/shard_map/ppermute | solution.py:268
  77.7 0.4 collective-permute-start.20
  78.1 3.0 %output.1 = bf16[1,128,1024]{2,1,0:T(8,128)(2,1)} custom-call(s32[7]{0:T(128)} %copy-done.4, bf16[8,128,128]{2,1,0:T(8,128)(2,1)} %copy-done.1, bf16[512,1024]{1,0:T(8,128)(2,1)} %refs_0_.3, bf16[256,1024]{1,0:T(8,128)(2,1)} %copy-done.2, bf16[256,1024]{1,0:T(8,128)(2,1)} %copy-done.3), custom_call_target="tpu_custom_call" | custom-call | tf_op jit(solution)/shard_map/output/pallas_call | solution.py:385
  81.1 0.0 collective-permute-done.18
  81.1 8.7 %collective-permute-done.19 = bf16[32,1024]{1,0:T(8,128)(2,1)S(1)} collective-permute-done((bf16[32,1024]{1,0:T(8,128)(2,1)S(1)}, bf16[32,1024]{1,0:T(8,128)(2,1)S(1)}, u32[]{:S(2)}, u32[]{:S(2)}) %collective-permute-start.19) | collective-permute-done | bytes 65568 | tf_op jit(solution)/shard_map/ppermute | solution.py:268
  89.8 0.0 collective-permute-done.20
  89.8 0.7 slice_add_fusion
  90.5 1.1 %unpack.1 = (bf16[1,128,1024]{2,1,0:T(8,128)(2,1)}, bf16[1,128,1024]{2,1,0:T(8,128)(2,1)}, bf16[1,128,1024]{2,1,0:T(8,128)(2,1)}) custom-call(bf16[8,384,128]{2,1,0:T(8,128)(2,1)S(1)} %all-to-all-done.2.recv_ref), custom_call_target="tpu_custom_call" | custom-call | tf_op jit(solution)/shard_map/unpack/pallas_call | solution.py:377
  (19 shorter events, 0.1 us)
Async XLA Ops:
  1.7 14.9 %collective-permute-start.1 = (bf16[256,1024]{1,0:T(8,128)(2,1)S(1)}, bf16[256,1024]{1,0:T(8,128)(2,1)S(1)}, u32[]{:S(2)}, u32[]{:S(2)}) collective-permute-start(bf16[256,1024]{1,0:T(8,128)(2,1)S(1)} %constant_dynamic-slice_fusion), channel_id=1, source_target_pairs={{0,16},{16,0},{1,17},{17,1},{2,18},{18,2},{3,19},{19,3},{4,20},{20... | collective-permute-start | bytes 1572872 | tf_op jit(solution)/shard_map/ppermute | solution.py:272
  6.7 10.0 %copy-start.6 = (bf16[1,128,1024]{2,1,0:T(8,128)(2,1)S(1)}, bf16[1,128,1024]{2,1,0:T(8,128)(2,1)}, u32[]{:S(2)}) copy-start(bf16[1,128,1024]{2,1,0:T(8,128)(2,1)} %refs_2_.1) | copy-start | bytes 786436
  6.7 11.9 %copy-start = (bf16[512,1024]{1,0:T(8,128)(2,1)S(1)}, bf16[512,1024]{1,0:T(8,128)(2,1)}, u32[]{:S(2)}) copy-start(bf16[512,1024]{1,0:T(8,128)(2,1)} %refs_0_.3) | copy-start | bytes 3145732
  6.7 31.9 %all-to-all-start = ((bf16[8,384,128]{2,1,0:T(8,128)(2,1)}), bf16[8,384,128]{2,1,0:T(8,128)(2,1)S(1)}, u32[]{:S(2)}, u32[]{:S(2)}) async-start(bf16[8,384,128]{2,1,0:T(8,128)(2,1)} %pack.1), calls=%async_computation | async-start | bytes 1572864 | tf_op jit(solution)/shard_map/all_to_all | solution.py:317
  16.6 3.2 %copy-start.2 = (bf16[256,1024]{1,0:T(8,128)(2,1)}, bf16[256,1024]{1,0:T(8,128)(2,1)S(1)}, u32[]{:S(2)}) copy-start(bf16[256,1024]{1,0:T(8,128)(2,1)S(1)} %collective-permute-done.1.refs_1_) | copy-start | bytes 1572868
  16.7 1.9 %collective-permute-start.2 = (bf16[256,1024]{1,0:T(8,128)(2,1)S(1)}, bf16[256,1024]{1,0:T(8,128)(2,1)S(1)}, u32[]{:S(2)}, u32[]{:S(2)}) collective-permute-start(bf16[256,1024]{1,0:T(8,128)(2,1)S(1)} %collective-permute-done.1.refs_1_), channel_id=1, source_target_pairs={{0,1},{1,0},{2,3},{3,2},{4,5},{5,4},{6,7},{7,6},{8,9},{9,8},{10,11... | collective-permute-start | bytes 1572872 | tf_op jit(solution)/shard_map/ppermute | solution.py:268
  16.7 9.6 %collective-permute-start = (bf16[1,128,1024]{2,1,0:T(8,128)(2,1)S(1)}, bf16[1,128,1024]{2,1,0:T(8,128)(2,1)S(1)}, u32[]{:S(2)}, u32[]{:S(2)}) collective-permute-start(bf16[1,128,1024]{2,1,0:T(8,128)(2,1)S(1)} %copy-done.6), channel_id=1, source_target_pairs={{0,1},{1,0},{2,3},{3,2},{4,5},{5,4},{6,7},{7,6},{8,9},{9,8},{10,11... | collective-permute-start | bytes 786440 | tf_op jit(solution)/shard_map/ppermute | solution.py:268
  17.2 41.6 %copy-start.4 = (s32[7]{0:T(128)}, s32[7]{0:T(128)S(1)}, u32[]{:S(2)}) copy-start(s32[7]{0:T(128)S(1)} %stack.28.ids_ref) | copy-start | bytes 88
  18.6 1.3 %copy-start.3 = (bf16[256,1024]{1,0:T(8,128)(2,1)}, bf16[256,1024]{1,0:T(8,128)(2,1)S(1)}, u32[]{:S(2)}) copy-start(bf16[256,1024]{1,0:T(8,128)(2,1)S(1)} %collective-permute-done.2.refs_2_) | copy-start | bytes 1572868
  19.9 19.3 %copy-start.9 = (s32[1,8,16,2]{2,3,1,0:T(2,128)S(1)}, s32[1,8,16,2]{2,3,1,0:T(2,128)}, u32[]{:S(2)}) copy-start(s32[1,8,16,2]{2,3,1,0:T(2,128)} %param.12) | copy-start | bytes 3076
  19.9 8.4 %collective-permute-start.3 = (bf16[128,128]{1,0:T(8,128)(2,1)S(1)}, bf16[128,128]{1,0:T(8,128)(2,1)S(1)}, u32[]{:S(2)}, u32[]{:S(2)}) collective-permute-start(bf16[128,128]{1,0:T(8,128)(2,1)S(1)} %get-tuple-element.42), channel_id=1, source_target_pairs={{0,2},{1,3},{2,0},{3,1},{4,6},{5,7},{6,4},{7,5},{8,10},{9,11},{10,... | collective-permute-start | bytes 98312 | tf_op jit(solution)/shard_map/ppermute | solution.py:268
  21.7 10.2 %collective-permute-start.4 = (bf16[128,128]{1,0:T(8,128)(2,1)S(1)}, bf16[128,128]{1,0:T(8,128)(2,1)S(1)}, u32[]{:S(2)}, u32[]{:S(2)}) collective-permute-start(bf16[128,128]{1,0:T(8,128)(2,1)S(1)} %get-tuple-element.43), channel_id=1, source_target_pairs={{0,4},{1,5},{2,6},{3,7},{4,0},{5,1},{6,2},{7,3},{8,12},{9,13},{10,... | collective-permute-start | bytes 98312 | tf_op jit(solution)/shard_map/ppermute | solution.py:268
  23.3 8.6 %collective-permute-start.5 = (bf16[128,128]{1,0:T(8,128)(2,1)S(1)}, bf16[128,128]{1,0:T(8,128)(2,1)S(1)}, u32[]{:S(2)}, u32[]{:S(2)}) collective-permute-start(bf16[128,128]{1,0:T(8,128)(2,1)S(1)} %get-tuple-element.44), channel_id=1, source_target_pairs={{0,6},{1,7},{2,4},{3,5},{4,2},{5,3},{6,0},{7,1},{8,14},{9,15},{10,... | collective-permute-start | bytes 98312 | tf_op jit(solution)/shard_map/ppermute | solution.py:268
  23.4 13.4 %collective-permute-start.6 = (bf16[128,128]{1,0:T(8,128)(2,1)S(1)}, bf16[128,128]{1,0:T(8,128)(2,1)S(1)}, u32[]{:S(2)}, u32[]{:S(2)}) collective-permute-start(bf16[128,128]{1,0:T(8,128)(2,1)S(1)} %get-tuple-element.45), channel_id=1, source_target_pairs={{0,8},{1,9},{2,10},{3,11},{4,12},{5,13},{6,14},{7,15},{8,0},{9,1},... | collective-permute-start | bytes 98312 | tf_op jit(solution)/shard_map/ppermute | solution.py:268
  26.3 0.7 copy-start.7
  27.0 11.0 %collective-permute-start.7 = (bf16[128,128]{1,0:T(8,128)(2,1)S(1)}, bf16[128,128]{1,0:T(8,128)(2,1)S(1)}, u32[]{:S(2)}, u32[]{:S(2)}) collective-permute-start(bf16[128,128]{1,0:T(8,128)(2,1)S(1)} %get-tuple-element.46), channel_id=1, source_target_pairs={{0,10},{1,11},{2,8},{3,9},{4,14},{5,15},{6,12},{7,13},{8,2},{9,3},... | collective-permute-start | bytes 98312 | tf_op jit(solution)/shard_map/ppermute | solution.py:268
  28.3 9.7 %collective-permute-start.8 = (bf16[128,128]{1,0:T(8,128)(2,1)S(1)}, bf16[128,128]{1,0:T(8,128)(2,1)S(1)}, u32[]{:S(2)}, u32[]{:S(2)}) collective-permute-start(bf16[128,128]{1,0:T(8,128)(2,1)S(1)} %get-tuple-element.47), channel_id=1, source_target_pairs={{0,12},{1,13},{2,14},{3,15},{4,8},{5,9},{6,10},{7,11},{8,4},{9,5},... | collective-permute-start | bytes 98312 | tf_op jit(solution)/shard_map/ppermute | solution.py:268
  31.9 6.7 %collective-permute-start.9 = (bf16[128,128]{1,0:T(8,128)(2,1)S(1)}, bf16[128,128]{1,0:T(8,128)(2,1)S(1)}, u32[]{:S(2)}, u32[]{:S(2)}) collective-permute-start(bf16[128,128]{1,0:T(8,128)(2,1)S(1)} %get-tuple-element.48), channel_id=1, source_target_pairs={{0,14},{1,15},{2,12},{3,13},{4,10},{5,11},{6,8},{7,9},{8,6},{9,7},... | collective-permute-start | bytes 98312 | tf_op jit(solution)/shard_map/ppermute | solution.py:268
  38.6 2.3 %copy-start.5 = (s32[1,8,16]{2,1,0:T(8,128)S(1)}, s32[1,8,16]{2,1,0:T(8,128)}, u32[]{:S(2)}) copy-start(s32[1,8,16]{2,1,0:T(8,128)} %cnt_ref.1) | copy-start | bytes 1540
  38.6 2.3 %collective-permute-start.10 = (bf16[8,384,128]{2,1,0:T(8,128)(2,1)S(1)}, bf16[8,384,128]{2,1,0:T(8,128)(2,1)S(1)}, u32[]{:S(2)}, u32[]{:S(2)}) collective-permute-start(bf16[8,384,128]{2,1,0:T(8,128)(2,1)S(1)} %all-to-all-done.refs_0_.refs_8_), channel_id=1, source_target_pairs={{0,1},{1,0},{2,3},{3,2},{4,5},{5,4},{6,7},{7,6},{8,9},{9,8},{10,11... | collective-permute-start | bytes 2359304 | tf_op jit(solution)/shard_map/ppermute | solution.py:268
  38.6 13.3 %collective-permute-start.11 = (bf16[1,128,1024]{2,1,0:T(8,128)(2,1)S(1)}, bf16[1,128,1024]{2,1,0:T(8,128)(2,1)S(1)}, u32[]{:S(2)}, u32[]{:S(2)}) collective-permute-start(bf16[1,128,1024]{2,1,0:T(8,128)(2,1)S(1)} %copy-done.6), channel_id=1, source_target_pairs={{0,2},{1,3},{2,0},{3,1},{4,6},{5,7},{6,4},{7,5},{8,10},{9,11},{10,... | collective-permute-start | bytes 786440 | tf_op jit(solution)/shard_map/ppermute | solution.py:268
  44.4 12.9 %all-to-all-start.1 = ((bf16[8,128,128]{2,1,0:T(8,128)(2,1)}), bf16[8,128,128]{2,1,0:T(8,128)(2,1)S(1)}, u32[]{:S(2)}, u32[]{:S(2)}) async-start(bf16[8,128,128]{2,1,0:T(8,128)(2,1)} %get-tuple-element.50), calls=%async_computation.1 | async-start | bytes 524288 | tf_op jit(solution)/shard_map/all_to_all | solution.py:317
  51.3 1.6 %collective-permute-start.13 = (bf16[8,128,128]{2,1,0:T(8,128)(2,1)S(1)}, bf16[8,128,128]{2,1,0:T(8,128)(2,1)S(1)}, u32[]{:S(2)}, u32[]{:S(2)}) collective-permute-start(bf16[8,128,128]{2,1,0:T(8,128)(2,1)S(1)} %get-tuple-element.63), channel_id=1, source_target_pairs={{0,1},{1,0},{2,3},{3,2},{4,5},{5,4},{6,7},{7,6},{8,9},{9,8},{10,11... | collective-permute-start | bytes 786440 | tf_op jit(solution)/shard_map/ppermute | solution.py:268
  51.5 1.8 %collective-permute-start.14 = (bf16[8,128,128]{2,1,0:T(8,128)(2,1)S(1)}, bf16[8,128,128]{2,1,0:T(8,128)(2,1)S(1)}, u32[]{:S(2)}, u32[]{:S(2)}) collective-permute-start(bf16[8,128,128]{2,1,0:T(8,128)(2,1)S(1)} %get-tuple-element.64), channel_id=1, source_target_pairs={{0,1},{1,0},{2,3},{3,2},{4,5},{5,4},{6,7},{7,6},{8,9},{9,8},{10,11... | collective-permute-start | bytes 786440 | tf_op jit(solution)/shard_map/ppermute | solution.py:268
  51.9 2.4 %collective-permute-start.12 = (bf16[1,128,1024]{2,1,0:T(8,128)(2,1)S(1)}, bf16[1,128,1024]{2,1,0:T(8,128)(2,1)S(1)}, u32[]{:S(2)}, u32[]{:S(2)}) collective-permute-start(bf16[1,128,1024]{2,1,0:T(8,128)(2,1)S(1)} %collective-permute-done.11.refs_3_), channel_id=1, source_target_pairs={{0,1},{1,0},{2,3},{3,2},{4,5},{5,4},{6,7},{7,6},{8,9},{9,8},{10,11... | collective-permute-start | bytes 786440 | tf_op jit(solution)/shard_map/ppermute | solution.py:268
  57.3 2.2 %copy-start.1 = (bf16[8,128,128]{2,1,0:T(8,128)(2,1)}, bf16[8,128,128]{2,1,0:T(8,128)(2,1)S(1)}, u32[]{:S(2)}) copy-start(bf16[8,128,128]{2,1,0:T(8,128)(2,1)S(1)} %all-to-all-done.1.back_ref.mine_ref) | copy-start | bytes 786436
  57.3 1.5 %collective-permute-start.15 = (bf16[8,128,128]{2,1,0:T(8,128)(2,1)S(1)}, bf16[8,128,128]{2,1,0:T(8,128)(2,1)S(1)}, u32[]{:S(2)}, u32[]{:S(2)}) collective-permute-start(bf16[8,128,128]{2,1,0:T(8,128)(2,1)S(1)} %all-to-all-done.1.back_ref.mine_ref), channel_id=1, source_target_pairs={{0,1},{1,0},{2,3},{3,2},{4,5},{5,4},{6,7},{7,6},{8,9},{9,8},{10,11... | collective-permute-start | bytes 786440 | tf_op jit(solution)/shard_map/ppermute | solution.py:268
  59.5 5.6 %copy-start.8 = (bf16[1,128,1024]{2,1,0:T(8,128)(2,1)S(1)}, bf16[1,128,1024]{2,1,0:T(8,128)(2,1)}, u32[]{:S(2)}) copy-start(bf16[1,128,1024]{2,1,0:T(8,128)(2,1)} %copy-done.7) | copy-start | bytes 786436
  59.5 5.6 %collective-permute-start.16 = (bf16[256,256]{1,0:T(8,128)(2,1)S(1)}, bf16[256,256]{1,0:T(8,128)(2,1)S(1)}, u32[]{:S(2)}, u32[]{:S(2)}) collective-permute-start(bf16[256,256]{1,0:T(8,128)(2,1)S(1)} %get-tuple-element.71), channel_id=1, source_target_pairs={{0,2},{1,3},{2,0},{3,1},{4,6},{5,7},{6,4},{7,5},{8,10},{9,11},{10,... | collective-permute-start | bytes 393224 | tf_op jit(solution)/shard_map/ppermute | solution.py:268
  61.0 29.5 %all-to-all-start.2 = ((bf16[8,384,128]{2,1,0:T(8,128)(2,1)}), bf16[8,384,128]{2,1,0:T(8,128)(2,1)S(1)}, u32[]{:S(2)}, u32[]{:S(2)}) async-start(bf16[8,384,128]{2,1,0:T(8,128)(2,1)} %combine.1), calls=%async_computation.2 | async-start | bytes 1572864 | tf_op jit(solution)/shard_map/all_to_all | solution.py:317
  65.9 7.6 %collective-permute-start.17 = (bf16[128,1024]{1,0:T(8,128)(2,1)S(1)}, bf16[128,1024]{1,0:T(8,128)(2,1)S(1)}, u32[]{:S(2)}, u32[]{:S(2)}) collective-permute-start(bf16[128,1024]{1,0:T(8,128)(2,1)S(1)} %get-tuple-element.76), channel_id=1, source_target_pairs={{0,16},{16,0},{1,17},{17,1},{2,18},{18,2},{3,19},{19,3},{4,20},{20... | collective-permute-start | bytes 786440 | tf_op jit(solution)/shard_map/ppermute | solution.py:272
  73.6 7.5 %collective-permute-start.18 = (bf16[32,1024]{1,0:T(8,128)(2,1)S(1)}, bf16[32,1024]{1,0:T(8,128)(2,1)S(1)}, u32[]{:S(2)}, u32[]{:S(2)}) collective-permute-start(bf16[32,1024]{1,0:T(8,128)(2,1)S(1)} %get-tuple-element.79), channel_id=1, source_target_pairs={{0,4},{1,5},{2,6},{3,7},{4,0},{5,1},{6,2},{7,3},{8,12},{9,13},{10,... | collective-permute-start | bytes 196616 | tf_op jit(solution)/shard_map/ppermute | solution.py:268
  75.3 14.5 %collective-permute-start.19 = (bf16[32,1024]{1,0:T(8,128)(2,1)S(1)}, bf16[32,1024]{1,0:T(8,128)(2,1)S(1)}, u32[]{:S(2)}, u32[]{:S(2)}) collective-permute-start(bf16[32,1024]{1,0:T(8,128)(2,1)S(1)} %get-tuple-element.81), channel_id=1, source_target_pairs={{0,8},{1,9},{2,10},{3,11},{4,12},{5,13},{6,14},{7,15},{8,0},{9,1},... | collective-permute-start | bytes 196616 | tf_op jit(solution)/shard_map/ppermute | solution.py:268
  77.7 12.1 %collective-permute-start.20 = (bf16[32,1024]{1,0:T(8,128)(2,1)S(1)}, bf16[32,1024]{1,0:T(8,128)(2,1)S(1)}, u32[]{:S(2)}, u32[]{:S(2)}) collective-permute-start(bf16[32,1024]{1,0:T(8,128)(2,1)S(1)} %get-tuple-element.80), channel_id=1, source_target_pairs={{0,12},{1,13},{2,14},{3,15},{4,8},{5,9},{6,10},{7,11},{8,4},{9,5},... | collective-permute-start | bytes 196616 | tf_op jit(solution)/shard_map/ppermute | solution.py:268

commit v5 on v4

--- a/solution.py
+++ b/solution.py
@@ -130,6 +130,13 @@
     return (block % group) ^ ids_ref[1], block // group
 
 
+KEYS, VALUES = slice(0, BLOCK), slice(BLOCK, 2 * BLOCK)
+
+
+def both_blocks(kv_ref, j, picks, rows):
+    return jnp.concatenate([kv_ref[0, j, rows, :], kv_ref[picks[j][0], picks[j][1], rows, :]], axis=0)
+
+
 def forward_body(group, ids_ref, kb_ref, cnt_ref, *refs):
     own_ref, *other_refs = refs[:group]
     send_ref, probs_ref, kv_ref, s_ref, p_ref, t_ref, sems = refs[group:]
@@ -141,9 +148,9 @@
     for j in range(HEADS):
         q = own_ref[j, :BLOCK, :]
         both = cnt_ref[0, ids_ref[0], j * group + ids_ref[1]] > 1
-        s_ref[j, :, :BLOCK] = dot(q, kv_ref[0, j, :BLOCK, :], NT) * SCALE
-        s1 = dot(q, kv_ref[picks[j][0], picks[j][1], :BLOCK, :], NT) * SCALE
-        s_ref[j, :, BLOCK:] = jnp.where(both, s1, -jnp.inf)
+        s = dot(q, both_blocks(kv_ref, j, picks, KEYS), NT) * SCALE
+        s_ref[j, :, :BLOCK] = s[:, :BLOCK]
+        s_ref[j, :, BLOCK:] = jnp.where(both, s[:, BLOCK:], -jnp.inf)
     for j in range(HEADS):
         s = s_ref[j]
         e = jnp.exp(s - jnp.max(s, axis=-1, keepdims=True))
@@ -152,9 +159,7 @@
     copies.append(pltpu.make_async_copy(p_ref, probs_ref, sems.at[0]))
     copies[-1].start()
     for j in range(HEADS):
-        attn = dot(p_ref[j, :, :BLOCK], kv_ref[0, j, BLOCK:, :], NN) + dot(
-            p_ref[j, :, BLOCK:], kv_ref[picks[j][0], picks[j][1], BLOCK:, :], NN
-        )
+        attn = dot(p_ref[j], both_blocks(kv_ref, j, picks, VALUES), NN)
         t_ref[j] = attn.T.astype(BF16)
     copies.append(pltpu.make_async_copy(t_ref, send_ref, sems.at[1]))
     copies[-1].start()
@@ -185,8 +190,7 @@
         copy.wait()
     for j in range(HEADS):
         do = do_ref[j]
-        dp_ref[j, :, :BLOCK] = dot(do, kv_ref[0, j, BLOCK:, :], NT)
-        dp_ref[j, :, BLOCK:] = dot(do, kv_ref[picks[j][0], picks[j][1], BLOCK:, :], NT)
+        dp_ref[j] = dot(do, both_blocks(kv_ref, j, picks, VALUES), NT)
     for copy in loads[group:]:
         copy.wait()
     for j in range(HEADS):
@@ -207,13 +211,7 @@
         acc_ref[r, jb, :BLOCK, :] += dp_ref[j, :, :BLOCK]
         acc_ref[r, jb, BLOCK:, :] += dp_ref[j, :, BLOCK:]
     for j in range(HEADS):
-        dq_ref[j] = (
-            (
-                dot(ds_ref[j, :, :BLOCK], kv_ref[0, j, :BLOCK, :], NN)
-                + dot(ds_ref[j, :, BLOCK:], kv_ref[picks[j][0], picks[j][1], :BLOCK, :], NN)
-            )
-            * SCALE
-        ).astype(BF16)
+        dq_ref[j] = (dot(ds_ref[j], both_blocks(kv_ref, j, picks, KEYS), NN) * SCALE).astype(BF16)
     near_ref[:, :BLOCK, :] = (acc_ref[0, :, :BLOCK, :] * SCALE).astype(BF16)
     near_ref[:, BLOCK:, :] = acc_ref[0, :, BLOCK:, :].astype(BF16)
     for r in range(1, group):
@@ -291,8 +289,7 @@
         n_vmem=2, n_hbm=4, vmem=16, flops=GW_FLOPS, name="grad_weight",
     )(features[0], ctx_swap(features[1], 2), *rows)
     total = (keep + dp_swap(send).astype(F32)).reshape(4, 32, columns)
-    parts = [ctx_swap(total[zr].astype(BF16), 4 * zr) for zr in range(1, 4)]
-    return total[0] + sum(part.astype(F32) for part in parts)
+    return total[0], [ctx_swap(total[zr].astype(BF16), 4 * zr) for zr in range(1, 4)]
 
 
 D_OUT_FLOPS = 2**32
@@ -376,7 +373,11 @@
     tokens = shape((1, BLOCK, HEADS * HEAD_SIZE))
     grad_queries, grad_keys, grad_values = call(unpack_body, [tokens] * 3, n_vmem=1, name="unpack")(grads)
     if small:
-        grad_weight = reduce_weight(own_features(ids, back), same + cross)
+        mine, parts = reduce_weight(own_features(ids, back), same + cross)
+        mine, grad_queries, grad_keys, grad_values = together(
+            mine, grad_queries, grad_keys, grad_values
+        )
+        grad_weight = mine + sum(part.astype(F32) for part in parts)
     else:
         grad_weight = lax.psum_scatter(
             dot(back.reshape(HEADS * HEAD_SIZE, BLOCK), out_grad[0], NN),

time: 92 us -> 90.9 us (0.988)
    ppermute x19, waiting for transfers between devices: 21.7 us -> 13 us  [ctx_swap(): return lax.ppermute(x, 'ctx', [(i, i ^ mask) for i in range(n)])]
    all_to_all x3, waiting for transfers between devices: 2.97 us -> 11 us  [exchange(): return lax.all_to_all(x, 'ctx', 0, 0, tiled=True, axis_index_groups=peers)]
  transfers between devices with their start and end apart: 24 -> 24, of which waited for: 13 -> 13; matrix products, arithmetic and copies ran while one was open for 1% -> 0% of each run, Pallas kernels for 16% -> 17%
where the time goes in v5:
time: 90.9 us; the launch traced here: 90.4 us
  starting transfers between devices  36.4 us (40%)
  waiting for transfers between devices  34 us (37%)
  Pallas kernels  16.3 us (18%)
  local copies, waits for them, and re-layouts  2.06 us (2%)
    ppermute x19, starting transfers between devices, ctx_swap(): return lax.ppermute(x, 'ctx', [(i, i ^ mask) for i in range(n)])  19 us
    ppermute x19, waiting for transfers between devices, ctx_swap(): return lax.ppermute(x, 'ctx', [(i, i ^ mask) for i in range(n)])  13 us
    all_to_all x3, starting transfers between devices, exchange(): return lax.all_to_all(x, 'ctx', 0, 0, tiled=True, axis_index_groups=peers)  12.9 us
    all_to_all x3, waiting for transfers between devices, exchange(): return lax.all_to_all(x, 'ctx', 0, 0, tiled=True, axis_index_groups=peers)  11 us
    ppermute x2, waiting for transfers between devices, dp_swap(): return lax.ppermute(x, 'dp', [(0, 1), (1, 0)])  10.1 us
    ppermute x2, starting transfers between devices, dp_swap(): return lax.ppermute(x, 'dp', [(0, 1), (1, 0)])  4.47 us
    pallas_call x1, Pallas kernels, local(): call(functools.partial(forward_body, group), [tile, shape(score)], [kv_sc...  3.41 us
    pallas_call x1, Pallas kernels, local(): call(functools.partial(backward_body, group), [tile, pair] + [tile] * (2...  3.12 us
  transfers between devices with their start and end apart: 24, of which 13 were waited for; matrix products, arithmetic and copies ran while one was open for 0% of the time, Pallas kernels for 17%

profile of v5, /device:TPU:0, one launch (start us, length us, event | category | flops | bytes accessed | tf_op | source)
XLA Modules:
  0.0 90.4 jit_solution(5642728793348724018)
XLA Ops:
  0.6 1.1 %constant_dynamic-slice_fusion = bf16[256,1024]{1,0:T(8,128)(2,1)S(1)} fusion(bf16[512,1024]{1,0:T(8,128)(2,1)} %refs_0_.3, s32[]{:T(128)S(6)} %select_n.16), kind=kLoop, calls=%fused_computation.2 | loop fusion | bytes 1048580 | tf_op jit(solution)/shard_map/dynamic_slice | solution.py:318
  1.7 3.0 %collective-permute-start.1 = (bf16[256,1024]{1,0:T(8,128)(2,1)S(1)}, bf16[256,1024]{1,0:T(8,128)(2,1)S(1)}, u32[]{:S(2)}, u32[]{:S(2)}) collective-permute-start(bf16[256,1024]{1,0:T(8,128)(2,1)S(1)} %constant_dynamic-slice_fusion), channel_id=1, source_target_pairs={{0,16},{16,0},{1,17},{17,1},{2,18},{18,2},{3,19},{19,3},{4,20},{20... | collective-permute-start | bytes 1572872 | tf_op jit(solution)/shard_map/ppermute | solution.py:270
  4.7 2.0 %pack.1 = bf16[8,384,128]{2,1,0:T(8,128)(2,1)} custom-call(bf16[1,128,1024]{2,1,0:T(8,128)(2,1)} %q_ref.1, bf16[1,128,1024]{2,1,0:T(8,128)(2,1)} %k_ref.1, bf16[1,128,1024]{2,1,0:T(8,128)(2,1)} %v_ref.1), custom_call_target="tpu_custom_call" | custom-call | flops 34359738368 | tf_op jit(solution)/shard_map/pack/pallas_call | solution.py:75
  6.7 0.0 copy-start.6
  6.7 0.0 copy-start
  6.7 6.0 %all-to-all-start = ((bf16[8,384,128]{2,1,0:T(8,128)(2,1)}), bf16[8,384,128]{2,1,0:T(8,128)(2,1)S(1)}, u32[]{:S(2)}, u32[]{:S(2)}) async-start(bf16[8,384,128]{2,1,0:T(8,128)(2,1)} %pack.1), calls=%async_computation | async-start | bytes 1572864 | tf_op jit(solution)/shard_map/all_to_all | solution.py:314
  12.7 4.0 %collective-permute-done.1.refs_1_ = bf16[256,1024]{1,0:T(8,128)(2,1)S(1)} collective-permute-done((bf16[256,1024]{1,0:T(8,128)(2,1)S(1)}, bf16[256,1024]{1,0:T(8,128)(2,1)S(1)}, u32[]{:S(2)}, u32[]{:S(2)}) %collective-permute-start.1) | collective-permute-done | bytes 524320 | tf_op jit(solution)/shard_map/ppermute | solution.py:270
  16.7 0.0 collective-permute-start.2
  16.7 0.5 collective-permute-start
  17.2 0.1 stack.28.ids_ref
  17.3 1.3 %collective-permute-done.2.refs_2_ = bf16[256,1024]{1,0:T(8,128)(2,1)S(1)} collective-permute-done((bf16[256,1024]{1,0:T(8,128)(2,1)S(1)}, bf16[256,1024]{1,0:T(8,128)(2,1)S(1)}, u32[]{:S(2)}, u32[]{:S(2)}) %collective-permute-start.2) | collective-permute-done | bytes 524320 | tf_op jit(solution)/shard_map/ppermute | solution.py:266
  18.6 1.3 %d_out.1 = (bf16[128,128]{1,0:T(8,128)(2,1)S(1)}, bf16[128,128]{1,0:T(8,128)(2,1)S(1)}, bf16[128,128]{1,0:T(8,128)(2,1)S(1)}, bf16[128,128]{1,0:T(8,128)(2,1)S(1...) custom-call(s32[7]{0:T(128)S(1)} %stack.28.ids_ref, ...), custom_call_target="tpu_custom_call" | custom-call | flops 4294967296 | tf_op jit(solution)/shard_map/d_out/pallas_call | solution.py:333
  19.9 0.0 copy-start.9
  19.9 1.8 %collective-permute-start.3 = (bf16[128,128]{1,0:T(8,128)(2,1)S(1)}, bf16[128,128]{1,0:T(8,128)(2,1)S(1)}, u32[]{:S(2)}, u32[]{:S(2)}) collective-permute-start(bf16[128,128]{1,0:T(8,128)(2,1)S(1)} %get-tuple-element.46), channel_id=1, source_target_pairs={{0,2},{1,3},{2,0},{3,1},{4,6},{5,7},{6,4},{7,5},{8,10},{9,11},{10,... | collective-permute-start | bytes 98312 | tf_op jit(solution)/shard_map/ppermute | solution.py:266
  21.7 1.6 %collective-permute-start.4 = (bf16[128,128]{1,0:T(8,128)(2,1)S(1)}, bf16[128,128]{1,0:T(8,128)(2,1)S(1)}, u32[]{:S(2)}, u32[]{:S(2)}) collective-permute-start(bf16[128,128]{1,0:T(8,128)(2,1)S(1)} %get-tuple-element.47), channel_id=1, source_target_pairs={{0,4},{1,5},{2,6},{3,7},{4,0},{5,1},{6,2},{7,3},{8,12},{9,13},{10,... | collective-permute-start | bytes 98312 | tf_op jit(solution)/shard_map/ppermute | solution.py:266
  23.3 0.1 collective-permute-start.5
  23.4 2.8 %collective-permute-start.6 = (bf16[128,128]{1,0:T(8,128)(2,1)S(1)}, bf16[128,128]{1,0:T(8,128)(2,1)S(1)}, u32[]{:S(2)}, u32[]{:S(2)}) collective-permute-start(bf16[128,128]{1,0:T(8,128)(2,1)S(1)} %get-tuple-element.49), channel_id=1, source_target_pairs={{0,8},{1,9},{2,10},{3,11},{4,12},{5,13},{6,14},{7,15},{8,0},{9,1},... | collective-permute-start | bytes 98312 | tf_op jit(solution)/shard_map/ppermute | solution.py:266
  26.3 0.0 collective-permute-done.refs_4_
  26.3 0.7 copy-done.7
  27.0 1.3 %collective-permute-start.7 = (bf16[128,128]{1,0:T(8,128)(2,1)S(1)}, bf16[128,128]{1,0:T(8,128)(2,1)S(1)}, u32[]{:S(2)}, u32[]{:S(2)}) collective-permute-start(bf16[128,128]{1,0:T(8,128)(2,1)S(1)} %get-tuple-element.50), channel_id=1, source_target_pairs={{0,10},{1,11},{2,8},{3,9},{4,14},{5,15},{6,12},{7,13},{8,2},{9,3},... | collective-permute-start | bytes 98312 | tf_op jit(solution)/shard_map/ppermute | solution.py:266
  28.3 0.0 collective-permute-done.3.refs_1_
  28.3 3.6 %collective-permute-start.8 = (bf16[128,128]{1,0:T(8,128)(2,1)S(1)}, bf16[128,128]{1,0:T(8,128)(2,1)S(1)}, u32[]{:S(2)}, u32[]{:S(2)}) collective-permute-start(bf16[128,128]{1,0:T(8,128)(2,1)S(1)} %get-tuple-element.51), channel_id=1, source_target_pairs={{0,12},{1,13},{2,14},{3,15},{4,8},{5,9},{6,10},{7,11},{8,4},{9,5},... | collective-permute-start | bytes 98312 | tf_op jit(solution)/shard_map/ppermute | solution.py:266
  31.9 0.0 collective-permute-done.4.refs_2_
  31.9 0.0 collective-permute-start.9
  31.9 0.0 collective-permute-done.5.refs_3_
  31.9 5.0 %collective-permute-done.6.refs_4_ = bf16[128,128]{1,0:T(8,128)(2,1)S(1)} collective-permute-done((bf16[128,128]{1,0:T(8,128)(2,1)S(1)}, bf16[128,128]{1,0:T(8,128)(2,1)S(1)}, u32[]{:S(2)}, u32[]{:S(2)}) %collective-permute-start.6) | collective-permute-done | bytes 32800 | tf_op jit(solution)/shard_map/ppermute | solution.py:266
  36.9 1.1 %collective-permute-done.7.refs_5_ = bf16[128,128]{1,0:T(8,128)(2,1)S(1)} collective-permute-done((bf16[128,128]{1,0:T(8,128)(2,1)S(1)}, bf16[128,128]{1,0:T(8,128)(2,1)S(1)}, u32[]{:S(2)}, u32[]{:S(2)}) %collective-permute-start.7) | collective-permute-done | bytes 32800 | tf_op jit(solution)/shard_map/ppermute | solution.py:266
  38.0 0.6 collective-permute-done.9.refs_7_
  38.6 0.0 all-to-all-done.refs_0_.refs_8_
  38.6 0.0 collective-permute-start.10
  38.6 0.6 collective-permute-start.11
  39.2 0.1 copy.12.kb_ref
  39.3 1.6 %collective-permute-done.10.refs_1_.refs_9_ = bf16[8,384,128]{2,1,0:T(8,128)(2,1)S(1)} collective-permute-done((bf16[8,384,128]{2,1,0:T(8,128)(2,1)S(1)}, bf16[8,384,128]{2,1,0:T(8,128)(2,1)S(1)}, u32[]{:S(2)}, u32[]{:S(2)}) %collective-permute-start.10) | collective-permute-done | bytes 786464 | tf_op jit(solution)/shard_map/ppermute | solution.py:266
  40.9 3.4 %forward.1 = (bf16[8,128,128]{2,1,0:T(8,128)(2,1)}, bf16[8,128,256]{2,1,0:T(8,128)(2,1)S(1)}) custom-call(s32[7]{0:T(128)S(1)} %stack.28.ids_ref, s32[1,8,16,2]{3,2,1,0:T(8,128)S(1)} %copy.12.kb_ref, s32[1,8,16]{2,1,0:T(8,128)S(1)} %copy-done.5, bf16[8,384,128]{2,1,0:T(8,128)(2,1)S(1)} %all-to-all-done.refs_0_.refs_8_, ...), custom_call_target="tpu_custom_call" | custom-call | tf_op jit(solution)/shard_map/forward/pallas_call | solution.py:345
  44.3 3.4 %all-to-all-start.1 = ((bf16[8,128,128]{2,1,0:T(8,128)(2,1)}), bf16[8,128,128]{2,1,0:T(8,128)(2,1)S(1)}, u32[]{:S(2)}, u32[]{:S(2)}) async-start(bf16[8,128,128]{2,1,0:T(8,128)(2,1)} %get-tuple-element.54), calls=%async_computation.1 | async-start | bytes 524288 | tf_op jit(solution)/shard_map/all_to_all | solution.py:314
  47.8 3.1 %backward.1 = (bf16[8,128,128]{2,1,0:T(8,128)(2,1)S(1)}, bf16[8,256,128]{2,1,0:T(8,128)(2,1)S(1)}, bf16[8,128,128]{2,1,0:T(8,128)(2,1)S(1)}, bf16[8,128,128]{2,1,0:T(8,128)(2,1)S(1)}) custom-call(s32[7]{0:T(128)S(1)} %stack.28.ids_ref, s32[1,8,16,2]{3,2,1,0:T(8,128)S(1)} %copy.12.kb_ref, bf16[128,128]{1,0:T(8,128)(2,1)S(1)} %get-tuple-element.56.refs_0_, ...), custom_call_target="tpu_custom_call" | custom-call | tf_op jit(solution)/shard_map/backward/pallas_call | solution.py:356
  50.9 0.2 collective-permute-start.13
  51.1 0.4 collective-permute-start.14
  51.5 0.0 collective-permute-done.11.refs_3_
  51.5 0.1 collective-permute-start.12
  51.6 0.9 collective-permute-done.13.refs_0_
  52.5 0.4 collective-permute-done.14.refs_1_
  52.9 1.0 %combine.1 = bf16[8,384,128]{2,1,0:T(8,128)(2,1)} custom-call(bf16[8,128,128]{2,1,0:T(8,128)(2,1)S(1)} %get-tuple-element.65.dq_ref, bf16[8,256,128]{2,1,0:T(8,128)(2,1)S(1)} %get-tuple-element.66.near_ref, bf16[8,128,128]{2,1,0:T(8,128)(2,1)S(1)} %collective-permute-done.13.refs_0_, bf16[8,128,128]{2,1,0:T(8,128)(2,1)S(1)} %collective-permute-done.14.refs_1_), custom_call_target="tpu_custom_call" | custom-call | tf_op jit(solution)/shard_map/combine/pallas_call | solution.py:367
  53.9 0.0 collective-permute-done.12.refs_5_
  53.9 3.3 %all-to-all-done.1.back_ref.mine_ref = bf16[8,128,128]{2,1,0:T(8,128)(2,1)S(1)} async-done(((bf16[8,128,128]{2,1,0:T(8,128)(2,1)}), bf16[8,128,128]{2,1,0:T(8,128)(2,1)S(1)}, u32[]{:S(2)}, u32[]{:S(2)}) %all-to-all-start.1) | async-done | bytes 262176 | tf_op jit(solution)/shard_map/all_to_all | solution.py:314
  57.2 0.0 collective-permute-start.15
  57.2 1.5 %collective-permute-done.15.pair_ref = bf16[8,128,128]{2,1,0:T(8,128)(2,1)S(1)} collective-permute-done((bf16[8,128,128]{2,1,0:T(8,128)(2,1)S(1)}, bf16[8,128,128]{2,1,0:T(8,128)(2,1)S(1)}, u32[]{:S(2)}, u32[]{:S(2)}) %collective-permute-start.15) | collective-permute-done | bytes 262176 | tf_op jit(solution)/shard_map/ppermute | solution.py:266
  58.7 0.6 features.1
  59.4 0.0 copy-start.8
  59.4 1.5 %collective-permute-start.16 = (bf16[256,256]{1,0:T(8,128)(2,1)S(1)}, bf16[256,256]{1,0:T(8,128)(2,1)S(1)}, u32[]{:S(2)}, u32[]{:S(2)}) collective-permute-start(bf16[256,256]{1,0:T(8,128)(2,1)S(1)} %get-tuple-element.71), channel_id=1, source_target_pairs={{0,2},{1,3},{2,0},{3,1},{4,6},{5,7},{6,4},{7,5},{8,10},{9,11},{10,... | collective-permute-start | bytes 393224 | tf_op jit(solution)/shard_map/ppermute | solution.py:266
  60.8 3.5 %all-to-all-start.2 = ((bf16[8,384,128]{2,1,0:T(8,128)(2,1)}), bf16[8,384,128]{2,1,0:T(8,128)(2,1)S(1)}, u32[]{:S(2)}, u32[]{:S(2)}) async-start(bf16[8,384,128]{2,1,0:T(8,128)(2,1)} %combine.1), calls=%async_computation.2 | async-start | bytes 1572864 | tf_op jit(solution)/shard_map/all_to_all | solution.py:314
  64.4 0.6 collective-permute-done.16.refs_1_
  65.0 0.8 grad_weight.1
  65.8 1.5 %collective-permute-start.17 = (bf16[128,1024]{1,0:T(8,128)(2,1)S(1)}, bf16[128,1024]{1,0:T(8,128)(2,1)S(1)}, u32[]{:S(2)}, u32[]{:S(2)}) collective-permute-start(bf16[128,1024]{1,0:T(8,128)(2,1)S(1)} %get-tuple-element.76), channel_id=1, source_target_pairs={{0,16},{16,0},{1,17},{17,1},{2,18},{18,2},{3,19},{19,3},{4,20},{20... | collective-permute-start | bytes 786440 | tf_op jit(solution)/shard_map/ppermute | solution.py:270
  67.2 6.1 %collective-permute-done.17 = bf16[128,1024]{1,0:T(8,128)(2,1)S(1)} collective-permute-done((bf16[128,1024]{1,0:T(8,128)(2,1)S(1)}, bf16[128,1024]{1,0:T(8,128)(2,1)S(1)}, u32[]{:S(2)}, u32[]{:S(2)}) %collective-permute-start.17) | collective-permute-done | bytes 262176 | tf_op jit(solution)/shard_map/ppermute | solution.py:270
  73.4 0.1 fusion
  73.5 1.7 %collective-permute-start.18 = (bf16[32,1024]{1,0:T(8,128)(2,1)S(1)}, bf16[32,1024]{1,0:T(8,128)(2,1)S(1)}, u32[]{:S(2)}, u32[]{:S(2)}) collective-permute-start(bf16[32,1024]{1,0:T(8,128)(2,1)S(1)} %get-tuple-element.87), channel_id=1, source_target_pairs={{0,4},{1,5},{2,6},{3,7},{4,0},{5,1},{6,2},{7,3},{8,12},{9,13},{10,... | collective-permute-start | bytes 196616 | tf_op jit(solution)/shard_map/ppermute | solution.py:266
  75.2 2.4 %collective-permute-start.19 = (bf16[32,1024]{1,0:T(8,128)(2,1)S(1)}, bf16[32,1024]{1,0:T(8,128)(2,1)S(1)}, u32[]{:S(2)}, u32[]{:S(2)}) collective-permute-start(bf16[32,1024]{1,0:T(8,128)(2,1)S(1)} %get-tuple-element.89), channel_id=1, source_target_pairs={{0,8},{1,9},{2,10},{3,11},{4,12},{5,13},{6,14},{7,15},{8,0},{9,1},... | collective-permute-start | bytes 196616 | tf_op jit(solution)/shard_map/ppermute | solution.py:266
  77.6 0.4 collective-permute-start.20
  77.9 3.0 %output.1 = bf16[1,128,1024]{2,1,0:T(8,128)(2,1)} custom-call(s32[7]{0:T(128)} %copy-done.4, bf16[8,128,128]{2,1,0:T(8,128)(2,1)} %copy-done.1, bf16[512,1024]{1,0:T(8,128)(2,1)} %refs_0_.3, bf16[256,1024]{1,0:T(8,128)(2,1)} %copy-done.2, bf16[256,1024]{1,0:T(8,128)(2,1)} %copy-done.3), custom_call_target="tpu_custom_call" | custom-call | tf_op jit(solution)/shard_map/output/pallas_call | solution.py:386
  81.0 7.7 %all-to-all-done.2.recv_ref = bf16[8,384,128]{2,1,0:T(8,128)(2,1)S(1)} async-done(((bf16[8,384,128]{2,1,0:T(8,128)(2,1)}), bf16[8,384,128]{2,1,0:T(8,128)(2,1)S(1)}, u32[]{:S(2)}, u32[]{:S(2)}) %all-to-all-start.2) | async-done | bytes 786464 | tf_op jit(solution)/shard_map/all_to_all | solution.py:314
  88.6 1.1 %unpack.1 = (bf16[1,128,1024]{2,1,0:T(8,128)(2,1)}, bf16[1,128,1024]{2,1,0:T(8,128)(2,1)}, bf16[1,128,1024]{2,1,0:T(8,128)(2,1)}) custom-call(bf16[8,384,128]{2,1,0:T(8,128)(2,1)S(1)} %all-to-all-done.2.recv_ref), custom_call_target="tpu_custom_call" | custom-call | tf_op jit(solution)/shard_map/unpack/pallas_call | solution.py:374
  89.7 0.0 collective-permute-done.18
  89.7 0.7 add_add_fusion
  (20 shorter events, 0.1 us)
Async XLA Ops:
  1.7 14.9 %collective-permute-start.1 = (bf16[256,1024]{1,0:T(8,128)(2,1)S(1)}, bf16[256,1024]{1,0:T(8,128)(2,1)S(1)}, u32[]{:S(2)}, u32[]{:S(2)}) collective-permute-start(bf16[256,1024]{1,0:T(8,128)(2,1)S(1)} %constant_dynamic-slice_fusion), channel_id=1, source_target_pairs={{0,16},{16,0},{1,17},{17,1},{2,18},{18,2},{3,19},{19,3},{4,20},{20... | collective-permute-start | bytes 1572872 | tf_op jit(solution)/shard_map/ppermute | solution.py:270
  6.7 10.0 %copy-start.6 = (bf16[1,128,1024]{2,1,0:T(8,128)(2,1)S(1)}, bf16[1,128,1024]{2,1,0:T(8,128)(2,1)}, u32[]{:S(2)}) copy-start(bf16[1,128,1024]{2,1,0:T(8,128)(2,1)} %refs_2_.1) | copy-start | bytes 786436
  6.7 11.9 %copy-start = (bf16[512,1024]{1,0:T(8,128)(2,1)S(1)}, bf16[512,1024]{1,0:T(8,128)(2,1)}, u32[]{:S(2)}) copy-start(bf16[512,1024]{1,0:T(8,128)(2,1)} %refs_0_.3) | copy-start | bytes 3145732
  6.7 31.9 %all-to-all-start = ((bf16[8,384,128]{2,1,0:T(8,128)(2,1)}), bf16[8,384,128]{2,1,0:T(8,128)(2,1)S(1)}, u32[]{:S(2)}, u32[]{:S(2)}) async-start(bf16[8,384,128]{2,1,0:T(8,128)(2,1)} %pack.1), calls=%async_computation | async-start | bytes 1572864 | tf_op jit(solution)/shard_map/all_to_all | solution.py:314
  16.6 3.2 %copy-start.2 = (bf16[256,1024]{1,0:T(8,128)(2,1)}, bf16[256,1024]{1,0:T(8,128)(2,1)S(1)}, u32[]{:S(2)}) copy-start(bf16[256,1024]{1,0:T(8,128)(2,1)S(1)} %collective-permute-done.1.refs_1_) | copy-start | bytes 1572868
  16.7 1.9 %collective-permute-start.2 = (bf16[256,1024]{1,0:T(8,128)(2,1)S(1)}, bf16[256,1024]{1,0:T(8,128)(2,1)S(1)}, u32[]{:S(2)}, u32[]{:S(2)}) collective-permute-start(bf16[256,1024]{1,0:T(8,128)(2,1)S(1)} %collective-permute-done.1.refs_1_), channel_id=1, source_target_pairs={{0,1},{1,0},{2,3},{3,2},{4,5},{5,4},{6,7},{7,6},{8,9},{9,8},{10,11... | collective-permute-start | bytes 1572872 | tf_op jit(solution)/shard_map/ppermute | solution.py:266
  16.7 9.6 %collective-permute-start = (bf16[1,128,1024]{2,1,0:T(8,128)(2,1)S(1)}, bf16[1,128,1024]{2,1,0:T(8,128)(2,1)S(1)}, u32[]{:S(2)}, u32[]{:S(2)}) collective-permute-start(bf16[1,128,1024]{2,1,0:T(8,128)(2,1)S(1)} %copy-done.6), channel_id=1, source_target_pairs={{0,1},{1,0},{2,3},{3,2},{4,5},{5,4},{6,7},{7,6},{8,9},{9,8},{10,11... | collective-permute-start | bytes 786440 | tf_op jit(solution)/shard_map/ppermute | solution.py:266
  17.2 41.5 %copy-start.4 = (s32[7]{0:T(128)}, s32[7]{0:T(128)S(1)}, u32[]{:S(2)}) copy-start(s32[7]{0:T(128)S(1)} %stack.28.ids_ref) | copy-start | bytes 88
  18.6 1.3 %copy-start.3 = (bf16[256,1024]{1,0:T(8,128)(2,1)}, bf16[256,1024]{1,0:T(8,128)(2,1)S(1)}, u32[]{:S(2)}) copy-start(bf16[256,1024]{1,0:T(8,128)(2,1)S(1)} %collective-permute-done.2.refs_2_) | copy-start | bytes 1572868
  19.9 19.3 %copy-start.9 = (s32[1,8,16,2]{2,3,1,0:T(2,128)S(1)}, s32[1,8,16,2]{2,3,1,0:T(2,128)}, u32[]{:S(2)}) copy-start(s32[1,8,16,2]{2,3,1,0:T(2,128)} %param.12) | copy-start | bytes 3076
  19.9 8.4 %collective-permute-start.3 = (bf16[128,128]{1,0:T(8,128)(2,1)S(1)}, bf16[128,128]{1,0:T(8,128)(2,1)S(1)}, u32[]{:S(2)}, u32[]{:S(2)}) collective-permute-start(bf16[128,128]{1,0:T(8,128)(2,1)S(1)} %get-tuple-element.46), channel_id=1, source_target_pairs={{0,2},{1,3},{2,0},{3,1},{4,6},{5,7},{6,4},{7,5},{8,10},{9,11},{10,... | collective-permute-start | bytes 98312 | tf_op jit(solution)/shard_map/ppermute | solution.py:266
  21.7 10.2 %collective-permute-start.4 = (bf16[128,128]{1,0:T(8,128)(2,1)S(1)}, bf16[128,128]{1,0:T(8,128)(2,1)S(1)}, u32[]{:S(2)}, u32[]{:S(2)}) collective-permute-start(bf16[128,128]{1,0:T(8,128)(2,1)S(1)} %get-tuple-element.47), channel_id=1, source_target_pairs={{0,4},{1,5},{2,6},{3,7},{4,0},{5,1},{6,2},{7,3},{8,12},{9,13},{10,... | collective-permute-start | bytes 98312 | tf_op jit(solution)/shard_map/ppermute | solution.py:266
  23.3 8.6 %collective-permute-start.5 = (bf16[128,128]{1,0:T(8,128)(2,1)S(1)}, bf16[128,128]{1,0:T(8,128)(2,1)S(1)}, u32[]{:S(2)}, u32[]{:S(2)}) collective-permute-start(bf16[128,128]{1,0:T(8,128)(2,1)S(1)} %get-tuple-element.48), channel_id=1, source_target_pairs={{0,6},{1,7},{2,4},{3,5},{4,2},{5,3},{6,0},{7,1},{8,14},{9,15},{10,... | collective-permute-start | bytes 98312 | tf_op jit(solution)/shard_map/ppermute | solution.py:266
  23.4 13.4 %collective-permute-start.6 = (bf16[128,128]{1,0:T(8,128)(2,1)S(1)}, bf16[128,128]{1,0:T(8,128)(2,1)S(1)}, u32[]{:S(2)}, u32[]{:S(2)}) collective-permute-start(bf16[128,128]{1,0:T(8,128)(2,1)S(1)} %get-tuple-element.49), channel_id=1, source_target_pairs={{0,8},{1,9},{2,10},{3,11},{4,12},{5,13},{6,14},{7,15},{8,0},{9,1},... | collective-permute-start | bytes 98312 | tf_op jit(solution)/shard_map/ppermute | solution.py:266
  26.3 0.7 copy-start.7
  27.0 11.0 %collective-permute-start.7 = (bf16[128,128]{1,0:T(8,128)(2,1)S(1)}, bf16[128,128]{1,0:T(8,128)(2,1)S(1)}, u32[]{:S(2)}, u32[]{:S(2)}) collective-permute-start(bf16[128,128]{1,0:T(8,128)(2,1)S(1)} %get-tuple-element.50), channel_id=1, source_target_pairs={{0,10},{1,11},{2,8},{3,9},{4,14},{5,15},{6,12},{7,13},{8,2},{9,3},... | collective-permute-start | bytes 98312 | tf_op jit(solution)/shard_map/ppermute | solution.py:266
  28.3 9.7 %collective-permute-start.8 = (bf16[128,128]{1,0:T(8,128)(2,1)S(1)}, bf16[128,128]{1,0:T(8,128)(2,1)S(1)}, u32[]{:S(2)}, u32[]{:S(2)}) collective-permute-start(bf16[128,128]{1,0:T(8,128)(2,1)S(1)} %get-tuple-element.51), channel_id=1, source_target_pairs={{0,12},{1,13},{2,14},{3,15},{4,8},{5,9},{6,10},{7,11},{8,4},{9,5},... | collective-permute-start | bytes 98312 | tf_op jit(solution)/shard_map/ppermute | solution.py:266
  31.9 6.7 %collective-permute-start.9 = (bf16[128,128]{1,0:T(8,128)(2,1)S(1)}, bf16[128,128]{1,0:T(8,128)(2,1)S(1)}, u32[]{:S(2)}, u32[]{:S(2)}) collective-permute-start(bf16[128,128]{1,0:T(8,128)(2,1)S(1)} %get-tuple-element.52), channel_id=1, source_target_pairs={{0,14},{1,15},{2,12},{3,13},{4,10},{5,11},{6,8},{7,9},{8,6},{9,7},... | collective-permute-start | bytes 98312 | tf_op jit(solution)/shard_map/ppermute | solution.py:266
  38.6 2.3 %copy-start.5 = (s32[1,8,16]{2,1,0:T(8,128)S(1)}, s32[1,8,16]{2,1,0:T(8,128)}, u32[]{:S(2)}) copy-start(s32[1,8,16]{2,1,0:T(8,128)} %cnt_ref.1) | copy-start | bytes 1540
  38.6 2.3 %collective-permute-start.10 = (bf16[8,384,128]{2,1,0:T(8,128)(2,1)S(1)}, bf16[8,384,128]{2,1,0:T(8,128)(2,1)S(1)}, u32[]{:S(2)}, u32[]{:S(2)}) collective-permute-start(bf16[8,384,128]{2,1,0:T(8,128)(2,1)S(1)} %all-to-all-done.refs_0_.refs_8_), channel_id=1, source_target_pairs={{0,1},{1,0},{2,3},{3,2},{4,5},{5,4},{6,7},{7,6},{8,9},{9,8},{10,11... | collective-permute-start | bytes 2359304 | tf_op jit(solution)/shard_map/ppermute | solution.py:266
  38.6 12.8 %collective-permute-start.11 = (bf16[1,128,1024]{2,1,0:T(8,128)(2,1)S(1)}, bf16[1,128,1024]{2,1,0:T(8,128)(2,1)S(1)}, u32[]{:S(2)}, u32[]{:S(2)}) collective-permute-start(bf16[1,128,1024]{2,1,0:T(8,128)(2,1)S(1)} %copy-done.6), channel_id=1, source_target_pairs={{0,2},{1,3},{2,0},{3,1},{4,6},{5,7},{6,4},{7,5},{8,10},{9,11},{10,... | collective-permute-start | bytes 786440 | tf_op jit(solution)/shard_map/ppermute | solution.py:266
  44.3 12.9 %all-to-all-start.1 = ((bf16[8,128,128]{2,1,0:T(8,128)(2,1)}), bf16[8,128,128]{2,1,0:T(8,128)(2,1)S(1)}, u32[]{:S(2)}, u32[]{:S(2)}) async-start(bf16[8,128,128]{2,1,0:T(8,128)(2,1)} %get-tuple-element.54), calls=%async_computation.1 | async-start | bytes 524288 | tf_op jit(solution)/shard_map/all_to_all | solution.py:314
  50.9 1.6 %collective-permute-start.13 = (bf16[8,128,128]{2,1,0:T(8,128)(2,1)S(1)}, bf16[8,128,128]{2,1,0:T(8,128)(2,1)S(1)}, u32[]{:S(2)}, u32[]{:S(2)}) collective-permute-start(bf16[8,128,128]{2,1,0:T(8,128)(2,1)S(1)} %get-tuple-element.67), channel_id=1, source_target_pairs={{0,1},{1,0},{2,3},{3,2},{4,5},{5,4},{6,7},{7,6},{8,9},{9,8},{10,11... | collective-permute-start | bytes 786440 | tf_op jit(solution)/shard_map/ppermute | solution.py:266
  51.1 1.8 %collective-permute-start.14 = (bf16[8,128,128]{2,1,0:T(8,128)(2,1)S(1)}, bf16[8,128,128]{2,1,0:T(8,128)(2,1)S(1)}, u32[]{:S(2)}, u32[]{:S(2)}) collective-permute-start(bf16[8,128,128]{2,1,0:T(8,128)(2,1)S(1)} %get-tuple-element.68), channel_id=1, source_target_pairs={{0,1},{1,0},{2,3},{3,2},{4,5},{5,4},{6,7},{7,6},{8,9},{9,8},{10,11... | collective-permute-start | bytes 786440 | tf_op jit(solution)/shard_map/ppermute | solution.py:266
  51.5 2.4 %collective-permute-start.12 = (bf16[1,128,1024]{2,1,0:T(8,128)(2,1)S(1)}, bf16[1,128,1024]{2,1,0:T(8,128)(2,1)S(1)}, u32[]{:S(2)}, u32[]{:S(2)}) collective-permute-start(bf16[1,128,1024]{2,1,0:T(8,128)(2,1)S(1)} %collective-permute-done.11.refs_3_), channel_id=1, source_target_pairs={{0,1},{1,0},{2,3},{3,2},{4,5},{5,4},{6,7},{7,6},{8,9},{9,8},{10,11... | collective-permute-start | bytes 786440 | tf_op jit(solution)/shard_map/ppermute | solution.py:266
  57.2 2.2 %copy-start.1 = (bf16[8,128,128]{2,1,0:T(8,128)(2,1)}, bf16[8,128,128]{2,1,0:T(8,128)(2,1)S(1)}, u32[]{:S(2)}) copy-start(bf16[8,128,128]{2,1,0:T(8,128)(2,1)S(1)} %all-to-all-done.1.back_ref.mine_ref) | copy-start | bytes 786436
  57.2 1.5 %collective-permute-start.15 = (bf16[8,128,128]{2,1,0:T(8,128)(2,1)S(1)}, bf16[8,128,128]{2,1,0:T(8,128)(2,1)S(1)}, u32[]{:S(2)}, u32[]{:S(2)}) collective-permute-start(bf16[8,128,128]{2,1,0:T(8,128)(2,1)S(1)} %all-to-all-done.1.back_ref.mine_ref), channel_id=1, source_target_pairs={{0,1},{1,0},{2,3},{3,2},{4,5},{5,4},{6,7},{7,6},{8,9},{9,8},{10,11... | collective-permute-start | bytes 786440 | tf_op jit(solution)/shard_map/ppermute | solution.py:266
  59.4 5.6 %copy-start.8 = (bf16[1,128,1024]{2,1,0:T(8,128)(2,1)S(1)}, bf16[1,128,1024]{2,1,0:T(8,128)(2,1)}, u32[]{:S(2)}) copy-start(bf16[1,128,1024]{2,1,0:T(8,128)(2,1)} %copy-done.7) | copy-start | bytes 786436
  59.4 5.6 %collective-permute-start.16 = (bf16[256,256]{1,0:T(8,128)(2,1)S(1)}, bf16[256,256]{1,0:T(8,128)(2,1)S(1)}, u32[]{:S(2)}, u32[]{:S(2)}) collective-permute-start(bf16[256,256]{1,0:T(8,128)(2,1)S(1)} %get-tuple-element.71), channel_id=1, source_target_pairs={{0,2},{1,3},{2,0},{3,1},{4,6},{5,7},{6,4},{7,5},{8,10},{9,11},{10,... | collective-permute-start | bytes 393224 | tf_op jit(solution)/shard_map/ppermute | solution.py:266
  60.8 27.8 %all-to-all-start.2 = ((bf16[8,384,128]{2,1,0:T(8,128)(2,1)}), bf16[8,384,128]{2,1,0:T(8,128)(2,1)S(1)}, u32[]{:S(2)}, u32[]{:S(2)}) async-start(bf16[8,384,128]{2,1,0:T(8,128)(2,1)} %combine.1), calls=%async_computation.2 | async-start | bytes 1572864 | tf_op jit(solution)/shard_map/all_to_all | solution.py:314
  65.8 7.6 %collective-permute-start.17 = (bf16[128,1024]{1,0:T(8,128)(2,1)S(1)}, bf16[128,1024]{1,0:T(8,128)(2,1)S(1)}, u32[]{:S(2)}, u32[]{:S(2)}) collective-permute-start(bf16[128,1024]{1,0:T(8,128)(2,1)S(1)} %get-tuple-element.76), channel_id=1, source_target_pairs={{0,16},{16,0},{1,17},{17,1},{2,18},{18,2},{3,19},{19,3},{4,20},{20... | collective-permute-start | bytes 786440 | tf_op jit(solution)/shard_map/ppermute | solution.py:270
  73.5 16.3 %collective-permute-start.18 = (bf16[32,1024]{1,0:T(8,128)(2,1)S(1)}, bf16[32,1024]{1,0:T(8,128)(2,1)S(1)}, u32[]{:S(2)}, u32[]{:S(2)}) collective-permute-start(bf16[32,1024]{1,0:T(8,128)(2,1)S(1)} %get-tuple-element.87), channel_id=1, source_target_pairs={{0,4},{1,5},{2,6},{3,7},{4,0},{5,1},{6,2},{7,3},{8,12},{9,13},{10,... | collective-permute-start | bytes 196616 | tf_op jit(solution)/shard_map/ppermute | solution.py:266
  75.2 14.6 %collective-permute-start.19 = (bf16[32,1024]{1,0:T(8,128)(2,1)S(1)}, bf16[32,1024]{1,0:T(8,128)(2,1)S(1)}, u32[]{:S(2)}, u32[]{:S(2)}) collective-permute-start(bf16[32,1024]{1,0:T(8,128)(2,1)S(1)} %get-tuple-element.89), channel_id=1, source_target_pairs={{0,8},{1,9},{2,10},{3,11},{4,12},{5,13},{6,14},{7,15},{8,0},{9,1},... | collective-permute-start | bytes 196616 | tf_op jit(solution)/shard_map/ppermute | solution.py:266
  77.6 12.2 %collective-permute-start.20 = (bf16[32,1024]{1,0:T(8,128)(2,1)S(1)}, bf16[32,1024]{1,0:T(8,128)(2,1)S(1)}, u32[]{:S(2)}, u32[]{:S(2)}) collective-permute-start(bf16[32,1024]{1,0:T(8,128)(2,1)S(1)} %get-tuple-element.88), channel_id=1, source_target_pairs={{0,12},{1,13},{2,14},{3,15},{4,8},{5,9},{6,10},{7,11},{8,4},{9,5},... | collective-permute-start | bytes 196616 | tf_op jit(solution)/shard_map/ppermute | solution.py:266

commit v6 on v5

--- a/solution.py
+++ b/solution.py
@@ -230,20 +230,18 @@
         send_ref[:, BLOCK + part * BLOCK : 2 * BLOCK + part * BLOCK, :] = total.astype(BF16)
 
 
-def feature_body(ids_ref, mine_ref, pair_ref, *out_refs):
+def feature_body(ids_ref, mine_ref, *out_refs):
     d, z, y, c = ids_ref[2], ids_ref[3], ids_ref[4], ids_ref[5]
-    for yr, ref in enumerate(out_refs):
-        first = pl.multiple_of((yr ^ y) * 64 + c * 32, 32)
+    for to, ref in enumerate(out_refs):
+        first = pl.multiple_of(((to >> 1) ^ y) * 64 + ((to & 1) ^ c) * 32, 32)
         for place in range(HEADS):
             h = ((place >> 2) ^ d) * 4 + ((place & 3) ^ z)
-            rows = slice(place * 32, (place + 1) * 32)
-            ref[rows, :BLOCK] = mine_ref[h, pl.ds(first, 32), :]
-            ref[rows, BLOCK:] = pair_ref[h, pl.ds(first, 32), :]
+            ref[place * 32 : (place + 1) * 32, :] = mine_ref[h, pl.ds(first, 32), :]
 
 
 def grad_weight_body(*refs):
-    attn_refs, grad_refs = refs[:2], refs[2:6]
-    keep_ref, send_ref, rows_ref, sems = refs[6:]
+    attn_refs, grad_refs = refs[:4], refs[4:8]
+    keep_ref, send_ref, rows_ref, sems = refs[8:]
     loads = [
         pltpu.make_async_copy(ref.at[0], rows_ref.at[i], sems.at[i]) for i, ref in enumerate(grad_refs)
     ]
@@ -256,8 +254,7 @@
         rows = slice(place * half, (place + 1) * half)
         total = jnp.zeros(ref.shape, F32)
         for i, attn_ref in enumerate(attn_refs):
-            total += dot(attn_ref[rows, :BLOCK], rows_ref[i], NN)
-            total += dot(attn_ref[rows, BLOCK:], rows_ref[i + 2], NN)
+            total += dot(attn_ref[rows, :], rows_ref[i], NN)
         ref[...] = total.astype(ref.dtype)
 
 
@@ -276,18 +273,19 @@
 
 def own_features(ids, back):
     return call(
-        feature_body, [shape((HEADS * 32, 2 * BLOCK))] * 2, n_smem=1, n_vmem=2, name="features"
-    )(ids, back, ctx_swap(back, 1))
+        feature_body, [shape((HEADS * 32, BLOCK))] * 4, n_smem=1, n_vmem=1, name="features"
+    )(ids, back)
 
 
 def reduce_weight(features, rows):
     columns = rows[0].shape[-1]
+    attn = [features[0]] + [ctx_swap(features[to], to) for to in (1, 2, 3)]
     keep, send = call(
         grad_weight_body,
         [shape((4 * 32, columns), F32), shape((4 * 32, columns))],
         [pltpu.VMEM((4, BLOCK, columns), BF16), pltpu.SemaphoreType.DMA((4,))],
-        n_vmem=2, n_hbm=4, vmem=16, flops=GW_FLOPS, name="grad_weight",
-    )(features[0], ctx_swap(features[1], 2), *rows)
+        n_vmem=4, n_hbm=4, vmem=16, flops=GW_FLOPS, name="grad_weight",
+    )(*attn, *rows)
     total = (keep + dp_swap(send).astype(F32)).reshape(4, 32, columns)
     return total[0], [ctx_swap(total[zr].astype(BF16), 4 * zr) for zr in range(1, 4)]
 
@@ -373,7 +371,7 @@
     tokens = shape((1, BLOCK, HEADS * HEAD_SIZE))
     grad_queries, grad_keys, grad_values = call(unpack_body, [tokens] * 3, n_vmem=1, name="unpack")(grads)
     if small:
-        mine, parts = reduce_weight(own_features(ids, back), same + cross)
+        mine, parts = reduce_weight(own_features(ids, back), [same[0], cross[0], same[1], cross[1]])
         mine, grad_queries, grad_keys, grad_values = together(
             mine, grad_queries, grad_keys, grad_values
         )

time: 90.9 us -> 90.2 us (level)
  waiting for transfers between devices: 34 us -> 32.9 us
    ppermute x19 -> x20, waiting for transfers between devices: 13 us -> 11.4 us  [ctx_swap(): return lax.ppermute(x, 'ctx', [(i, i ^ mask) for i in range(n)])]
    ppermute x2, waiting for transfers between devices: 10.1 us -> 11 us  [dp_swap(): return lax.ppermute(x, 'dp', [(0, 1), (1, 0)])]
    ppermute x19 -> x20, starting transfers between devices: 19 us -> 19.5 us  [ctx_swap(): return lax.ppermute(x, 'ctx', [(i, i ^ mask) for i in range(n)])]
  transfers between devices with their start and end apart: 24 -> 25, of which waited for: 13 -> 13; matrix products, arithmetic and copies ran while one was open for 0% -> 0% of each run, Pallas kernels for 17% -> 18%
where the time goes in v6:
time: 90.2 us; the launch traced here: 89.7 us
  starting transfers between devices  36.9 us (41%)
  waiting for transfers between devices  32.9 us (36%)
  Pallas kernels  16.3 us (18%)
  local copies, waits for them, and re-layouts  2.06 us (2%)
    ppermute x20, starting transfers between devices, ctx_swap(): return lax.ppermute(x, 'ctx', [(i, i ^ mask) for i in range(n)])  19.5 us
    all_to_all x3, starting transfers between devices, exchange(): return lax.all_to_all(x, 'ctx', 0, 0, tiled=True, axis_index_groups=peers)  13 us
    ppermute x20, waiting for transfers between devices, ctx_swap(): return lax.ppermute(x, 'ctx', [(i, i ^ mask) for i in range(n)])  11.4 us
    ppermute x2, waiting for transfers between devices, dp_swap(): return lax.ppermute(x, 'dp', [(0, 1), (1, 0)])  11 us
    all_to_all x3, waiting for transfers between devices, exchange(): return lax.all_to_all(x, 'ctx', 0, 0, tiled=True, axis_index_groups=peers)  10.5 us
    ppermute x2, starting transfers between devices, dp_swap(): return lax.ppermute(x, 'dp', [(0, 1), (1, 0)])  4.44 us
    pallas_call x1, Pallas kernels, local(): call(functools.partial(forward_body, group), [tile, shape(score)], [kv_sc...  3.41 us
    pallas_call x1, Pallas kernels, local(): call(functools.partial(backward_body, group), [tile, pair] + [tile] * (2...  3.13 us
  transfers between devices with their start and end apart: 25, of which 13 were waited for; matrix products, arithmetic and copies ran while one was open for 0% of the time, Pallas kernels for 18%

profile of v6, /device:TPU:0, one launch (start us, length us, event | category | flops | bytes accessed | tf_op | source)
XLA Modules:
  0.0 89.7 jit_solution(4341005876343783765)
XLA Ops:
  0.6 1.1 %constant_dynamic-slice_fusion = bf16[256,1024]{1,0:T(8,128)(2,1)S(1)} fusion(bf16[512,1024]{1,0:T(8,128)(2,1)} %refs_0_.3, s32[]{:T(128)S(6)} %select_n.16), kind=kLoop, calls=%fused_computation.2 | loop fusion | bytes 1048580 | tf_op jit(solution)/shard_map/dynamic_slice | solution.py:316
  1.7 3.0 %collective-permute-start.1 = (bf16[256,1024]{1,0:T(8,128)(2,1)S(1)}, bf16[256,1024]{1,0:T(8,128)(2,1)S(1)}, u32[]{:S(2)}, u32[]{:S(2)}) collective-permute-start(bf16[256,1024]{1,0:T(8,128)(2,1)S(1)} %constant_dynamic-slice_fusion), channel_id=1, source_target_pairs={{0,16},{16,0},{1,17},{17,1},{2,18},{18,2},{3,19},{19,3},{4,20},{20... | collective-permute-start | bytes 1572872 | tf_op jit(solution)/shard_map/ppermute | solution.py:267
  4.7 1.9 %pack.1 = bf16[8,384,128]{2,1,0:T(8,128)(2,1)} custom-call(bf16[1,128,1024]{2,1,0:T(8,128)(2,1)} %q_ref.1, bf16[1,128,1024]{2,1,0:T(8,128)(2,1)} %k_ref.1, bf16[1,128,1024]{2,1,0:T(8,128)(2,1)} %v_ref.1), custom_call_target="tpu_custom_call" | custom-call | flops 34359738368 | tf_op jit(solution)/shard_map/pack/pallas_call | solution.py:75
  6.7 0.0 copy-start.6
  6.7 0.0 copy-start
  6.7 6.0 %all-to-all-start = ((bf16[8,384,128]{2,1,0:T(8,128)(2,1)}), bf16[8,384,128]{2,1,0:T(8,128)(2,1)S(1)}, u32[]{:S(2)}, u32[]{:S(2)}) async-start(bf16[8,384,128]{2,1,0:T(8,128)(2,1)} %pack.1), calls=%async_computation | async-start | bytes 1572864 | tf_op jit(solution)/shard_map/all_to_all | solution.py:312
  12.7 4.0 %collective-permute-done.1.refs_1_ = bf16[256,1024]{1,0:T(8,128)(2,1)S(1)} collective-permute-done((bf16[256,1024]{1,0:T(8,128)(2,1)S(1)}, bf16[256,1024]{1,0:T(8,128)(2,1)S(1)}, u32[]{:S(2)}, u32[]{:S(2)}) %collective-permute-start.1) | collective-permute-done | bytes 524320 | tf_op jit(solution)/shard_map/ppermute | solution.py:267
  16.7 0.0 collective-permute-start.2
  16.7 0.5 collective-permute-start
  17.2 0.1 stack.28.ids_ref
  17.3 1.3 %collective-permute-done.2.refs_2_ = bf16[256,1024]{1,0:T(8,128)(2,1)S(1)} collective-permute-done((bf16[256,1024]{1,0:T(8,128)(2,1)S(1)}, bf16[256,1024]{1,0:T(8,128)(2,1)S(1)}, u32[]{:S(2)}, u32[]{:S(2)}) %collective-permute-start.2) | collective-permute-done | bytes 524320 | tf_op jit(solution)/shard_map/ppermute | solution.py:263
  18.6 1.3 %d_out.1 = (bf16[128,128]{1,0:T(8,128)(2,1)S(1)}, bf16[128,128]{1,0:T(8,128)(2,1)S(1)}, bf16[128,128]{1,0:T(8,128)(2,1)S(1)}, bf16[128,128]{1,0:T(8,128)(2,1)S(1...) custom-call(s32[7]{0:T(128)S(1)} %stack.28.ids_ref, ...), custom_call_target="tpu_custom_call" | custom-call | flops 4294967296 | tf_op jit(solution)/shard_map/d_out/pallas_call | solution.py:331
  19.9 0.0 copy-start.9
  19.9 1.8 %collective-permute-start.3 = (bf16[128,128]{1,0:T(8,128)(2,1)S(1)}, bf16[128,128]{1,0:T(8,128)(2,1)S(1)}, u32[]{:S(2)}, u32[]{:S(2)}) collective-permute-start(bf16[128,128]{1,0:T(8,128)(2,1)S(1)} %get-tuple-element.48), channel_id=1, source_target_pairs={{0,2},{1,3},{2,0},{3,1},{4,6},{5,7},{6,4},{7,5},{8,10},{9,11},{10,... | collective-permute-start | bytes 98312 | tf_op jit(solution)/shard_map/ppermute | solution.py:263
  21.7 1.6 %collective-permute-start.4 = (bf16[128,128]{1,0:T(8,128)(2,1)S(1)}, bf16[128,128]{1,0:T(8,128)(2,1)S(1)}, u32[]{:S(2)}, u32[]{:S(2)}) collective-permute-start(bf16[128,128]{1,0:T(8,128)(2,1)S(1)} %get-tuple-element.49), channel_id=1, source_target_pairs={{0,4},{1,5},{2,6},{3,7},{4,0},{5,1},{6,2},{7,3},{8,12},{9,13},{10,... | collective-permute-start | bytes 98312 | tf_op jit(solution)/shard_map/ppermute | solution.py:263
  23.3 0.1 collective-permute-start.5
  23.4 2.8 %collective-permute-start.6 = (bf16[128,128]{1,0:T(8,128)(2,1)S(1)}, bf16[128,128]{1,0:T(8,128)(2,1)S(1)}, u32[]{:S(2)}, u32[]{:S(2)}) collective-permute-start(bf16[128,128]{1,0:T(8,128)(2,1)S(1)} %get-tuple-element.51), channel_id=1, source_target_pairs={{0,8},{1,9},{2,10},{3,11},{4,12},{5,13},{6,14},{7,15},{8,0},{9,1},... | collective-permute-start | bytes 98312 | tf_op jit(solution)/shard_map/ppermute | solution.py:263
  26.3 0.0 collective-permute-done.refs_5_
  26.3 0.7 copy-done.7
  27.0 1.3 %collective-permute-start.7 = (bf16[128,128]{1,0:T(8,128)(2,1)S(1)}, bf16[128,128]{1,0:T(8,128)(2,1)S(1)}, u32[]{:S(2)}, u32[]{:S(2)}) collective-permute-start(bf16[128,128]{1,0:T(8,128)(2,1)S(1)} %get-tuple-element.52), channel_id=1, source_target_pairs={{0,10},{1,11},{2,8},{3,9},{4,14},{5,15},{6,12},{7,13},{8,2},{9,3},... | collective-permute-start | bytes 98312 | tf_op jit(solution)/shard_map/ppermute | solution.py:263
  28.3 0.0 collective-permute-done.3.refs_1_
  28.3 3.6 %collective-permute-start.8 = (bf16[128,128]{1,0:T(8,128)(2,1)S(1)}, bf16[128,128]{1,0:T(8,128)(2,1)S(1)}, u32[]{:S(2)}, u32[]{:S(2)}) collective-permute-start(bf16[128,128]{1,0:T(8,128)(2,1)S(1)} %get-tuple-element.53), channel_id=1, source_target_pairs={{0,12},{1,13},{2,14},{3,15},{4,8},{5,9},{6,10},{7,11},{8,4},{9,5},... | collective-permute-start | bytes 98312 | tf_op jit(solution)/shard_map/ppermute | solution.py:263
  31.9 0.0 collective-permute-start.9
  31.9 0.0 collective-permute-done.5.refs_3_
  31.9 4.9 %collective-permute-done.6.refs_4_ = bf16[128,128]{1,0:T(8,128)(2,1)S(1)} collective-permute-done((bf16[128,128]{1,0:T(8,128)(2,1)S(1)}, bf16[128,128]{1,0:T(8,128)(2,1)S(1)}, u32[]{:S(2)}, u32[]{:S(2)}) %collective-permute-start.6) | collective-permute-done | bytes 32800 | tf_op jit(solution)/shard_map/ppermute | solution.py:263
  36.8 1.1 %collective-permute-done.7.refs_5_ = bf16[128,128]{1,0:T(8,128)(2,1)S(1)} collective-permute-done((bf16[128,128]{1,0:T(8,128)(2,1)S(1)}, bf16[128,128]{1,0:T(8,128)(2,1)S(1)}, u32[]{:S(2)}, u32[]{:S(2)}) %collective-permute-start.7) | collective-permute-done | bytes 32800 | tf_op jit(solution)/shard_map/ppermute | solution.py:263
  38.0 0.0 collective-permute-done.8.refs_6_
  38.0 0.7 collective-permute-done.9.refs_7_
  38.6 0.0 all-to-all-done.refs_0_.refs_8_
  38.6 0.0 collective-permute-start.10
  38.6 0.6 collective-permute-start.11
  39.2 0.1 copy.12.kb_ref
  39.3 1.6 %collective-permute-done.10.refs_1_.refs_9_ = bf16[8,384,128]{2,1,0:T(8,128)(2,1)S(1)} collective-permute-done((bf16[8,384,128]{2,1,0:T(8,128)(2,1)S(1)}, bf16[8,384,128]{2,1,0:T(8,128)(2,1)S(1)}, u32[]{:S(2)}, u32[]{:S(2)}) %collective-permute-start.10) | collective-permute-done | bytes 786464 | tf_op jit(solution)/shard_map/ppermute | solution.py:263
  40.9 3.4 %forward.1 = (bf16[8,128,128]{2,1,0:T(8,128)(2,1)}, bf16[8,128,256]{2,1,0:T(8,128)(2,1)S(1)}) custom-call(s32[7]{0:T(128)S(1)} %stack.28.ids_ref, s32[1,8,16,2]{3,2,1,0:T(8,128)S(1)} %copy.12.kb_ref, s32[1,8,16]{2,1,0:T(8,128)S(1)} %copy-done.5, bf16[8,384,128]{2,1,0:T(8,128)(2,1)S(1)} %all-to-all-done.refs_0_.refs_8_, ...), custom_call_target="tpu_custom_call" | custom-call | tf_op jit(solution)/shard_map/forward/pallas_call | solution.py:343
  44.3 3.4 %all-to-all-start.1 = ((bf16[8,128,128]{2,1,0:T(8,128)(2,1)}), bf16[8,128,128]{2,1,0:T(8,128)(2,1)S(1)}, u32[]{:S(2)}, u32[]{:S(2)}) async-start(bf16[8,128,128]{2,1,0:T(8,128)(2,1)} %get-tuple-element.56), calls=%async_computation.1 | async-start | bytes 524288 | tf_op jit(solution)/shard_map/all_to_all | solution.py:312
  47.8 3.1 %backward.1 = (bf16[8,128,128]{2,1,0:T(8,128)(2,1)S(1)}, bf16[8,256,128]{2,1,0:T(8,128)(2,1)S(1)}, bf16[8,128,128]{2,1,0:T(8,128)(2,1)S(1)}, bf16[8,128,128]{2,1,0:T(8,128)(2,1)S(1)}) custom-call(s32[7]{0:T(128)S(1)} %stack.28.ids_ref, s32[1,8,16,2]{3,2,1,0:T(8,128)S(1)} %copy.12.kb_ref, bf16[128,128]{1,0:T(8,128)(2,1)S(1)} %get-tuple-element.58.refs_0_, ...), custom_call_target="tpu_custom_call" | custom-call | tf_op jit(solution)/shard_map/backward/pallas_call | solution.py:354
  50.9 0.2 collective-permute-start.13
  51.1 0.4 collective-permute-start.14
  51.5 0.1 collective-permute-start.12
  51.6 0.9 collective-permute-done.13.refs_0_
  52.5 0.4 collective-permute-done.14.refs_1_
  52.9 1.0 %combine.1 = bf16[8,384,128]{2,1,0:T(8,128)(2,1)} custom-call(bf16[8,128,128]{2,1,0:T(8,128)(2,1)S(1)} %get-tuple-element.67.dq_ref, bf16[8,256,128]{2,1,0:T(8,128)(2,1)S(1)} %get-tuple-element.68.near_ref, bf16[8,128,128]{2,1,0:T(8,128)(2,1)S(1)} %collective-permute-done.13.refs_0_, bf16[8,128,128]{2,1,0:T(8,128)(2,1)S(1)} %collective-permute-done.14.refs_1_), custom_call_target="tpu_custom_call" | custom-call | tf_op jit(solution)/shard_map/combine/pallas_call | solution.py:365
  53.9 0.0 collective-permute-done.12.refs_7_
  53.9 3.3 %all-to-all-done.1.back_ref.mine_ref = bf16[8,128,128]{2,1,0:T(8,128)(2,1)S(1)} async-done(((bf16[8,128,128]{2,1,0:T(8,128)(2,1)}), bf16[8,128,128]{2,1,0:T(8,128)(2,1)S(1)}, u32[]{:S(2)}, u32[]{:S(2)}) %all-to-all-start.1) | async-done | bytes 262176 | tf_op jit(solution)/shard_map/all_to_all | solution.py:312
  57.2 0.6 features.1
  57.8 0.1 collective-permute-start.15
  57.9 1.5 %collective-permute-start.16 = (bf16[256,128]{1,0:T(8,128)(2,1)S(1)}, bf16[256,128]{1,0:T(8,128)(2,1)S(1)}, u32[]{:S(2)}, u32[]{:S(2)}) collective-permute-start(bf16[256,128]{1,0:T(8,128)(2,1)S(1)} %get-tuple-element.74), channel_id=1, source_target_pairs={{0,2},{1,3},{2,0},{3,1},{4,6},{5,7},{6,4},{7,5},{8,10},{9,11},{10,... | collective-permute-start | bytes 196616 | tf_op jit(solution)/shard_map/ppermute | solution.py:263
  59.3 0.4 collective-permute-start.17
  59.7 3.6 %all-to-all-start.2 = ((bf16[8,384,128]{2,1,0:T(8,128)(2,1)}), bf16[8,384,128]{2,1,0:T(8,128)(2,1)S(1)}, u32[]{:S(2)}, u32[]{:S(2)}) async-start(bf16[8,384,128]{2,1,0:T(8,128)(2,1)} %combine.1), calls=%async_computation.2 | async-start | bytes 1572864 | tf_op jit(solution)/shard_map/all_to_all | solution.py:312
  63.3 0.0 collective-permute-done.15.refs_1_
  63.3 0.2 collective-permute-done.17.refs_3_
  63.5 0.8 grad_weight.1
  64.3 1.4 %collective-permute-start.18 = (bf16[128,1024]{1,0:T(8,128)(2,1)S(1)}, bf16[128,1024]{1,0:T(8,128)(2,1)S(1)}, u32[]{:S(2)}, u32[]{:S(2)}) collective-permute-start(bf16[128,1024]{1,0:T(8,128)(2,1)S(1)} %get-tuple-element.80), channel_id=1, source_target_pairs={{0,16},{16,0},{1,17},{17,1},{2,18},{18,2},{3,19},{19,3},{4,20},{20... | collective-permute-start | bytes 786440 | tf_op jit(solution)/shard_map/ppermute | solution.py:267
  65.7 7.0 %collective-permute-done.18 = bf16[128,1024]{1,0:T(8,128)(2,1)S(1)} collective-permute-done((bf16[128,1024]{1,0:T(8,128)(2,1)S(1)}, bf16[128,1024]{1,0:T(8,128)(2,1)S(1)}, u32[]{:S(2)}, u32[]{:S(2)}) %collective-permute-start.18) | collective-permute-done | bytes 262176 | tf_op jit(solution)/shard_map/ppermute | solution.py:267
  72.8 0.1 fusion
  72.9 1.7 %collective-permute-start.19 = (bf16[32,1024]{1,0:T(8,128)(2,1)S(1)}, bf16[32,1024]{1,0:T(8,128)(2,1)S(1)}, u32[]{:S(2)}, u32[]{:S(2)}) collective-permute-start(bf16[32,1024]{1,0:T(8,128)(2,1)S(1)} %get-tuple-element.91), channel_id=1, source_target_pairs={{0,4},{1,5},{2,6},{3,7},{4,0},{5,1},{6,2},{7,3},{8,12},{9,13},{10,... | collective-permute-start | bytes 196616 | tf_op jit(solution)/shard_map/ppermute | solution.py:263
  74.6 2.4 %collective-permute-start.20 = (bf16[32,1024]{1,0:T(8,128)(2,1)S(1)}, bf16[32,1024]{1,0:T(8,128)(2,1)S(1)}, u32[]{:S(2)}, u32[]{:S(2)}) collective-permute-start(bf16[32,1024]{1,0:T(8,128)(2,1)S(1)} %get-tuple-element.93), channel_id=1, source_target_pairs={{0,8},{1,9},{2,10},{3,11},{4,12},{5,13},{6,14},{7,15},{8,0},{9,1},... | collective-permute-start | bytes 196616 | tf_op jit(solution)/shard_map/ppermute | solution.py:263
  77.0 0.4 collective-permute-start.21
  77.3 3.0 %output.1 = bf16[1,128,1024]{2,1,0:T(8,128)(2,1)} custom-call(s32[7]{0:T(128)} %copy-done.4, bf16[8,128,128]{2,1,0:T(8,128)(2,1)} %copy-done.1, bf16[512,1024]{1,0:T(8,128)(2,1)} %refs_0_.3, bf16[256,1024]{1,0:T(8,128)(2,1)} %copy-done.2, bf16[256,1024]{1,0:T(8,128)(2,1)} %copy-done.3), custom_call_target="tpu_custom_call" | custom-call | tf_op jit(solution)/shard_map/output/pallas_call | solution.py:384
  80.4 7.2 %all-to-all-done.2.recv_ref = bf16[8,384,128]{2,1,0:T(8,128)(2,1)S(1)} async-done(((bf16[8,384,128]{2,1,0:T(8,128)(2,1)}), bf16[8,384,128]{2,1,0:T(8,128)(2,1)S(1)}, u32[]{:S(2)}, u32[]{:S(2)}) %all-to-all-start.2) | async-done | bytes 786464 | tf_op jit(solution)/shard_map/all_to_all | solution.py:312
  87.6 1.1 %unpack.1 = (bf16[1,128,1024]{2,1,0:T(8,128)(2,1)}, bf16[1,128,1024]{2,1,0:T(8,128)(2,1)}, bf16[1,128,1024]{2,1,0:T(8,128)(2,1)}) custom-call(bf16[8,384,128]{2,1,0:T(8,128)(2,1)S(1)} %all-to-all-done.2.recv_ref), custom_call_target="tpu_custom_call" | custom-call | tf_op jit(solution)/shard_map/unpack/pallas_call | solution.py:372
  88.7 0.3 collective-permute-done.20
  89.0 0.0 collective-permute-done.21
  89.0 0.7 add_add_fusion
  (22 shorter events, 0.1 us)
Async XLA Ops:
  1.7 14.9 %collective-permute-start.1 = (bf16[256,1024]{1,0:T(8,128)(2,1)S(1)}, bf16[256,1024]{1,0:T(8,128)(2,1)S(1)}, u32[]{:S(2)}, u32[]{:S(2)}) collective-permute-start(bf16[256,1024]{1,0:T(8,128)(2,1)S(1)} %constant_dynamic-slice_fusion), channel_id=1, source_target_pairs={{0,16},{16,0},{1,17},{17,1},{2,18},{18,2},{3,19},{19,3},{4,20},{20... | collective-permute-start | bytes 1572872 | tf_op jit(solution)/shard_map/ppermute | solution.py:267
  6.7 10.0 %copy-start.6 = (bf16[1,128,1024]{2,1,0:T(8,128)(2,1)S(1)}, bf16[1,128,1024]{2,1,0:T(8,128)(2,1)}, u32[]{:S(2)}) copy-start(bf16[1,128,1024]{2,1,0:T(8,128)(2,1)} %refs_4_.1) | copy-start | bytes 786436
  6.7 11.9 %copy-start = (bf16[512,1024]{1,0:T(8,128)(2,1)S(1)}, bf16[512,1024]{1,0:T(8,128)(2,1)}, u32[]{:S(2)}) copy-start(bf16[512,1024]{1,0:T(8,128)(2,1)} %refs_0_.3) | copy-start | bytes 3145732
  6.7 31.9 %all-to-all-start = ((bf16[8,384,128]{2,1,0:T(8,128)(2,1)}), bf16[8,384,128]{2,1,0:T(8,128)(2,1)S(1)}, u32[]{:S(2)}, u32[]{:S(2)}) async-start(bf16[8,384,128]{2,1,0:T(8,128)(2,1)} %pack.1), calls=%async_computation | async-start | bytes 1572864 | tf_op jit(solution)/shard_map/all_to_all | solution.py:312
  16.6 3.2 %copy-start.2 = (bf16[256,1024]{1,0:T(8,128)(2,1)}, bf16[256,1024]{1,0:T(8,128)(2,1)S(1)}, u32[]{:S(2)}) copy-start(bf16[256,1024]{1,0:T(8,128)(2,1)S(1)} %collective-permute-done.1.refs_1_) | copy-start | bytes 1572868
  16.7 1.9 %collective-permute-start.2 = (bf16[256,1024]{1,0:T(8,128)(2,1)S(1)}, bf16[256,1024]{1,0:T(8,128)(2,1)S(1)}, u32[]{:S(2)}, u32[]{:S(2)}) collective-permute-start(bf16[256,1024]{1,0:T(8,128)(2,1)S(1)} %collective-permute-done.1.refs_1_), channel_id=1, source_target_pairs={{0,1},{1,0},{2,3},{3,2},{4,5},{5,4},{6,7},{7,6},{8,9},{9,8},{10,11... | collective-permute-start | bytes 1572872 | tf_op jit(solution)/shard_map/ppermute | solution.py:263
  16.7 9.6 %collective-permute-start = (bf16[1,128,1024]{2,1,0:T(8,128)(2,1)S(1)}, bf16[1,128,1024]{2,1,0:T(8,128)(2,1)S(1)}, u32[]{:S(2)}, u32[]{:S(2)}) collective-permute-start(bf16[1,128,1024]{2,1,0:T(8,128)(2,1)S(1)} %copy-done.6), channel_id=1, source_target_pairs={{0,1},{1,0},{2,3},{3,2},{4,5},{5,4},{6,7},{7,6},{8,9},{9,8},{10,11... | collective-permute-start | bytes 786440 | tf_op jit(solution)/shard_map/ppermute | solution.py:263
  17.2 39.9 %copy-start.4 = (s32[7]{0:T(128)}, s32[7]{0:T(128)S(1)}, u32[]{:S(2)}) copy-start(s32[7]{0:T(128)S(1)} %stack.28.ids_ref) | copy-start | bytes 88
  18.6 1.3 %copy-start.3 = (bf16[256,1024]{1,0:T(8,128)(2,1)}, bf16[256,1024]{1,0:T(8,128)(2,1)S(1)}, u32[]{:S(2)}) copy-start(bf16[256,1024]{1,0:T(8,128)(2,1)S(1)} %collective-permute-done.2.refs_2_) | copy-start | bytes 1572868
  19.9 19.3 %copy-start.9 = (s32[1,8,16,2]{2,3,1,0:T(2,128)S(1)}, s32[1,8,16,2]{2,3,1,0:T(2,128)}, u32[]{:S(2)}) copy-start(s32[1,8,16,2]{2,3,1,0:T(2,128)} %param.12) | copy-start | bytes 3076
  19.9 8.4 %collective-permute-start.3 = (bf16[128,128]{1,0:T(8,128)(2,1)S(1)}, bf16[128,128]{1,0:T(8,128)(2,1)S(1)}, u32[]{:S(2)}, u32[]{:S(2)}) collective-permute-start(bf16[128,128]{1,0:T(8,128)(2,1)S(1)} %get-tuple-element.48), channel_id=1, source_target_pairs={{0,2},{1,3},{2,0},{3,1},{4,6},{5,7},{6,4},{7,5},{8,10},{9,11},{10,... | collective-permute-start | bytes 98312 | tf_op jit(solution)/shard_map/ppermute | solution.py:263
  21.7 10.2 %collective-permute-start.4 = (bf16[128,128]{1,0:T(8,128)(2,1)S(1)}, bf16[128,128]{1,0:T(8,128)(2,1)S(1)}, u32[]{:S(2)}, u32[]{:S(2)}) collective-permute-start(bf16[128,128]{1,0:T(8,128)(2,1)S(1)} %get-tuple-element.49), channel_id=1, source_target_pairs={{0,4},{1,5},{2,6},{3,7},{4,0},{5,1},{6,2},{7,3},{8,12},{9,13},{10,... | collective-permute-start | bytes 98312 | tf_op jit(solution)/shard_map/ppermute | solution.py:263
  23.3 8.6 %collective-permute-start.5 = (bf16[128,128]{1,0:T(8,128)(2,1)S(1)}, bf16[128,128]{1,0:T(8,128)(2,1)S(1)}, u32[]{:S(2)}, u32[]{:S(2)}) collective-permute-start(bf16[128,128]{1,0:T(8,128)(2,1)S(1)} %get-tuple-element.50), channel_id=1, source_target_pairs={{0,6},{1,7},{2,4},{3,5},{4,2},{5,3},{6,0},{7,1},{8,14},{9,15},{10,... | collective-permute-start | bytes 98312 | tf_op jit(solution)/shard_map/ppermute | solution.py:263
  23.4 13.4 %collective-permute-start.6 = (bf16[128,128]{1,0:T(8,128)(2,1)S(1)}, bf16[128,128]{1,0:T(8,128)(2,1)S(1)}, u32[]{:S(2)}, u32[]{:S(2)}) collective-permute-start(bf16[128,128]{1,0:T(8,128)(2,1)S(1)} %get-tuple-element.51), channel_id=1, source_target_pairs={{0,8},{1,9},{2,10},{3,11},{4,12},{5,13},{6,14},{7,15},{8,0},{9,1},... | collective-permute-start | bytes 98312 | tf_op jit(solution)/shard_map/ppermute | solution.py:263
  26.3 0.7 copy-start.7
  27.0 11.0 %collective-permute-start.7 = (bf16[128,128]{1,0:T(8,128)(2,1)S(1)}, bf16[128,128]{1,0:T(8,128)(2,1)S(1)}, u32[]{:S(2)}, u32[]{:S(2)}) collective-permute-start(bf16[128,128]{1,0:T(8,128)(2,1)S(1)} %get-tuple-element.52), channel_id=1, source_target_pairs={{0,10},{1,11},{2,8},{3,9},{4,14},{5,15},{6,12},{7,13},{8,2},{9,3},... | collective-permute-start | bytes 98312 | tf_op jit(solution)/shard_map/ppermute | solution.py:263
  28.3 9.7 %collective-permute-start.8 = (bf16[128,128]{1,0:T(8,128)(2,1)S(1)}, bf16[128,128]{1,0:T(8,128)(2,1)S(1)}, u32[]{:S(2)}, u32[]{:S(2)}) collective-permute-start(bf16[128,128]{1,0:T(8,128)(2,1)S(1)} %get-tuple-element.53), channel_id=1, source_target_pairs={{0,12},{1,13},{2,14},{3,15},{4,8},{5,9},{6,10},{7,11},{8,4},{9,5},... | collective-permute-start | bytes 98312 | tf_op jit(solution)/shard_map/ppermute | solution.py:263
  31.9 6.7 %collective-permute-start.9 = (bf16[128,128]{1,0:T(8,128)(2,1)S(1)}, bf16[128,128]{1,0:T(8,128)(2,1)S(1)}, u32[]{:S(2)}, u32[]{:S(2)}) collective-permute-start(bf16[128,128]{1,0:T(8,128)(2,1)S(1)} %get-tuple-element.54), channel_id=1, source_target_pairs={{0,14},{1,15},{2,12},{3,13},{4,10},{5,11},{6,8},{7,9},{8,6},{9,7},... | collective-permute-start | bytes 98312 | tf_op jit(solution)/shard_map/ppermute | solution.py:263
  38.6 2.3 %copy-start.5 = (s32[1,8,16]{2,1,0:T(8,128)S(1)}, s32[1,8,16]{2,1,0:T(8,128)}, u32[]{:S(2)}) copy-start(s32[1,8,16]{2,1,0:T(8,128)} %cnt_ref.1) | copy-start | bytes 1540
  38.6 2.3 %collective-permute-start.10 = (bf16[8,384,128]{2,1,0:T(8,128)(2,1)S(1)}, bf16[8,384,128]{2,1,0:T(8,128)(2,1)S(1)}, u32[]{:S(2)}, u32[]{:S(2)}) collective-permute-start(bf16[8,384,128]{2,1,0:T(8,128)(2,1)S(1)} %all-to-all-done.refs_0_.refs_8_), channel_id=1, source_target_pairs={{0,1},{1,0},{2,3},{3,2},{4,5},{5,4},{6,7},{7,6},{8,9},{9,8},{10,11... | collective-permute-start | bytes 2359304 | tf_op jit(solution)/shard_map/ppermute | solution.py:263
  38.6 12.8 %collective-permute-start.11 = (bf16[1,128,1024]{2,1,0:T(8,128)(2,1)S(1)}, bf16[1,128,1024]{2,1,0:T(8,128)(2,1)S(1)}, u32[]{:S(2)}, u32[]{:S(2)}) collective-permute-start(bf16[1,128,1024]{2,1,0:T(8,128)(2,1)S(1)} %copy-done.6), channel_id=1, source_target_pairs={{0,2},{1,3},{2,0},{3,1},{4,6},{5,7},{6,4},{7,5},{8,10},{9,11},{10,... | collective-permute-start | bytes 786440 | tf_op jit(solution)/shard_map/ppermute | solution.py:263
  44.3 12.9 %all-to-all-start.1 = ((bf16[8,128,128]{2,1,0:T(8,128)(2,1)}), bf16[8,128,128]{2,1,0:T(8,128)(2,1)S(1)}, u32[]{:S(2)}, u32[]{:S(2)}) async-start(bf16[8,128,128]{2,1,0:T(8,128)(2,1)} %get-tuple-element.56), calls=%async_computation.1 | async-start | bytes 524288 | tf_op jit(solution)/shard_map/all_to_all | solution.py:312
  50.9 1.6 %collective-permute-start.13 = (bf16[8,128,128]{2,1,0:T(8,128)(2,1)S(1)}, bf16[8,128,128]{2,1,0:T(8,128)(2,1)S(1)}, u32[]{:S(2)}, u32[]{:S(2)}) collective-permute-start(bf16[8,128,128]{2,1,0:T(8,128)(2,1)S(1)} %get-tuple-element.69), channel_id=1, source_target_pairs={{0,1},{1,0},{2,3},{3,2},{4,5},{5,4},{6,7},{7,6},{8,9},{9,8},{10,11... | collective-permute-start | bytes 786440 | tf_op jit(solution)/shard_map/ppermute | solution.py:263
  51.1 1.8 %collective-permute-start.14 = (bf16[8,128,128]{2,1,0:T(8,128)(2,1)S(1)}, bf16[8,128,128]{2,1,0:T(8,128)(2,1)S(1)}, u32[]{:S(2)}, u32[]{:S(2)}) collective-permute-start(bf16[8,128,128]{2,1,0:T(8,128)(2,1)S(1)} %get-tuple-element.70), channel_id=1, source_target_pairs={{0,1},{1,0},{2,3},{3,2},{4,5},{5,4},{6,7},{7,6},{8,9},{9,8},{10,11... | collective-permute-start | bytes 786440 | tf_op jit(solution)/shard_map/ppermute | solution.py:263
  51.5 2.4 %collective-permute-start.12 = (bf16[1,128,1024]{2,1,0:T(8,128)(2,1)S(1)}, bf16[1,128,1024]{2,1,0:T(8,128)(2,1)S(1)}, u32[]{:S(2)}, u32[]{:S(2)}) collective-permute-start(bf16[1,128,1024]{2,1,0:T(8,128)(2,1)S(1)} %collective-permute-done.11.refs_6_), channel_id=1, source_target_pairs={{0,1},{1,0},{2,3},{3,2},{4,5},{5,4},{6,7},{7,6},{8,9},{9,8},{10,11... | collective-permute-start | bytes 786440 | tf_op jit(solution)/shard_map/ppermute | solution.py:263
  57.2 2.5 %copy-start.1 = (bf16[8,128,128]{2,1,0:T(8,128)(2,1)}, bf16[8,128,128]{2,1,0:T(8,128)(2,1)S(1)}, u32[]{:S(2)}) copy-start(bf16[8,128,128]{2,1,0:T(8,128)(2,1)S(1)} %all-to-all-done.1.back_ref.mine_ref) | copy-start | bytes 786436
  57.8 5.5 %collective-permute-start.15 = (bf16[256,128]{1,0:T(8,128)(2,1)S(1)}, bf16[256,128]{1,0:T(8,128)(2,1)S(1)}, u32[]{:S(2)}, u32[]{:S(2)}) collective-permute-start(bf16[256,128]{1,0:T(8,128)(2,1)S(1)} %get-tuple-element.73), channel_id=1, source_target_pairs={{0,1},{1,0},{2,3},{3,2},{4,5},{5,4},{6,7},{7,6},{8,9},{9,8},{10,11... | collective-permute-start | bytes 196616 | tf_op jit(solution)/shard_map/ppermute | solution.py:263
  57.9 5.4 %collective-permute-start.16 = (bf16[256,128]{1,0:T(8,128)(2,1)S(1)}, bf16[256,128]{1,0:T(8,128)(2,1)S(1)}, u32[]{:S(2)}, u32[]{:S(2)}) collective-permute-start(bf16[256,128]{1,0:T(8,128)(2,1)S(1)} %get-tuple-element.74), channel_id=1, source_target_pairs={{0,2},{1,3},{2,0},{3,1},{4,6},{5,7},{6,4},{7,5},{8,10},{9,11},{10,... | collective-permute-start | bytes 196616 | tf_op jit(solution)/shard_map/ppermute | solution.py:263
  59.3 4.2 %copy-start.8 = (bf16[1,128,1024]{2,1,0:T(8,128)(2,1)S(1)}, bf16[1,128,1024]{2,1,0:T(8,128)(2,1)}, u32[]{:S(2)}) copy-start(bf16[1,128,1024]{2,1,0:T(8,128)(2,1)} %copy-done.7) | copy-start | bytes 786436
  59.3 4.1 %collective-permute-start.17 = (bf16[256,128]{1,0:T(8,128)(2,1)S(1)}, bf16[256,128]{1,0:T(8,128)(2,1)S(1)}, u32[]{:S(2)}, u32[]{:S(2)}) collective-permute-start(bf16[256,128]{1,0:T(8,128)(2,1)S(1)} %get-tuple-element.75), channel_id=1, source_target_pairs={{0,3},{1,2},{2,1},{3,0},{4,7},{5,6},{6,5},{7,4},{8,11},{9,10},{10,... | collective-permute-start | bytes 196616 | tf_op jit(solution)/shard_map/ppermute | solution.py:263
  59.7 27.9 %all-to-all-start.2 = ((bf16[8,384,128]{2,1,0:T(8,128)(2,1)}), bf16[8,384,128]{2,1,0:T(8,128)(2,1)S(1)}, u32[]{:S(2)}, u32[]{:S(2)}) async-start(bf16[8,384,128]{2,1,0:T(8,128)(2,1)} %combine.1), calls=%async_computation.2 | async-start | bytes 1572864 | tf_op jit(solution)/shard_map/all_to_all | solution.py:312
  64.3 8.5 %collective-permute-start.18 = (bf16[128,1024]{1,0:T(8,128)(2,1)S(1)}, bf16[128,1024]{1,0:T(8,128)(2,1)S(1)}, u32[]{:S(2)}, u32[]{:S(2)}) collective-permute-start(bf16[128,1024]{1,0:T(8,128)(2,1)S(1)} %get-tuple-element.80), channel_id=1, source_target_pairs={{0,16},{16,0},{1,17},{17,1},{2,18},{18,2},{3,19},{19,3},{4,20},{20... | collective-permute-start | bytes 786440 | tf_op jit(solution)/shard_map/ppermute | solution.py:267
  72.9 15.8 %collective-permute-start.19 = (bf16[32,1024]{1,0:T(8,128)(2,1)S(1)}, bf16[32,1024]{1,0:T(8,128)(2,1)S(1)}, u32[]{:S(2)}, u32[]{:S(2)}) collective-permute-start(bf16[32,1024]{1,0:T(8,128)(2,1)S(1)} %get-tuple-element.91), channel_id=1, source_target_pairs={{0,4},{1,5},{2,6},{3,7},{4,0},{5,1},{6,2},{7,3},{8,12},{9,13},{10,... | collective-permute-start | bytes 196616 | tf_op jit(solution)/shard_map/ppermute | solution.py:263
  74.6 14.4 %collective-permute-start.20 = (bf16[32,1024]{1,0:T(8,128)(2,1)S(1)}, bf16[32,1024]{1,0:T(8,128)(2,1)S(1)}, u32[]{:S(2)}, u32[]{:S(2)}) collective-permute-start(bf16[32,1024]{1,0:T(8,128)(2,1)S(1)} %get-tuple-element.93), channel_id=1, source_target_pairs={{0,8},{1,9},{2,10},{3,11},{4,12},{5,13},{6,14},{7,15},{8,0},{9,1},... | collective-permute-start | bytes 196616 | tf_op jit(solution)/shard_map/ppermute | solution.py:263
  77.0 12.1 %collective-permute-start.21 = (bf16[32,1024]{1,0:T(8,128)(2,1)S(1)}, bf16[32,1024]{1,0:T(8,128)(2,1)S(1)}, u32[]{:S(2)}, u32[]{:S(2)}) collective-permute-start(bf16[32,1024]{1,0:T(8,128)(2,1)S(1)} %get-tuple-element.92), channel_id=1, source_target_pairs={{0,12},{1,13},{2,14},{3,15},{4,8},{5,9},{6,10},{7,11},{8,4},{9,5},... | collective-permute-start | bytes 196616 | tf_op jit(solution)/shard_map/ppermute | solution.py:263
